TPU v7x, 256 devices: a whole 4x4x8 slice. The times are simulated.
256 devices in a mesh: slab: 256 (over z, x, y, core).
Axes of the slice: x: 4, y: 4, z: 8, core: 2. Of those that a mesh axis runs over, the one named last changes fastest.
Arguments:
- newton_rhs: float32 [3, 1024, 128, 128], P(None, 'slab'), may hold values from -8 to 8
- stiffness: float32 [1024, 128, 128], P('slab'), may hold values from 0.25 to 4
- stencil: float32 [27, 3, 3], replicated, may hold values from -0.1 to 10.1, as said below
- dual_weight: float32 [1024, 128], P('slab'), may hold values from 0.5 to 2
- mortar: bfloat16 [1024, 3, 128, 128], P('slab'), may hold values from -0.3125 to 0.3125
- partner: int32 [1024, 3], P('slab'), may hold values from 0 to 1023, as said below
- active: int32 [1024], P('slab'), may hold values 0 or 1
Outputs:
- increment: float32 [3, 1024, 128, 128], P(None, 'slab')
- residual: float32 [3, 1024, 128, 128], P(None, 'slab')
Inputs may be any that keep to these rules, and one draw needn't show every extreme that they name: stencil[26 - k] is the transpose of stencil[k]; entries off the centre block lie within 0.1 in magnitude, and the centre block stencil[13] is 10 times the identity plus a symmetric matrix of entries within 0.1. `partner`: slave tile t lies on device d = t // 4; slot s of it names a tile on device (1 - d // 128) * 128 + (d % 128 + s - 1) modulo 128.
All inputs are finite; a program needn't handle non-finite values. No bound on the sum of `active` on one device may be relied on, other than what follows from the above.
Results may differ from a plain program's by a relative error of at most 0.0003.
Values sent between devices are 32-bit elements; how exact they have to be, the bound alone decides.
No kernel may reach another device: no remote copies, remote signals or barrier semaphores. Data moves between devices by JAX's collectives and lax.ppermute only.
A program may use at most 64 MiB of HBM per device.

v0:
```python
import jax
import jax.numpy as jnp
from jax import lax
from jax.sharding import PartitionSpec as P

ITERS = 2


def with_halo(array, sides, width):
    for axis, dim in sides:
        peers, length = (lax.axis_size(axis), array.shape[dim])
        up = [(i, (i + 1) % peers) for i in range(peers)]
        down = [(j, i) for i, j in up]
        last = lax.slice_in_dim(array, length - width, length, axis=dim)
        initial = lax.slice_in_dim(array, 0, width, axis=dim)
        before = lax.ppermute(last, axis, up)
        after = lax.ppermute(initial, axis, down)
        array = jnp.concatenate([before, array, after], axis=dim)
    return array


def stencil_part(field_in, stencil):
    padded = with_halo(field_in, (("slab", 1),), 1)
    slab_index = lax.axis_index("slab")
    quarter_count = lax.axis_size("slab") // 4
    lower_cut = jnp.logical_or(slab_index == quarter_count, slab_index == 3 * quarter_count)
    upper_cut = jnp.logical_or(slab_index == quarter_count - 1, slab_index == 3 * quarter_count - 1)
    lower_rim = jnp.where(lower_cut, 0.0, padded[:, :1])
    upper_rim = jnp.where(upper_cut, 0.0, padded[:, -1:])
    padded = jnp.concatenate([lower_rim, padded[:, 1:-1], upper_rim], axis=1)
    padded = jnp.pad(padded, ((0, 0), (0, 0), (1, 1), (1, 1)))
    plane_count = field_in.shape[1]
    node_count = field_in.shape[2]
    depth_count = field_in.shape[3]
    outputs = [jnp.zeros(field_in.shape[1:], jnp.float32) for out_comp in range(3)]
    for along_x in range(3):
        for along_y in range(3):
            for along_z in range(3):
                offset_index = 9 * along_x + 3 * along_y + along_z
                window_view = padded[
                    :,
                    along_x : along_x + plane_count,
                    along_y : along_y + node_count,
                    along_z : along_z + depth_count,
                ]
                for out_comp in range(3):
                    for in_comp in range(3):
                        outputs[out_comp] = (
                            outputs[out_comp]
                            + stencil[offset_index, out_comp, in_comp] * window_view[in_comp]
                        )
    return jnp.stack(outputs)


def contact_gather(master, slave_face, dual_weight, mortar_full, partner, active_float):
    planes = master.shape[0]
    tile_width = master.shape[1]
    all_faces = lax.all_gather(master, "slab", axis=0, tiled=True)
    facing = jnp.take(all_faces, partner, axis=0)
    pulled = jnp.einsum("tpij,tpj->ti", mortar_full, facing, precision=lax.Precision.HIGHEST)
    push_force = 4.0 * active_float[:, None] * (dual_weight * slave_face - pulled)
    back_force = -jnp.einsum(
        "tpij,ti->tpj", mortar_full, push_force, precision=lax.Precision.HIGHEST
    )
    reaction_table = jnp.zeros((planes * lax.axis_size("slab"), tile_width), jnp.float32)
    reaction_table = reaction_table.at[partner.reshape(-1)].add(back_force.reshape(-1, tile_width))
    master_add = lax.psum_scatter(reaction_table, "slab", scatter_dimension=0, tiled=True)
    return (dual_weight * push_force, master_add)


def apply_operator(field_in, stencil, stiffness, dual_weight, mortar_full, partner, active_float):
    result = stencil_part(field_in, stencil) + stiffness[None] * field_in
    slave_face = field_in[2, :, :, -1]
    master = field_in[2, :, :, 0]
    slave_add, master_add = contact_gather(
        master, slave_face, dual_weight, mortar_full, partner, active_float
    )
    result = result.at[2, :, :, -1].add(slave_add)
    result = result.at[2, :, :, 0].add(master_add)
    return result


def residual_squares(residual):
    return lax.psum(jnp.sum(residual * residual), "slab")


def local(newton_rhs, stiffness, stencil, dual_weight, mortar, partner, active):
    mortar_full = mortar.astype(jnp.float32)
    active_float = active.astype(jnp.float32)
    increment = jnp.zeros_like(newton_rhs)
    residual = newton_rhs
    direction = newton_rhs
    norm_now = residual_squares(residual)
    for iteration in range(ITERS):
        image = apply_operator(
            direction, stencil, stiffness, dual_weight, mortar_full, partner, active_float
        )
        curvature = lax.psum(jnp.sum(direction * image), "slab")
        step_size = norm_now / curvature
        increment = increment + step_size * direction
        residual = residual - step_size * image
        norm_next = residual_squares(residual)
        direction = residual + norm_next / norm_now * direction
        norm_now = norm_next
    return (increment, residual)


def solution(mesh):
    placed = (
        P(None, "slab", None, None),
        P("slab", None, None),
        P(),
        P("slab", None),
        P("slab", None, None, None),
        P("slab", None),
        P("slab"),
    )
    return jax.shard_map(
        local,
        mesh=mesh,
        in_specs=placed,
        out_specs=(P(None, "slab", None, None), P(None, "slab", None, None)),
        check_vma=False,
    )
```

profile of v0, /device:TPU:1, one launch (start us, length us, event | category | flops | bytes accessed | tf_op | source)
XLA Modules:
  0.0 1311.5 jit_solution(6436635839375762363)
XLA Ops:
  8.5 3.3 collective-permute-start.1
  17.3 2.1 fusion.26
  19.4 2.1 fusion.34
  25.4 2.1 fusion.31
  33.5 2.1 fusion.27
  35.6 2.1 fusion.37
  39.8 2.1 fusion.35
  44.7 75.9 %all-gather = f32[1,1024,128,1]{2,3,0,1:T(1,128)S(1)} all-gather(f32[1,4,128,1]{2,3,0,1:T(1,128)S(1)} %copy.72), channel_id=2, replica_groups=mesh['slab'=256] {'slab'}, dimensions={1}, use_global_device_ids=true | all-gather | bytes 526336 | tf_op jit(solution)/shard_map/all_gather | solution.py:58
  122.2 2.5 select_maximum_fusion.2
  124.7 59.7 %multiply_add_fusion.7 = (f32[1,4,128,128]{2,1,3,0:T(4,128)S(1)}, f32[1,4,128,128]{2,1,3,0:T(4,128)S(1)}, f32[1,4,128,128]{2,1,3,0:T(4,128)S(1)}, f32[1,4,128,12...) fusion(f32[3,6,130,130]{2,1,3,0:T(8,128)S(1)} %select_maximum_f, ...), kind=kLoop, calls=%fused_computation.50 | loop fusion | flops 10944512 | bytes 22675780 | tf_op jit(solution)/shard_map/add | solution.py:49
  184.4 59.1 %multiply_add_fusion.6 = f32[1,4,128,128]{2,1,3,0:T(4,128)S(1)} fusion(f32[1,4,128,128]{2,1,3,0:T(4,128)S(1)} %get-tuple-element.76, f32[1,4,128,128]{2,1,3,0:T(4,128)S(1)} %get-tuple-element.75, f32[1,4,128,128]{2,1,3,0:T(4,128)S(1)} %get-tuple-element.74, f32[1,4,128,128]{2,1,3,0:T(4,128)S(1)} %get-tuple-element.73, ...), kind=kLoop, calls=%fused_computation.49 | loop fusion | flops 10551296 | bytes 21496132 | tf_op jit(solution)/shard_map/add | solution.py:49
  243.5 59.0 %multiply_add_fusion.5 = f32[1,4,128,128]{2,1,3,0:T(4,128)S(1)} fusion(f32[1,4,128,128]{2,1,3,0:T(4,128)S(1)} %get-tuple-element.76, f32[1,4,128,128]{2,1,3,0:T(4,128)S(1)} %get-tuple-element.75, f32[1,4,128,128]{2,1,3,0:T(4,128)S(1)} %get-tuple-element.74, f32[1,4,128,128]{2,1,3,0:T(4,128)S(1)} %get-tuple-element.73, ...), kind=kLoop, calls=%fused_computation.48 | loop fusion | flops 10551296 | bytes 21496132 | tf_op jit(solution)/shard_map/add | solution.py:49
  305.6 246.9 %all-reduce.8.cloned.1.call-done = f32[1024,128]{1,0:T(8,128)} async-done(((f32[1024,128]{1,0:T(8,128)}), f32[1024,128]{1,0:T(8,128)}) %all-reduce.8.cloned.1.call-update) | async-done | bytes 524304
  554.2 77.8 %all-reduce.4 = (f32[]{:T(128)}, f32[]{:T(128)}) all-reduce(f32[]{:T(128)} %multiply_reduce_fusion.3, f32[]{:T(128)} %multiply_reduce_fusion.2), channel_id=1, replica_groups=mesh['slab'=256] {'slab'}, use_global_device_ids=true, to_apply=%region_1.0 | all-reduce | flops 2 | bytes 16 | tf_op jit(solution)/shard_map/psum | solution.py:84
  634.4 73.2 %psum.30 = f32[]{:T(128)} all-reduce(f32[]{:T(128)} %multiply_reduce_fusion.1), channel_id=1, replica_groups=mesh['slab'=256] {'slab'}, use_global_device_ids=true, to_apply=%region_7.9 | all-reduce | flops 1 | bytes 8 | tf_op jit(solution)/shard_map/psum | solution.py:84
  711.4 72.0 %all-gather.1 = f32[1,1024,128,1]{2,3,0,1:T(1,128)S(1)} all-gather(f32[1,4,128,1]{2,3,0,1:T(1,128)S(1)} %bitcast.335), channel_id=3, replica_groups=mesh['slab'=256] {'slab'}, dimensions={1}, use_global_device_ids=true | all-gather | bytes 526336 | tf_op jit(solution)/shard_map/all_gather | solution.py:58
  785.9 2.5 select_maximum_fusion
  788.4 59.4 %multiply_add_fusion.4 = (f32[1,4,128,128]{2,1,3,0:T(4,128)S(1)}, f32[1,4,128,128]{2,1,3,0:T(4,128)S(1)}, f32[1,4,128,128]{2,1,3,0:T(4,128)S(1)}, f32[1,4,128,12...) fusion(f32[3,6,130,130]{2,1,3,0:T(8,128)S(1)} %select_maximum_f, ...), kind=kLoop, calls=%fused_computation.43 | loop fusion | flops 10944512 | bytes 22675780 | tf_op jit(solution)/shard_map/add | solution.py:49
  847.9 59.1 %multiply_add_fusion.3 = f32[1,4,128,128]{2,1,3,0:T(4,128)S(1)} fusion(f32[1,4,128,128]{2,1,3,0:T(4,128)S(1)} %get-tuple-element.67, f32[1,4,128,128]{2,1,3,0:T(4,128)S(1)} %get-tuple-element.66, f32[1,4,128,128]{2,1,3,0:T(4,128)S(1)} %get-tuple-element.65, f32[1,4,128,128]{2,1,3,0:T(4,128)S(1)} %get-tuple-element.64, ...), kind=kLoop, calls=%fused_computation.42 | loop fusion | flops 10551296 | bytes 21496132 | tf_op jit(solution)/shard_map/add | solution.py:49
  907.0 59.0 %multiply_add_fusion.2 = f32[1,4,128,128]{2,1,3,0:T(4,128)S(1)} fusion(f32[1,4,128,128]{2,1,3,0:T(4,128)S(1)} %get-tuple-element.67, f32[1,4,128,128]{2,1,3,0:T(4,128)S(1)} %get-tuple-element.66, f32[1,4,128,128]{2,1,3,0:T(4,128)S(1)} %get-tuple-element.65, f32[1,4,128,128]{2,1,3,0:T(4,128)S(1)} %get-tuple-element.64, ...), kind=kLoop, calls=%fused_computation.41 | loop fusion | flops 10551296 | bytes 21496132 | tf_op jit(solution)/shard_map/add | solution.py:49
  968.3 249.6 %all-reduce.10.cloned.1.call-done = f32[1024,128]{1,0:T(8,128)} async-done(((f32[1024,128]{1,0:T(8,128)}), f32[1024,128]{1,0:T(8,128)}) %all-reduce.10.cloned.1.call-update) | async-done | bytes 524304
  1219.6 77.6 %psum.31 = f32[]{:T(128)} all-reduce(f32[]{:T(128)} %multiply_reduce_fusion), channel_id=1, replica_groups=mesh['slab'=256] {'slab'}, use_global_device_ids=true, to_apply=%region_11.13 | all-reduce | flops 1 | bytes 8 | tf_op jit(solution)/shard_map/psum | solution.py:98
  1299.9 2.3 copy.62
  1302.2 2.3 copy.63
  (83 shorter events, 39.1 us)
Async XLA Ops:
  7.2 114.1 %copy-start = (bf16[4,3,128,128]{3,2,1,0:T(8,128)(2,1)S(1)}, bf16[4,3,128,128]{3,2,1,0:T(8,128)(2,1)}, u32[]{:S(2)}) copy-start(bf16[4,3,128,128]{3,2,1,0:T(8,128)(2,1)} %param.21) | copy-start | bytes 1179652
  7.2 37.1 %copy-start.6 = (s32[4]{0:T(128)S(1)}, s32[4]{0:T(128)}, u32[]{:S(2)}) copy-start(s32[4]{0:T(128)} %param.23) | copy-start | bytes 52
  7.2 37.2 %copy-start.4 = (f32[4,128,128]{2,1,0:T(8,128)S(1)}, f32[4,128,128]{2,1,0:T(8,128)}, u32[]{:S(2)}) copy-start(f32[4,128,128]{2,1,0:T(8,128)} %param.18) | copy-start | bytes 786436
  7.2 545.3 %all-reduce.8.cloned.1.call-start = ((), (), s32[]{:S(2)}) async-start(), calls=%async_computation | async-start | bytes 1048576
  8.5 113.3 %collective-permute-start.1 = (f32[3,1,128,128]{2,1,3,0:T(1,128)S(1)}, f32[3,1,128,128]{2,1,3,0:T(1,128)S(1)}, u32[]{:S(2)}, u32[]{:S(2)}) collective-permute-start(f32[3,1,128,128]{2,1,3,0:T(1,128)S(1)} %copy.46), channel_id=1, source_target_pairs={{1,0},{2,1},{3,2},{4,3},{5,4},{6,5},{7,6},{8,7},{9,8},{10,9},{11,1... | collective-permute-start | bytes 589832 | tf_op jit(solution)/shard_map/ppermute | solution.py:17
  11.9 110.1 %collective-permute-start = (f32[3,1,128,128]{2,1,3,0:T(1,128)S(1)}, f32[3,1,128,128]{2,1,3,0:T(1,128)S(1)}, u32[]{:S(2)}, u32[]{:S(2)}) collective-permute-start(f32[3,1,128,128]{2,1,3,0:T(1,128)S(1)} %copy.45), channel_id=1, source_target_pairs={{0,1},{1,2},{2,3},{3,4},{4,5},{5,6},{6,7},{7,8},{8,9},{9,10},{10,1... | collective-permute-start | bytes 589832 | tf_op jit(solution)/shard_map/ppermute | solution.py:16
  44.5 258.0 %copy-start.2 = (f32[4,128,128]{1,0,2:T(4,128)}, f32[4,128,128]{1,0,2:T(4,128)S(1)}, u32[]{:S(2)}) copy-start(f32[4,128,128]{1,0,2:T(4,128)S(1)} %copy.53) | copy-start | bytes 786436
  121.8 181.5 %copy-start.7 = (s32[12]{0:T(128)}, s32[12]{0:T(128)S(1)}, u32[]{:S(2)}) copy-start(s32[12]{0:T(128)S(1)} %fusion.21) | copy-start | bytes 148
  243.5 59.3 %copy-start.5 = (f32[4,128]{1,0:T(4,128)S(1)}, f32[4,128]{1,0:T(4,128)}, u32[]{:S(2)}) copy-start(f32[4,128]{1,0:T(4,128)} %param.20) | copy-start | bytes 6148
  302.5 2.3 copy-start.1
  304.7 913.2 %all-reduce.10.cloned.1.call-start = ((), (), s32[]{:S(2)}) async-start(), calls=%async_computation.1 | async-start | bytes 1048576
  710.2 74.4 %collective-permute-start.2 = (f32[3,1,128,128]{2,1,3,0:T(1,128)}, f32[3,1,128,128]{2,1,3,0:T(1,128)}, u32[]{:S(2)}, u32[]{:S(2)}) collective-permute-start(f32[3,1,128,128]{2,1,3,0:T(1,128)} %get-tuple-element.79), channel_id=1, source_target_pairs={{0,1},{1,2},{2,3},{3,4},{4,5},{5,6},{6,7},{7,8},{8,9},{9,10},{10,1... | collective-permute-start | bytes 589832 | tf_op jit(solution)/shard_map/ppermute | solution.py:16
  711.4 74.3 %collective-permute-start.3 = (f32[3,1,128,128]{2,1,3,0:T(1,128)}, f32[3,1,128,128]{2,1,3,0:T(1,128)S(1)}, u32[]{:S(2)}, u32[]{:S(2)}) collective-permute-start(f32[3,1,128,128]{2,1,3,0:T(1,128)} %get-tuple-element.80), channel_id=1, source_target_pairs={{1,0},{2,1},{3,2},{4,3},{5,4},{6,5},{7,6},{8,7},{9,8},{10,9},{11,1... | collective-permute-start | bytes 589832 | tf_op jit(solution)/shard_map/ppermute | solution.py:17
  907.0 59.0 %copy-start.3 = (f32[4,128,128]{1,0,2:T(4,128)S(1)}, f32[4,128,128]{1,0,2:T(4,128)}, u32[]{:S(2)}) copy-start(f32[4,128,128]{1,0,2:T(4,128)} %copy-done.2) | copy-start | bytes 786436
Sparse Core Ops, SparseCore 0:
  304.8 247.6 all-reduce.7
  968.4 249.4 all-reduce.9
where the time goes:
time: 1320 us; the launch traced here: 1310 us
  waiting for transfers between devices  497 us (38%)
  blocking collectives  377 us (29%)
  other arithmetic  374 us (28%)
  local copies, waits for them, and re-layouts  39.3 us (3%)
  between operations  18.7 us (1%)
    unnamed x4, waiting for transfers between devices  496 us
    add x6, other arithmetic, stencil_part(): outputs[out_comp]  355 us
    psum x2, blocking collectives, residual_squares(): return lax.psum(jnp.sum(residual * residual), 'slab')  151 us
    all_gather x2, blocking collectives, contact_gather(): all_faces = lax.all_gather(master, 'slab', axis=0, tiled=True)  148 us
    psum x1, blocking collectives, local(): curvature = lax.psum(jnp.sum(direction * image), 'slab')  77.6 us
    slice x14, local copies, waits for them, and re-layouts, stencil_part(): stencil[offset_index, out_comp, in_comp] * window_view[in_comp]  27.6 us
  transfers between devices with their start and end apart: 6, of which 2 were waited for; matrix products, arithmetic and copies ran while one was open for 3% of the time, Pallas kernels for 0%

commit v1 on v0

v1 whole, which is shorter than its diff:
```python
import functools
import jax
import jax.numpy as jnp
from jax import lax
from jax.experimental import pallas as pl
from jax.experimental.pallas import tpu as pltpu
from jax.sharding import PartitionSpec as P

F32 = jnp.float32
VMEM_LIMIT = 24 * 1024 * 1024
W = 128
PLANES = 4
HALO = 3 * W


def vmem():
    return pl.BlockSpec(memory_space=pltpu.VMEM)


def smem():
    return pl.BlockSpec(memory_space=pltpu.SMEM)


def f32(*shape):
    return jax.ShapeDtypeStruct(shape, F32)


def call(kernel, outs, ins, scratch=(), flops=1000, name=None):
    return pl.pallas_call(
        kernel,
        out_shape=outs,
        in_specs=ins,
        out_specs=jax.tree.map(lambda _: vmem(), outs),
        scratch_shapes=list(scratch),
        compiler_params=pltpu.CompilerParams(vmem_limit_bytes=VMEM_LIMIT),
        cost_estimate=pl.CostEstimate(flops=flops, bytes_accessed=1000000, transcendentals=0),
        name=name,
    )


def iota(axis, shape=(W, W)):
    return lax.broadcasted_iota(jnp.int32, shape, axis)


def shift_of(st):
    return (st[13, 0, 0] + st[13, 1, 1] + st[13, 2, 2]) * F32(1.0 / 3.0) + F32(2.125)


def columns_to_rows(columns):
    lane = iota(1)
    block = jnp.zeros((W, W), F32)
    for k, column in enumerate(columns):
        block = jnp.where(lane == k, column, block)
    return block.T


def pick(flag, yes, no):
    return jnp.where(flag, yes, no)


def pack_kernel(dev, field, mate, far):
    odd = dev[0] % 2 == 1
    for c in range(3):
        low, high = field[c, 0], field[c, PLANES - 1]
        mate[c * W : (c + 1) * W, :] = pick(odd, low, high)
        far[c * W : (c + 1) * W, :] = pick(odd, high, low)
    rows = columns_to_rows([field[2, t, :, 0:1] for t in range(PLANES)])[0:8, :]
    mate[HALO : HALO + 8, :] = rows
    far[HALO : HALO + 8, :] = rows


def fill_shifted(s):
    row = iota(0)

    def body(i, _):
        v = s[1, i]
        s[0, i] = jnp.where(row == 0, 0.0, pltpu.roll(v, 1, 0))
        s[2, i] = jnp.where(row == W - 1, 0.0, pltpu.roll(v, W - 1, 0))
        return 0

    lax.fori_loop(0, 18, body, 0)


BLOCK = 32


def sweep(s, st, emit, dots):
    lane = iota(1, (BLOCK, W))

    def body(it, dots):
        x = it // (W // BLOCK)
        y = pl.multiple_of((it % (W // BLOCK)) * BLOCK, BLOCK)
        rows = pl.ds(y, BLOCK)
        acc = [[None] * 3 for _ in range(3)]
        for dx in range(3):
            for dy in range(3):
                for e in range(3):
                    v = s[dy, e * 6 + x + dx, rows, :]
                    for dz in range(3):
                        for c in range(3):
                            term = st[9 * dx + 3 * dy + dz, c, e] * v
                            acc[dz][c] = term if acc[dz][c] is None else acc[dz][c] + term
        out = []
        for c in range(3):
            below = jnp.where(lane == 0, 0.0, pltpu.roll(acc[0][c], 1, 1))
            above = jnp.where(lane == W - 1, 0.0, pltpu.roll(acc[2][c], W - 1, 1))
            out.append(acc[1][c] + (below + above))
        return emit(x, rows, out, dots)

    return lax.fori_loop(0, PLANES * (W // BLOCK), body, dots)


def fold(v):
    return jnp.sum(v.reshape(BLOCK // 8, 8, W), axis=0)


def first_kernel(dev, st, field, mate, far, stiff, u, dots, s):
    odd = dev[0] % 2 == 1
    place = dev[0] % 128
    cut = jnp.logical_or(place == 63, place == 64)
    for c in range(3):
        a = mate[c * W : (c + 1) * W, :]
        b = pick(cut, 0.0, far[c * W : (c + 1) * W, :])
        s[1, c * 6] = pick(odd, a, b)
        s[1, c * 6 + 5] = pick(odd, b, a)
        for x in range(PLANES):
            s[1, c * 6 + 1 + x] = field[c, x]
    fill_shifted(s)
    theta = shift_of(st)

    def emit(x, rows, out, sums):
        square, energy = sums
        k = stiff[x, rows, :]
        for c in range(3):
            v = s[1, c * 6 + 1 + x, rows, :]
            image = out[c] + k * v
            u[c, x, rows, :] = image - theta * v
            square += fold(v * v)
            energy += fold(v * image)
        return square, energy

    zero = jnp.zeros((8, W), F32)
    square, energy = sweep(s, st, emit, (zero, zero))
    dots[0:8, :] = square
    dots[8:16, :] = energy


def contact(active, partner, field, table, dual, mortar, back, push_rows):
    back[...] = jnp.zeros(back.shape, F32)
    energy = jnp.zeros((W, 1), F32)
    weights = dual[...].T
    columns = []
    for t in range(PLANES):
        blocks = [mortar[t, s].astype(F32) for s in range(3)]
        slots = [4 * s + partner[t, s] % 4 for s in range(3)]
        total = jnp.zeros((W, W), F32)
        for s in range(3):
            total += blocks[s] * table[pl.ds(slots[s], 1), :]
        pulled = jnp.sum(total, axis=1, keepdims=True)
        weight = weights[:, t : t + 1]
        gap = weight * field(t) - pulled
        push = (F32(4.0) * active[t].astype(F32)) * gap
        energy += push * gap
        columns.append(weight * push)
        for s in range(3):
            row = jnp.sum(blocks[s] * push, axis=0, keepdims=True)
            back[pl.ds(slots[s], 1), :] = back[pl.ds(slots[s], 1), :] - row
    push_rows[...] = columns_to_rows(columns)[0:8, :]
    return energy


def contact0_kernel(dev, active, partner, faces, far, field, dual, mortar, back, push_rows, dots, table):
    odd = dev[0] % 2 == 1
    place = dev[0] % 128
    wrap = jnp.logical_or(place == 0, place == 127)
    own, mate = faces[0:4, :], faces[4:8, :]
    other = pick(wrap, far[HALO : HALO + 4, :], faces[8:12, :])
    table[0:4, :] = pick(odd, mate, other)
    table[4:8, :] = own
    table[8:12, :] = pick(odd, other, mate)
    energy = contact(
        active, partner, lambda t: field[0, t, :, W - 1 : W], table, dual, mortar, back, push_rows
    )
    dots[...] = jnp.where(iota(1, (8, W)) == 0, fold_column(energy), 0.0)


def fold_column(column):
    return jnp.sum(column.reshape(W // 8, 8, 1), axis=0)


def lists(pack, other, odd, swap_far, swap_next):
    own = pack[12:24, :]
    mate = pack[24:36, :]
    far = pick(swap_far, other[36:48, :], pack[36:48, :])
    far_mate = pick(swap_far, other[48:60, :], pack[48:60, :])
    mate_far = pick(swap_next, other[60:72, :], pack[60:72, :])
    m1 = pick(odd, mate, far)
    m2 = pick(odd, mate_far, far_mate)
    p1 = pick(odd, far, mate)
    p2 = pick(odd, far_mate, mate_far)
    return (
        m2[8:12] + m1[4:8] + own[0:4],
        m1[8:12] + own[4:8] + p1[0:4],
        own[8:12] + p1[4:8] + p2[0:4],
    )


def second_kernel(dev, st, u, mate, far, pack, cross, push, stiff, z, kz, dots, table, s, rows):
    odd = dev[0] % 2 == 1
    place = dev[0] % 128
    cut = jnp.logical_or(place == 63, place == 64)
    swap_far = jnp.logical_or(place == 0, place == 127)
    swap_next = jnp.logical_or(place == 1, place == 126)
    slave = lists(pack, cross, odd, swap_far, swap_next)
    master = lists(cross, pack, odd, swap_far, swap_next)
    other = pick(swap_far, pack[8:12, :], cross[8:12, :])
    table[0:4, :] = pick(odd, cross[4:8, :], other) + slave[0]
    table[4:8, :] = cross[0:4, :] + slave[1]
    table[8:12, :] = pick(odd, other, cross[4:8, :]) + slave[2]
    table[12:16, :] = jnp.zeros((4, W), F32)
    before = pick(place == 0, slave[0], master[0])
    after = pick(place == 127, slave[2], master[2])
    mate_push = mate[HALO + 16 : HALO + 20, :]
    far_push = far[HALO + 16 : HALO + 20, :]
    rows[...] = jnp.zeros((W, W), F32)
    rows[0:1, :] = before[3:4]
    rows[1:5, :] = master[1]
    rows[5:6, :] = after[0:1]
    rows[8:9, :] = pick(odd, mate_push, far_push)[3:4]
    rows[9:13, :] = push[0:4, :]
    rows[13:14, :] = pick(odd, far_push, mate_push)[0:1]
    columns = rows[...].T
    lane = iota(1)

    def corrected(plane, x):
        return (
            plane
            + jnp.where(lane == 0, columns[:, x : x + 1], 0.0)
            + jnp.where(lane == W - 1, columns[:, 8 + x : 9 + x], 0.0)
        )

    for c in range(3):
        a = mate[c * W : (c + 1) * W, :]
        b = far[c * W : (c + 1) * W, :]
        low, high = pick(odd, a, b), pick(odd, b, a)
        if c == 2:
            low, high = corrected(low, 0), corrected(high, 5)
        even = jnp.logical_not(odd)
        s[1, c * 6] = pick(jnp.logical_and(cut, even), 0.0, low)
        s[1, c * 6 + 5] = pick(jnp.logical_and(cut, odd), 0.0, high)
        for x in range(PLANES):
            v = u[c, x]
            if c == 2:
                v = corrected(v, x + 1)
            s[1, c * 6 + 1 + x] = v
            z[c, x] = v
    fill_shifted(s)

    def emit(x, rows, out, sums):
        square, energy = sums
        k = stiff[x, rows, :]
        for c in range(3):
            v = s[1, c * 6 + 1 + x, rows, :]
            image = out[c] + k * v
            kz[c, x, rows, :] = image
            square += fold(v * v)
            energy += fold(v * image)
        return square, energy

    zero = jnp.zeros((8, W), F32)
    square, energy = sweep(s, st, emit, (zero, zero))
    dots[0:8, :] = square
    dots[8:16, :] = energy


def contact1_kernel(active, partner, table, field, dual, mortar, dots_a, dots_c, dots_z, back, push_rows, dots):
    energy = contact(
        active, partner, lambda t: field[0, t, :, W - 1 : W], table, dual, mortar, back, push_rows
    )
    lane = iota(1, (8, W))
    bending = jnp.where(lane == 0, fold_column(energy), 0.0)
    values = (
        dots_a[0:8, :],
        dots_a[8:16, :] + dots_c[...],
        dots_z[0:8, :],
        dots_z[8:16, :] + bending,
    )
    row = jnp.zeros((8, W), F32)
    for k, value in enumerate(values):
        total = jnp.sum(jnp.sum(value, axis=0, keepdims=True), axis=1, keepdims=True)
        row = jnp.where(lane == k, total, row)
    dots[...] = row


def final_kernel(dev, st, field, z, kz, got, extra, push, inc, res):
    place = dev[0] % 128
    swap_far = jnp.logical_or(place == 0, place == 127)
    theta = shift_of(st)
    lane8 = iota(1, (8, W))
    row = jnp.sum(got[:, 0:8, :].reshape(8, 8, W), axis=0)[0:1, :]
    lane1 = iota(1, (1, W))

    def total(k):
        return jnp.sum(jnp.where(lane1 == k, row, 0.0), axis=1, keepdims=True)

    norm0, curve0, zz, zaz = total(0), total(1), total(2), total(3)
    step0 = norm0 / curve0
    lead = 1.0 - step0 * theta
    norm1 = step0 * step0 * zz - lead * lead * norm0
    rz = curve0 - theta * norm0
    zw = zz + theta * rz
    a = lead + norm1 / norm0
    curve1 = a * a * curve0 - 2.0 * a * step0 * zw + step0 * step0 * zaz
    step1 = norm1 / curve1
    both = step0 + step1 * a
    cross = step1 * step0
    keep = 1.0 - theta * both
    opposite = (dev[0] // 32) ^ 4
    master = got[opposite, 4:8, :] + pick(swap_far, extra[0:4, :], 0.0)
    block = jnp.concatenate([master, push[0:4, :], jnp.zeros((W - 8, W), F32)], axis=0)
    columns = block.T
    lane = iota(1)
    for c in range(3):
        for x in range(PLANES):
            r, v, k = field[c, x], z[c, x], kz[c, x]
            if c == 2:
                k = (
                    k
                    + jnp.where(lane == 0, columns[:, x : x + 1], 0.0)
                    + jnp.where(lane == W - 1, columns[:, 4 + x : 5 + x], 0.0)
                )
            inc[c, x] = both * r - cross * v
            res[c, x] = keep * r - both * v + cross * k


def pairs(f):
    return [(i, f(i) % 256) for i in range(256)]


MATE = pairs(lambda i: i ^ 1)
FAR = pairs(lambda i: i + 1 if i % 2 else i - 1)
CROSS = pairs(lambda i: i ^ 128)
PLANE_GROUPS = [[32 * a + b for b in range(32)] for a in range(8)]
COLUMN_GROUPS = [[32 * a + b for a in range(8)] for b in range(32)]


def swap(x, table):
    return lax.ppermute(x, "slab", table)


def local(rhs, stiff, stencil, dual, mortar, partner, active):
    dev = lax.axis_index("slab").astype(jnp.int32).reshape(1)
    shape = rhs.shape
    dual8 = jnp.concatenate([dual, jnp.zeros((W - PLANES, W), F32)], axis=0)
    face = pl.BlockSpec((1, PLANES, W, W), lambda i: (2, 0, 0, 0))

    def whole(n):
        return [vmem()] * n

    def contact_call(kernel, outs, ins, scratch, name):
        return pl.pallas_call(
            kernel,
            grid=(1,),
            out_shape=outs,
            in_specs=ins,
            out_specs=jax.tree.map(lambda _: vmem(), outs),
            scratch_shapes=scratch,
            compiler_params=pltpu.CompilerParams(vmem_limit_bytes=VMEM_LIMIT),
            cost_estimate=pl.CostEstimate(flops=2000000, bytes_accessed=1000000, transcendentals=0),
            name=name,
        )

    def pack(field, name):
        return call(
            pack_kernel, (f32(HALO + 8, W), f32(HALO + 8, W)), [smem(), vmem()], name=name
        )(dev, field)

    a_mate, a_far = pack(rhs, "pack0")
    g_mate = swap(a_mate, MATE)
    g_far = swap(a_far, FAR)
    own_faces = jnp.concatenate(
        [a_mate[HALO : HALO + 4], g_mate[HALO : HALO + 4], g_far[HALO : HALO + 4], jnp.zeros((4, W), F32)]
    )
    faces = swap(own_faces, CROSS)
    u, dots_a = call(
        first_kernel,
        (f32(*shape), f32(16, W)),
        [smem(), smem()] + whole(4),
        [pltpu.VMEM((3, 18, W, W), F32)],
        flops=40000000,
        name="first",
    )(dev, stencil, rhs, g_mate, g_far, stiff)
    back0, push0, dots_c = contact_call(
        contact0_kernel,
        (f32(16, W), f32(8, W), f32(8, W)),
        [smem(), smem(), smem(), vmem(), vmem(), face, vmem(), vmem()],
        [pltpu.VMEM((16, W), F32)],
        "contact0",
    )(dev, active, partner, faces, g_far, rhs, dual8, mortar)
    b_mate, b_far = pack(u, "pack1")
    items = jnp.concatenate([back0[0:12], push0[0:4]])
    b_mate = jnp.concatenate([b_mate[: HALO + 4], back0[0:12], push0[0:4]])
    h_mate = swap(b_mate, MATE)
    b_far = jnp.concatenate([b_far[: HALO + 4], back0[0:12], push0[0:4], h_mate[HALO + 4 : HALO + 16]])
    h_far = swap(b_far, FAR)
    h_next = swap(h_far[HALO + 4 : HALO + 16], MATE)
    pack_own = jnp.concatenate(
        [
            b_mate[HALO : HALO + 4],
            h_mate[HALO : HALO + 4],
            h_far[HALO : HALO + 4],
            back0[0:12],
            h_mate[HALO + 4 : HALO + 16],
            h_far[HALO + 4 : HALO + 16],
            h_far[HALO + 20 : HALO + 32],
            h_next,
        ]
    )
    cross = swap(pack_own, CROSS)
    z, kz, dots_z, table = call(
        second_kernel,
        (f32(*shape), f32(*shape), f32(16, W), f32(16, W)),
        [smem(), smem()] + whole(7),
        [pltpu.VMEM((3, 18, W, W), F32), pltpu.VMEM((W, W), F32)],
        flops=40000000,
        name="second",
    )(dev, stencil, u, h_mate, h_far, pack_own, cross, push0, stiff)
    back1, push1, row = contact_call(
        contact1_kernel,
        (f32(16, W), f32(8, W), f32(8, W)),
        [smem(), smem(), vmem(), face] + whole(5),
        [],
        "contact1",
    )(active, partner, table, z, dual8, mortar, dots_a, dots_c, dots_z)

    odd = dev[0] % 2 == 1
    place = dev[0] % 128
    swap_far = jnp.logical_or(place == 0, place == 127)
    from_mate = swap(back1, MATE)
    from_far = swap(back1, FAR)
    stage1 = lax.all_to_all(
        jnp.broadcast_to(row[0:1], (32, W)), "slab", 0, 0, tiled=True, axis_index_groups=PLANE_GROUPS
    )
    sums = jnp.sum(stage1, axis=0, keepdims=True)
    far_part = jnp.where(odd, from_far[0:4], from_far[8:12])
    mate_part = jnp.where(odd, from_mate[8:12], from_mate[0:4])
    total = back1[4:8] + mate_part + jnp.where(swap_far, 0.0, far_part)
    block = jnp.concatenate([sums, jnp.zeros((3, W), F32), total])
    got = lax.all_to_all(
        jnp.broadcast_to(block[None], (8, 8, W)), "slab", 0, 0, tiled=True, axis_index_groups=COLUMN_GROUPS
    )
    return call(
        final_kernel,
        (f32(*shape), f32(*shape)),
        [smem(), smem()] + whole(6),
        flops=1000000,
        name="final",
    )(dev, stencil, rhs, z, kz, got, far_part, push1)


def solution(mesh):
    placed = (
        P(None, "slab", None, None),
        P("slab", None, None),
        P(),
        P("slab", None),
        P("slab", None, None, None),
        P("slab", None),
        P("slab"),
    )
    return jax.shard_map(
        local,
        mesh=mesh,
        in_specs=placed,
        out_specs=(P(None, "slab", None, None), P(None, "slab", None, None)),
        check_vma=False,
    )
```

time: 1320 us -> 94.6 us (0.07)
  waiting for transfers between devices: 497 us -> 20.5 us
  other arithmetic: 374 us -> 0.16 us
  blocking collectives: 377 us -> 12.2 us
  local copies, waits for them, and re-layouts: 39.3 us -> 5.9 us
  starting transfers between devices: 4.7 us -> 33.6 us
  Pallas kernels: 0 us -> 21.2 us
  between operations: 18.7 us -> 0.82 us
    unnamed x4 -> x0, waiting for transfers between devices: 496 us -> none
    add x9 -> x1, other arithmetic: 356 us -> 0.01 us  [local(): total = back1[4:8] + mate_part + jnp.where(swap_far, 0.0, far_part)]
    psum x3 -> x0, blocking collectives: 229 us -> none  [the longest x2 151 us: residual_squares(): return lax.psum(jnp.sum(residual * residual), 'slab')]
    all_gather x2 -> x0, blocking collectives: 148 us -> none  [contact_gather(): all_faces = lax.all_gather(master, 'slab', axis=0, tiled=True)]
    slice x20 -> x11, local copies, waits for them, and re-layouts: 31 us -> 0.03 us  [the longest x1 0.01 us: local(): b_mate = jnp.concatenate([b_mate[:HALO + 4], back0[0:12], push0[0:4]])]
    ppermute x4 -> x9, starting transfers between devices: 4.62 us -> 30 us  [swap(): return lax.ppermute(x, 'slab', table)]
    pallas_call x0 -> x7, Pallas kernels: none -> 21.2 us  [the longest x1 7.7 us: local(): call(second_kernel, (f32(*shape), f32(*shape), f32(16, W), f32(16, W)), [...]
    ppermute x4 -> x9, waiting for transfers between devices: 0.02 us -> 13.6 us  [swap(): return lax.ppermute(x, 'slab', table)]
  transfers between devices with their start and end apart: 6 -> 10, of which waited for: 2 -> 6; matrix products, arithmetic and copies ran while one was open for 3% -> 1% of each run, Pallas kernels for 0% -> 8%
where the time goes in v1:
time: 94.6 us; the launch traced here: 94.3 us
  starting transfers between devices  33.6 us (36%)
  Pallas kernels  21.2 us (22%)
  waiting for transfers between devices  20.5 us (22%)
  blocking collectives  12.2 us (13%)
  local copies, waits for them, and re-layouts  5.9 us (6%)
    ppermute x9, starting transfers between devices, swap(): return lax.ppermute(x, 'slab', table)  30 us
    ppermute x9, waiting for transfers between devices, swap(): return lax.ppermute(x, 'slab', table)  13.6 us
    all_to_all x1, blocking collectives, local(): lax.all_to_all(jnp.broadcast_to(block[None], (8, 8, W)), 'slab', 0, 0, ti...  12.2 us
    pallas_call x1, Pallas kernels, local(): call(second_kernel, (f32(*shape), f32(*shape), f32(16, W), f32(16, W)), [...  7.7 us
    pallas_call x1, Pallas kernels, local(): call(first_kernel, (f32(*shape), f32(16, W)), [smem(), smem()] + whole(4)...  7.39 us
    all_to_all x1, waiting for transfers between devices, local(): lax.all_to_all(jnp.broadcast_to(row[0:1], (32, W)), 'slab', 0, 0, tiled=T...  6.84 us
    unnamed x27, local copies, waits for them, and re-layouts  4.82 us
    all_to_all x1, starting transfers between devices, local(): lax.all_to_all(jnp.broadcast_to(row[0:1], (32, W)), 'slab', 0, 0, tiled=T...  3.62 us
  transfers between devices with their start and end apart: 10, of which 6 were waited for; matrix products, arithmetic and copies ran while one was open for 1% of the time, Pallas kernels for 8%

profile of v1, /device:TPU:1, one launch (start us, length us, event | category | flops | bytes accessed | tf_op | source)
XLA Modules:
  0.0 94.3 jit_solution(3041671890984899219)
XLA Ops:
  0.6 1.1 %copy-done = f32[3,4,128,128]{3,2,1,0:T(8,128)S(1)} copy-done((f32[3,4,128,128]{3,2,1,0:T(8,128)S(1)}, f32[3,4,128,128]{3,2,1,0:T(8,128)}, u32[]{:S(2)}) %copy-start) | copy-done | bytes 786456
  1.9 2.7 %collective-permute-start.1 = (f32[392,128]{1,0:T(8,128)S(1)}, f32[392,128]{1,0:T(8,128)S(1)}, u32[]{:S(2)}, u32[]{:S(2)}) collective-permute-start(f32[392,128]{1,0:T(8,128)S(1)} %get-tuple-element.19), channel_id=1, source_target_pairs={{0,255},{1,2},{2,1},{3,4},{4,3},{5,6},{6,5},{7,8},{8,7},{9,10},{10... | collective-permute-start | bytes 602120 | tf_op jit(solution)/shard_map/ppermute | solution.py:348
  4.7 8.8 %collective-permute-start = (f32[392,128]{1,0:T(8,128)S(1)}, f32[392,128]{1,0:T(8,128)S(1)}, u32[]{:S(2)}, u32[]{:S(2)}) collective-permute-start(f32[392,128]{1,0:T(8,128)S(1)} %get-tuple-element.18), channel_id=1, source_target_pairs={{0,1},{1,0},{2,3},{3,2},{4,5},{5,4},{6,7},{7,6},{8,9},{9,8},{10,11... | collective-permute-start | bytes 602120 | tf_op jit(solution)/shard_map/ppermute | solution.py:348
  13.4 1.1 %collective-permute-done.mate = f32[392,128]{1,0:T(8,128)S(1)} collective-permute-done((f32[392,128]{1,0:T(8,128)S(1)}, f32[392,128]{1,0:T(8,128)S(1)}, u32[]{:S(2)}, u32[]{:S(2)}) %collective-permute-start) | collective-permute-done | bytes 200736 | tf_op jit(solution)/shard_map/ppermute | solution.py:348
  14.5 1.2 %collective-permute-start.2 = (f32[16,128]{1,0:T(8,128)S(1)}, f32[16,128]{1,0:T(8,128)S(1)}, u32[]{:S(2)}, u32[]{:S(2)}) collective-permute-start(f32[16,128]{1,0:T(8,128)S(1)} %pad_maximum_fusion.2), channel_id=1, source_target_pairs={{0,128},{1,129},{2,130},{3,131},{4,132},{5,133},{6,134},{7,135},{8... | collective-permute-start | bytes 24584 | tf_op jit(solution)/shard_map/ppermute | solution.py:348
  16.0 0.9 copy-done.3
  16.9 7.4 %first.1 = (f32[3,4,128,128]{3,2,1,0:T(8,128)S(1)}, f32[16,128]{1,0:T(8,128)S(1)}) custom-call(s32[1]{0:T(128)} %bitcast.dev, f32[27,3,3]{2,1,0:T(4,128)S(1)} %copy.18.st, f32[3,4,128,128]{3,2,1,0:T(8,128)S(1)} %copy-done.1, f32[392,128]{1,0:T(8,128)S(1)} %collective-permute-done.mate, f32[392,128]{1,0:T(8,128)S(1)} %collective-permute-done.1.far, ...), custom_call_target="tpu_custom_call" | custom-call | flops 40000000 | bytes 1000000 | tf_op jit(solution)/shard_map/first/pallas_call | solution.py:385
  25.3 1.4 %contact0.1 = (f32[16,128]{1,0:T(8,128)S(1)}, f32[8,128]{1,0:T(8,128)S(1)}, f32[8,128]{1,0:T(8,128)S(1)}) custom-call(s32[1]{0:T(128)} %bitcast.dev, s32[4]{0:T(128)S(1)} %copy-done.10, s32[4,3]{1,0:T(4,128)S(1)} %copy-done.9, f32[16,128]{1,0:T(8,128)S(1)} %collective-permute-done.2.faces, f32[392,128]{1,0:T(8,128)S(1)} %collective-permute-done.1.far, ...), custom_call_target="tpu_custom_call" | custom-call | flops 2000000 | bytes 1000000 | tf_op jit(solution)/shard_map/contact0/pallas_call | solution.py:393
  26.8 5.7 %collective-permute-start.3 = (f32[404,128]{1,0:T(8,128)S(1)}, f32[404,128]{1,0:T(8,128)S(1)}, u32[]{:S(2)}, u32[]{:S(2)}) collective-permute-start(f32[404,128]{1,0:T(8,128)S(1)} %pad_maximum_fusion.1), channel_id=1, source_target_pairs={{0,1},{1,0},{2,3},{3,2},{4,5},{5,4},{6,7},{7,6},{8,9},{9,8},{10,11... | collective-permute-start | bytes 620552 | tf_op jit(solution)/shard_map/ppermute | solution.py:348
  32.4 1.1 %collective-permute-done.3.mate = f32[404,128]{1,0:T(8,128)S(1)} collective-permute-done((f32[404,128]{1,0:T(8,128)S(1)}, f32[404,128]{1,0:T(8,128)S(1)}, u32[]{:S(2)}, u32[]{:S(2)}) %collective-permute-start.3) | collective-permute-done | bytes 206880 | tf_op jit(solution)/shard_map/ppermute | solution.py:348
  33.7 5.3 %collective-permute-done.4.far = f32[416,128]{1,0:T(8,128)S(1)} collective-permute-done((f32[416,128]{1,0:T(8,128)S(1)}, f32[416,128]{1,0:T(8,128)S(1)}, u32[]{:S(2)}, u32[]{:S(2)}) %collective-permute-start.4) | collective-permute-done | bytes 213024 | tf_op jit(solution)/shard_map/ppermute | solution.py:348
  38.9 5.8 %collective-permute-start.5 = (f32[12,128]{1,0:T(8,128)S(1)}, f32[12,128]{1,0:T(8,128)S(1)}, u32[]{:S(2)}, u32[]{:S(2)}) collective-permute-start(f32[12,128]{1,0:T(8,128)S(1)} %get-tuple-element.37), channel_id=1, source_target_pairs={{0,1},{1,0},{2,3},{3,2},{4,5},{5,4},{6,7},{7,6},{8,9},{9,8},{10,11... | collective-permute-start | bytes 18440 | tf_op jit(solution)/shard_map/ppermute | solution.py:348
  44.8 0.8 collective-permute-done.5
  45.9 1.3 %collective-permute-start.6 = (f32[72,128]{1,0:T(8,128)S(1)}, f32[72,128]{1,0:T(8,128)S(1)}, u32[]{:S(2)}, u32[]{:S(2)}) collective-permute-start(f32[72,128]{1,0:T(8,128)S(1)} %concatenate.22.pack), channel_id=1, source_target_pairs={{0,128},{1,129},{2,130},{3,131},{4,132},{5,133},{6,134},{7,135},{8... | collective-permute-start | bytes 110600 | tf_op jit(solution)/shard_map/ppermute | solution.py:348
  47.3 5.4 %collective-permute-done.6.cross = f32[72,128]{1,0:T(8,128)S(1)} collective-permute-done((f32[72,128]{1,0:T(8,128)S(1)}, f32[72,128]{1,0:T(8,128)S(1)}, u32[]{:S(2)}, u32[]{:S(2)}) %collective-permute-start.6) | collective-permute-done | bytes 36896 | tf_op jit(solution)/shard_map/ppermute | solution.py:348
  52.7 0.9 copy-done.8
  53.7 7.7 %second.1 = (f32[3,4,128,128]{3,2,1,0:T(8,128)S(1)}, f32[3,4,128,128]{3,2,1,0:T(8,128)S(1)}, f32[16,128]{1,0:T(8,128)S(1)}, f32[16,128]{1,0:T(8,128)S(1)}) custom-call(s32[1]{0:T(128)} %bitcast.dev, f32[27,3,3]{2,1,0:T(4,128)S(1)} %copy.18.st, f32[3,4,128,128]{3,2,1,0:T(8,128)S(1)} %get-tuple-element.20.field.u, f32[404,128]{1,0:T(8,128)S(1)} %copy-done.8, ...), custom_call_target="tpu_custom_call" | custom-call | flops 40000000 | bytes 1000000 | tf_op jit(solution)/shard_map/second/pallas_call | solution.py:420
  61.4 0.9 copy-done.5
  62.3 1.4 %contact1.1 = (f32[16,128]{1,0:T(8,128)S(1)}, f32[8,128]{1,0:T(8,128)S(1)}, f32[8,128]{1,0:T(8,128)S(1)}) custom-call(s32[4]{0:T(128)S(1)} %copy-done.10, s32[4,3]{1,0:T(4,128)S(1)} %copy-done.9, f32[16,128]{1,0:T(8,128)S(1)} %get-tuple-element.27.table, f32[3,4,128,128]{3,2,1,0:T(8,128)S(1)} %get-tuple-element.25.field.z, f32[128,128]{1,0:T(8,128)S(1)} %concatenate.19.dual, ...), custom_call_target="tpu_custom_call" | custom-call | flops 2000000 | bytes 1000000 | tf_op jit(solution)/shard_map/contact1/pallas_call | solution.py:428
  63.7 4.2 %collective-permute-start.7 = (f32[16,128]{1,0:T(8,128)S(1)}, f32[16,128]{1,0:T(8,128)S(1)}, u32[]{:S(2)}, u32[]{:S(2)}) collective-permute-start(f32[16,128]{1,0:T(8,128)S(1)} %get-tuple-element.32), channel_id=1, source_target_pairs={{0,1},{1,0},{2,3},{3,2},{4,5},{5,4},{6,7},{7,6},{8,9},{9,8},{10,11... | collective-permute-start | bytes 24584 | tf_op jit(solution)/shard_map/ppermute | solution.py:348
  68.6 3.6 %all-to-all-start = ((f32[32,1,128]{2,1,0:T(1,128)}), f32[32,1,128]{2,1,0:T(1,128)S(1)}, u32[]{:S(2)}, u32[]{:S(2)}) async-start(f32[32,1,128]{2,1,0:T(1,128)} %broadcast_in_dim.24), calls=%async_computation | async-start | bytes 32768 | tf_op jit(solution)/shard_map/all_to_all | solution.py:441
  72.3 6.8 %all-to-all-done = f32[32,1,128]{2,1,0:T(1,128)S(1)} async-done(((f32[32,1,128]{2,1,0:T(1,128)}), f32[32,1,128]{2,1,0:T(1,128)S(1)}, u32[]{:S(2)}, u32[]{:S(2)}) %all-to-all-start) | async-done | bytes 16416 | tf_op jit(solution)/shard_map/all_to_all | solution.py:441
  79.2 12.2 %all_to_all.11.got = f32[8,8,128]{2,1,0:T(8,128)S(1)} all-to-all(f32[8,8,128]{2,1,0:T(8,128)S(1)} %broadcast_in_dim.27), channel_id=1, replica_groups={{0,32,64,96,128,160,192,224},{1,33,65,97,129,161,193,225},{2,34,66,98,1..., dimensions={0} | all-to-all | bytes 65536 | tf_op jit(solution)/shard_map/all_to_all | solution.py:449
  91.4 2.9 %final.1 = (f32[3,4,128,128]{3,2,1,0:T(8,128)}, f32[3,4,128,128]{3,2,1,0:T(8,128)}) custom-call(s32[1]{0:T(128)} %bitcast.dev, f32[27,3,3]{2,1,0:T(4,128)S(1)} %copy.18.st, f32[3,4,128,128]{3,2,1,0:T(8,128)S(1)} %copy-done.1, f32[3,4,128,128]{3,2,1,0:T(8,128)S(1)} %get-tuple-element.25.field.z, f32[3,4,128,128]{3,2,1,0:T(8,128)S(1)} %copy-done.6, ...), custom_call_target="tpu_custom_call" | custom-call | flops 1000000 | bytes 1000000 | tf_op jit(solution)/shard_map/final/pallas_call | solution.py:452
  (55 shorter events, 2.7 us)
Async XLA Ops:
  0.6 1.1 %copy-start = (f32[3,4,128,128]{3,2,1,0:T(8,128)S(1)}, f32[3,4,128,128]{3,2,1,0:T(8,128)}, u32[]{:S(2)}) copy-start(f32[3,4,128,128]{3,2,1,0:T(8,128)} %field.7) | copy-start | bytes 2359300
  1.8 14.2 %copy-start.1 = (f32[3,4,128,128]{3,2,1,0:T(8,128)S(1)}, f32[3,4,128,128]{3,2,1,0:T(8,128)}, u32[]{:S(2)}) copy-start(f32[3,4,128,128]{3,2,1,0:T(8,128)} %field.7) | copy-start | bytes 2359300
  1.9 11.5 %collective-permute-start.1 = (f32[392,128]{1,0:T(8,128)S(1)}, f32[392,128]{1,0:T(8,128)S(1)}, u32[]{:S(2)}, u32[]{:S(2)}) collective-permute-start(f32[392,128]{1,0:T(8,128)S(1)} %get-tuple-element.19), channel_id=1, source_target_pairs={{0,255},{1,2},{2,1},{3,4},{4,3},{5,6},{6,5},{7,8},{8,7},{9,10},{10... | collective-permute-start | bytes 602120 | tf_op jit(solution)/shard_map/ppermute | solution.py:348
  4.7 9.8 %collective-permute-start = (f32[392,128]{1,0:T(8,128)S(1)}, f32[392,128]{1,0:T(8,128)S(1)}, u32[]{:S(2)}, u32[]{:S(2)}) collective-permute-start(f32[392,128]{1,0:T(8,128)S(1)} %get-tuple-element.18), channel_id=1, source_target_pairs={{0,1},{1,0},{2,3},{3,2},{4,5},{5,4},{6,7},{7,6},{8,9},{9,8},{10,11... | collective-permute-start | bytes 602120 | tf_op jit(solution)/shard_map/ppermute | solution.py:348
  14.5 1.3 %copy-start.11 = (f32[27,3,3]{0,2,1:T(4,128)S(1)}, f32[27,3,3]{0,2,1:T(4,128)}, u32[]{:S(2)}) copy-start(f32[27,3,3]{0,2,1:T(4,128)} %param.9) | copy-start | bytes 2920
  14.5 1.4 %copy-start.12 = (f32[4,128]{1,0:T(4,128)S(1)}, f32[4,128]{1,0:T(4,128)}, u32[]{:S(2)}) copy-start(f32[4,128]{1,0:T(4,128)} %param.10) | copy-start | bytes 6148
  14.5 10.0 %collective-permute-start.2 = (f32[16,128]{1,0:T(8,128)S(1)}, f32[16,128]{1,0:T(8,128)S(1)}, u32[]{:S(2)}, u32[]{:S(2)}) collective-permute-start(f32[16,128]{1,0:T(8,128)S(1)} %pad_maximum_fusion.2), channel_id=1, source_target_pairs={{0,128},{1,129},{2,130},{3,131},{4,132},{5,133},{6,134},{7,135},{8... | collective-permute-start | bytes 24584 | tf_op jit(solution)/shard_map/ppermute | solution.py:348
  15.9 1.0 %copy-start.3 = (f32[4,128,128]{2,1,0:T(8,128)S(1)}, f32[4,128,128]{2,1,0:T(8,128)}, u32[]{:S(2)}) copy-start(f32[4,128,128]{2,1,0:T(8,128)} %stiff.3) | copy-start | bytes 786436
  24.3 1.0 %copy-start.2 = (bf16[4,3,128,128]{3,2,1,0:T(8,128)(2,1)S(1)}, bf16[4,3,128,128]{3,2,1,0:T(8,128)(2,1)}, u32[]{:S(2)}) copy-start(bf16[4,3,128,128]{3,2,1,0:T(8,128)(2,1)} %mortar.3) | copy-start | bytes 1179652
  24.3 1.0 %copy-start.9 = (s32[4,3]{1,0:T(4,128)S(1)}, s32[4,3]{1,0:T(4,128)}, u32[]{:S(2)}) copy-start(s32[4,3]{1,0:T(4,128)} %partner.3) | copy-start | bytes 148
  24.3 1.0 %copy-start.10 = (s32[4]{0:T(128)S(1)}, s32[4]{0:T(128)}, u32[]{:S(2)}) copy-start(s32[4]{0:T(128)} %active.3) | copy-start | bytes 52
  26.8 6.8 %collective-permute-start.3 = (f32[404,128]{1,0:T(8,128)S(1)}, f32[404,128]{1,0:T(8,128)S(1)}, u32[]{:S(2)}, u32[]{:S(2)}) collective-permute-start(f32[404,128]{1,0:T(8,128)S(1)} %pad_maximum_fusion.1), channel_id=1, source_target_pairs={{0,1},{1,0},{2,3},{3,2},{4,5},{5,4},{6,7},{7,6},{8,9},{9,8},{10,11... | collective-permute-start | bytes 620552 | tf_op jit(solution)/shard_map/ppermute | solution.py:348
  33.5 11.2 %copy-start.7 = (f32[404,128]{1,0:T(8,128)}, f32[404,128]{1,0:T(8,128)S(1)}, u32[]{:S(2)}) copy-start(f32[404,128]{1,0:T(8,128)S(1)} %collective-permute-done.3.mate) | copy-start | bytes 620548
  33.5 19.2 %copy-start.4 = (f32[4,128,128]{2,1,0:T(8,128)S(1)}, f32[4,128,128]{2,1,0:T(8,128)}, u32[]{:S(2)}) copy-start(f32[4,128,128]{2,1,0:T(8,128)} %stiff.3) | copy-start | bytes 786436
  33.6 5.4 %collective-permute-start.4 = (f32[416,128]{1,0:T(8,128)S(1)}, f32[416,128]{1,0:T(8,128)S(1)}, u32[]{:S(2)}, u32[]{:S(2)}) collective-permute-start(f32[416,128]{1,0:T(8,128)S(1)} %pad_maximum_fusion), channel_id=1, source_target_pairs={{0,255},{1,2},{2,1},{3,4},{4,3},{5,6},{6,5},{7,8},{8,7},{9,10},{10... | collective-permute-start | bytes 638984 | tf_op jit(solution)/shard_map/ppermute | solution.py:348
  38.9 6.6 %collective-permute-start.5 = (f32[12,128]{1,0:T(8,128)S(1)}, f32[12,128]{1,0:T(8,128)S(1)}, u32[]{:S(2)}, u32[]{:S(2)}) collective-permute-start(f32[12,128]{1,0:T(8,128)S(1)} %get-tuple-element.37), channel_id=1, source_target_pairs={{0,1},{1,0},{2,3},{3,2},{4,5},{5,4},{6,7},{7,6},{8,9},{9,8},{10,11... | collective-permute-start | bytes 18440 | tf_op jit(solution)/shard_map/ppermute | solution.py:348
  44.7 0.8 slice-start
  45.9 6.8 %collective-permute-start.6 = (f32[72,128]{1,0:T(8,128)S(1)}, f32[72,128]{1,0:T(8,128)S(1)}, u32[]{:S(2)}, u32[]{:S(2)}) collective-permute-start(f32[72,128]{1,0:T(8,128)S(1)} %concatenate.22.pack), channel_id=1, source_target_pairs={{0,128},{1,129},{2,130},{3,131},{4,132},{5,133},{6,134},{7,135},{8... | collective-permute-start | bytes 110600 | tf_op jit(solution)/shard_map/ppermute | solution.py:348
  52.7 0.9 copy-start.8
  61.4 0.9 copy-start.5
  62.3 29.1 %copy-start.6 = (f32[3,4,128,128]{3,2,1,0:T(8,128)S(1)}, f32[3,4,128,128]{3,2,1,0:T(8,128)}, u32[]{:S(2)}) copy-start(f32[3,4,128,128]{3,2,1,0:T(8,128)} %copy-done.5) | copy-start | bytes 2359300
  63.7 8.6 %collective-permute-start.8 = (f32[16,128]{1,0:T(8,128)S(1)}, f32[16,128]{1,0:T(8,128)S(1)}, u32[]{:S(2)}, u32[]{:S(2)}) collective-permute-start(f32[16,128]{1,0:T(8,128)S(1)} %get-tuple-element.32), channel_id=1, source_target_pairs={{0,255},{1,2},{2,1},{3,4},{4,3},{5,6},{6,5},{7,8},{8,7},{9,10},{10... | collective-permute-start | bytes 24584 | tf_op jit(solution)/shard_map/ppermute | solution.py:348
  63.7 8.5 %collective-permute-start.7 = (f32[16,128]{1,0:T(8,128)S(1)}, f32[16,128]{1,0:T(8,128)S(1)}, u32[]{:S(2)}, u32[]{:S(2)}) collective-permute-start(f32[16,128]{1,0:T(8,128)S(1)} %get-tuple-element.32), channel_id=1, source_target_pairs={{0,1},{1,0},{2,3},{3,2},{4,5},{5,4},{6,7},{7,6},{8,9},{9,8},{10,11... | collective-permute-start | bytes 24584 | tf_op jit(solution)/shard_map/ppermute | solution.py:348
  68.6 10.5 %all-to-all-start = ((f32[32,1,128]{2,1,0:T(1,128)}), f32[32,1,128]{2,1,0:T(1,128)S(1)}, u32[]{:S(2)}, u32[]{:S(2)}) async-start(f32[32,1,128]{2,1,0:T(1,128)} %broadcast_in_dim.24), calls=%async_computation | async-start | bytes 32768 | tf_op jit(solution)/shard_map/all_to_all | solution.py:441

commit v2 on v0

v2 whole, which is shorter than its diff:
```python
import functools
import jax
import jax.numpy as jnp
from jax import lax
from jax.experimental import pallas as pl
from jax.experimental.pallas import tpu as pltpu
from jax.sharding import PartitionSpec as P

F32 = jnp.float32
VMEM_LIMIT = 24 * 1024 * 1024
W = 128
PLANES = 4
HALO = 3 * W


def vmem():
    return pl.BlockSpec(memory_space=pltpu.VMEM)


def smem():
    return pl.BlockSpec(memory_space=pltpu.SMEM)


def f32(*shape):
    return jax.ShapeDtypeStruct(shape, F32)


def anywhere():
    return pl.BlockSpec(memory_space=pl.ANY)


def call(kernel, name, ins, outs, scratch=(), cost=1000000, out_specs=None):
    return pl.pallas_call(
        kernel,
        out_shape=outs,
        in_specs=ins,
        out_specs=jax.tree.map(lambda _: vmem(), outs) if out_specs is None else out_specs,
        scratch_shapes=list(scratch),
        compiler_params=pltpu.CompilerParams(vmem_limit_bytes=VMEM_LIMIT),
        cost_estimate=pl.CostEstimate(flops=1000, bytes_accessed=cost, transcendentals=0),
        name=name,
    )


def iota(axis, shape=(W, W)):
    return lax.broadcasted_iota(jnp.int32, shape, axis)


def coefficient(st, k, c, e):
    return st[9 * k + 3 * c + e]


def shift_of(st):
    trace = coefficient(st, 13, 0, 0) + coefficient(st, 13, 1, 1) + coefficient(st, 13, 2, 2)
    return trace * F32(1.0 / 3.0) + F32(2.125)


def columns_to_rows(columns):
    lane = iota(1)
    block = jnp.zeros((W, W), F32)
    for k, column in enumerate(columns):
        block = jnp.where(lane == k, column, block)
    return block.T


def pick(flag, yes, no):
    return jnp.where(flag, yes, no)


def pick(flag, yes, no):
    return jnp.where(flag, yes, no)


def place_of(dev, at=0):
    odd = dev[at] % 2 == 1
    place = dev[at] % 128
    return odd, place


def is_cut(place):
    return jnp.logical_or(place == 63, place == 64)


def is_wrap(place):
    return jnp.logical_or(place == 0, place == 127)


def pack_kernel(dev, field, mate, far):
    odd, _ = place_of(dev)
    for c in range(3):
        low, high = field[c, 0], field[c, PLANES - 1]
        mate[c * W : (c + 1) * W, :] = pick(odd, low, high)
        far[c * W : (c + 1) * W, :] = pick(odd, high, low)
    rows = columns_to_rows([field[2, t, :, 0:1] for t in range(PLANES)])[0:8, :]
    mate[HALO : HALO + 8, :] = rows
    far[HALO : HALO + 8, :] = rows


BLOCK = 32


def fill_shifted(s, planes):
    row = iota(0)

    def body(c, _):
        for x in range(planes):
            i = c * planes + x
            v = s[1, i]
            s[0, i] = jnp.where(row == 0, 0.0, pltpu.roll(v, 1, 0))
            s[2, i] = jnp.where(row == W - 1, 0.0, pltpu.roll(v, W - 1, 0))
        return 0

    lax.fori_loop(0, 3, body, 0)


def sweep(s, st, planes, centre, emit):
    lane = iota(1, (BLOCK, W))
    steps = W // BLOCK

    def body(it, dots):
        x = it // steps
        y = pl.multiple_of((it % steps) * BLOCK, BLOCK)
        rows = pl.ds(y, BLOCK)
        acc = [[None] * 3 for _ in range(3)]
        for dx in range(3):
            for dy in range(3):
                for e in range(3):
                    v = s[dy, e * planes + centre(x) + dx - 1, rows, :]
                    for dz in range(3):
                        for c in range(3):
                            term = coefficient(st, 9 * dx + 3 * dy + dz, c, e) * v
                            acc[dz][c] = term if acc[dz][c] is None else acc[dz][c] + term
        out = []
        for c in range(3):
            below = jnp.where(lane == 0, 0.0, pltpu.roll(acc[0][c], 1, 1))
            above = jnp.where(lane == W - 1, 0.0, pltpu.roll(acc[2][c], W - 1, 1))
            out.append(acc[1][c] + (below + above))
        values = [s[1, c * planes + centre(x), rows, :] for c in range(3)]
        return emit(x, rows, out, values, dots)

    zero = jnp.zeros((8, W), F32)
    return lax.fori_loop(0, 2 * steps, body, (zero, zero))


def fold(v):
    return jnp.sum(v.reshape(BLOCK // 8, 8, W), axis=0)


def emitter(target, stiff, plane, theta):
    def emit(x, rows, out, values, sums):
        square, energy = sums
        k = stiff[plane(x), rows, :]
        for c in range(3):
            v = values[c]
            image = out[c] + k * v
            target[c, x, rows, :] = image if theta is None else image - theta * v
            square += fold(v * v)
            energy += fold(v * image)
        return square, energy

    return emit


def store_dots(dots, sums):
    dots[0:8, :] = sums[0]
    dots[8:16, :] = sums[1]


FACE_TERMS = [(3 * j + dz, c) for dz in range(3) for c in range(3) for j in range(9)]


def inner(x):
    return x + 1


def outer(x):
    return 3 * x


def inner_first_kernel(st, field, dual, stiff, mortar, ui, dots, stiff_v, mortar_v, weights, theta, s, sems):
    stiff_copy = pltpu.make_async_copy(stiff, stiff_v, sems.at[0])
    mortar_copy = pltpu.make_async_copy(mortar, mortar_v, sems.at[1])
    stiff_copy.start()
    mortar_copy.start()
    for c in range(3):
        for x in range(PLANES):
            s[1, c * 4 + x] = field[c, x]
    fill_shifted(s, 4)
    block = jnp.concatenate([dual[...], jnp.zeros((W - PLANES, W), F32)], axis=0)
    weights[...] = block.T
    stiff_copy.wait()
    theta[...] = jnp.full((8, W), shift_of(st), F32)
    store_dots(dots, sweep(s, st, 4, inner, emitter(ui, stiff_v, inner, shift_of(st))))
    mortar_copy.wait()


def fill_halo(dev, s, mate, far, edge_planes, inner_planes):
    odd, place = place_of(dev)
    cut = is_cut(place)
    for c in range(3):
        a = mate[c * W : (c + 1) * W, :]
        b = pick(cut, 0.0, far[c * W : (c + 1) * W, :])
        s[1, c * 6] = pick(odd, a, b)
        s[1, c * 6 + 5] = pick(odd, b, a)
        s[1, c * 6 + 1] = edge_planes(c, 0)
        s[1, c * 6 + 4] = edge_planes(c, 1)
        s[1, c * 6 + 2] = inner_planes(c, 0)
        s[1, c * 6 + 3] = inner_planes(c, 1)
    fill_shifted(s, 6)


def face_rows(edge, mid):
    planes = (edge.at[2, 0], mid.at[2, 0], mid.at[2, 1], edge.at[2, 1])
    return columns_to_rows([p[:, 0:1] for p in planes] + [p[:, W - 1 : W] for p in planes])[0:8, :]


def centre6(x):
    return 3 * x + 1


def edge_first_kernel(dev, st, field, mate, far, stiff, ui, ue, dots, to_mate, to_far, s):
    odd, _ = place_of(dev)
    fill_halo(dev, s, mate, far, lambda c, i: field[c, 3 * i], lambda c, i: field[c, 1 + i])
    store_dots(dots, sweep(s, st, 6, centre6, emitter(ue, stiff, outer, shift_of(st))))
    for c in range(3):
        low, high = ue[c, 0], ue[c, 1]
        to_mate[c * W : (c + 1) * W, :] = pick(odd, low, high)
        to_far[c * W : (c + 1) * W, :] = pick(odd, high, low)
    rows = face_rows(ue, ui)
    to_mate[HALO : HALO + 8, :] = rows
    to_far[HALO : HALO + 8, :] = rows


def inner_second_kernel(st, ui, ue, stiff, ki, dots, stiff_rows, coefs, s):
    for c in range(3):
        s[1, c * 4] = ue[c, 0]
        s[1, c * 4 + 1] = ui[c, 0]
        s[1, c * 4 + 2] = ui[c, 1]
        s[1, c * 4 + 3] = ue[c, 1]
    fill_shifted(s, 4)
    store_dots(dots, sweep(s, st, 4, inner, emitter(ki, stiff, inner, None)))
    faces = [stiff[t, :, 0:1] for t in range(PLANES)] + [stiff[t, :, W - 1 : W] for t in range(PLANES)]
    stiff_rows[...] = columns_to_rows(faces)[0:8, :]
    for i, (k, c) in enumerate(FACE_TERMS):
        coefs[i : i + 1, :] = jnp.full((1, W), coefficient(st, k, c, 2), F32)


def edge_second_kernel(dev, st, ui, ue, mate, far, stiff, ki, ke, dots, rows, s):
    fill_halo(dev, s, mate, far, lambda c, i: ue[c, i], lambda c, i: ui[c, i])
    store_dots(dots, sweep(s, st, 6, centre6, emitter(ke, stiff, outer, None)))
    rows[...] = face_rows(ke, ki)


def contact(meta, slave, table, weights, mortar, back):
    energy = jnp.zeros((W, 1), F32)
    columns, pushes, slots = [], [], []
    for t in range(PLANES):
        total = None
        for s in range(3):
            row = table[pl.ds(4 * s + meta[3 * t + s], 1), :]
            term = mortar[t, s].astype(F32) * row
            total = term if total is None else total + term
        pulled = jnp.sum(total, axis=1, keepdims=True)
        weight = weights[:, t : t + 1]
        gap = weight * slave(t) - pulled
        push = (F32(4.0) * meta[12 + t].astype(F32)) * gap
        energy += push * gap
        columns.append(weight * push)
        pushes.append(push)
    for s in range(3):
        rows = [
            jnp.sum(mortar[t, s].astype(F32) * pushes[t], axis=0, keepdims=True) for t in range(PLANES)
        ]
        for k in range(4):
            total = None
            for t in range(PLANES):
                term = jnp.where(meta[3 * t + s] == k, rows[t], 0.0)
                total = term if total is None else total + term
            back[4 * s + k : 4 * s + k + 1, :] = -total
    return energy, columns


def fold_column(column):
    return jnp.where(iota(1, (8, W)) == 0, jnp.sum(column.reshape(W // 8, 8, 1), axis=0), 0.0)


def contact0_kernel(meta, faces, far, field, weights, mortar, items, push_cols, dots, table):
    odd, place = place_of(meta, 16)
    own, mate = faces[0:4, :], faces[4:8, :]
    other = pick(is_wrap(place), far[HALO : HALO + 4, :], faces[8:12, :])
    table[0:4, :] = pick(odd, mate, other)
    table[4:8, :] = own
    table[8:12, :] = pick(odd, other, mate)
    energy, columns = contact(
        meta, lambda t: field[2, t, :, W - 1 : W], table, weights, mortar, items
    )
    lane = iota(1)
    block = jnp.zeros((W, W), F32)
    for k, column in enumerate(columns):
        block = jnp.where(lane == k, column, block)
    push_cols[...] = block
    items[12:16, :] = block.T[0:4, :]
    dots[...] = fold_column(energy)


def lists(pack, other, odd, swap_far, swap_next):
    own = pack[12:24, :]
    mate = pack[24:36, :]
    far = pick(swap_far, other[36:48, :], pack[36:48, :])
    far_mate = pick(swap_far, other[48:60, :], pack[48:60, :])
    mate_far = pick(swap_next, other[60:72, :], pack[60:72, :])
    m1 = pick(odd, mate, far)
    m2 = pick(odd, mate_far, far_mate)
    p1 = pick(odd, far, mate)
    p2 = pick(odd, far_mate, mate_far)
    return (
        m2[8:12] + m1[4:8] + own[0:4],
        m1[8:12] + own[4:8] + p1[0:4],
        own[8:12] + p1[4:8] + p2[0:4],
    )


def total_of(v):
    return jnp.sum(jnp.sum(v, axis=0, keepdims=True), axis=1, keepdims=True)


def join_kernel(
    meta, coefs, ui, ue, mate, far, pack, cross, items, push_cols, stiff_rows, u_rows, k_rows,
    weights, mortar, dots_ui, dots_ue, dots_c, dots_ki, dots_ke,
    send, k_cols, table, back,
):
    odd, place = place_of(meta, 16)
    cut, swap_far = is_cut(place), is_wrap(place)
    even = jnp.logical_not(odd)
    swap_next = jnp.logical_or(place == 1, place == 126)
    slave = lists(pack, cross, odd, swap_far, swap_next)
    master = lists(cross, pack, odd, swap_far, swap_next)
    other = pick(swap_far, pack[8:12, :], cross[8:12, :])
    table[0:4, :] = pick(odd, cross[4:8, :], other) + slave[0]
    table[4:8, :] = cross[0:4, :] + slave[1]
    table[8:12, :] = pick(odd, other, cross[4:8, :]) + slave[2]

    def slave_column(t):
        plane = ue.at[2, t // 3] if t in (0, 3) else ui.at[2, t - 1]
        return plane[:, W - 1 : W] + push_cols[:, t : t + 1]

    energy, columns = contact(meta, slave_column, table, weights, mortar, back)

    low = jnp.logical_and(cut, even)
    high = jnp.logical_and(cut, odd)
    own_total, own_push = master[1], items[12:16, :]
    before = pick(place == 0, slave[0], master[0])[3:4]
    after = pick(place == 127, slave[2], master[2])[0:1]
    mate_push = mate[HALO + 20 : HALO + 24, :]
    far_push = far[HALO + 20 : HALO + 24, :]
    push_before = pick(odd, mate_push, far_push)[3:4]
    push_after = pick(odd, far_push, mate_push)[0:1]
    totals = jnp.concatenate([pick(low, 0.0, before), own_total, pick(high, 0.0, after)], axis=0)
    pushes = jnp.concatenate([pick(low, 0.0, push_before), own_push, pick(high, 0.0, push_after)], axis=0)
    lane = iota(1, (PLANES, W))

    def shifts(rows6):
        out = []
        for dx in range(3):
            v = rows6[dx : dx + PLANES]
            out.append(
                (
                    jnp.where(lane == 0, 0.0, pltpu.roll(v, 1, 1)),
                    v,
                    jnp.where(lane == W - 1, 0.0, pltpu.roll(v, W - 1, 1)),
                )
            )
        return out

    lines = {}
    for k, (rows6, dz) in enumerate(((totals, 1), (totals, 0), (pushes, 2), (pushes, 1))):
        moved = shifts(rows6)
        for c in range(3):
            total = None
            for dx in range(3):
                for dy in range(3):
                    at = FACE_TERMS.index((9 * dx + 3 * dy + dz, c))
                    term = coefs[at : at + 1, :] * moved[dx][dy]
                    total = term if total is None else total + term
            lines[k, c] = total
    lines[0, 2] = lines[0, 2] + stiff_rows[0:4, :] * own_total
    lines[3, 2] = lines[3, 2] + stiff_rows[4:8, :] * own_push
    block = jnp.concatenate(
        [lines[k, c] for k in range(4) for c in range(3)] + [own_total, jnp.zeros((W - 52, W), F32)], axis=0
    )
    cols = block.T
    wide = iota(1)
    for t in range(PLANES):
        cols = jnp.where(wide == 44 + t, cols + columns[t], cols)
    k_cols[...] = cols

    face = own_total * u_rows[0:4, :] + own_push * u_rows[4:8, :]
    square = own_total * own_total + own_push * own_push
    image = own_total * (2.0 * k_rows[0:4, :] + lines[0, 2]) + own_push * (2.0 * k_rows[4:8, :] + lines[3, 2])
    values = (
        dots_ui[0:8, :] + dots_ue[0:8, :],
        dots_ui[8:16, :] + dots_ue[8:16, :] + dots_c[...],
        dots_ki[0:8, :] + dots_ke[0:8, :],
        dots_ki[8:16, :] + dots_ke[8:16, :] + fold_column(energy),
    )
    extra = (None, None, 2.0 * face + square, image)
    wide8 = iota(1, (8, W))
    row = jnp.zeros((8, W), F32)
    for k, value in enumerate(values):
        total = total_of(value)
        if extra[k] is not None:
            total = total + total_of(extra[k])
        row = jnp.where(wide8 == k, total, row)
    row = jnp.where(iota(0, (8, W)) == 0, row, 0.0)
    send[...] = jnp.broadcast_to(row[None], (32, 8, W))
    column = meta[16] % 32
    send[(column + 31) % 32, 4:8, :] = back[0:4, :]
    send[column, 4:8, :] = back[4:8, :]
    send[(column + 1) % 32, 4:8, :] = back[8:12, :]


def gather_kernel(u_rows, mate, far, following, items, pack):
    start = HALO + 8
    parts = [
        u_rows[0:4, :],
        mate[HALO : HALO + 4, :],
        far[HALO : HALO + 4, :],
        items[0:12, :],
        mate[start : start + 12, :],
        far[start : start + 12, :],
        far[start + 16 : start + 28, :],
        following[0:12, :],
    ]
    pack[...] = jnp.concatenate(parts, axis=0)


def relay_kernel(dev, got, send):
    column = dev[0] % 32
    level = dev[0] // 32
    dots = jnp.sum(got[:, 0:8, :], axis=0)
    first, last = column == 0, column == 31
    left = got[(column + 31) % 32, 4:8, :]
    right = got[(column + 1) % 32, 4:8, :]
    near = got[column, 4:8, :] + pick(first, 0.0, left) + pick(last, 0.0, right)
    side = 4 * (1 - level // 4)
    crossing = pick(first, left, pick(last, right, 0.0))
    goal = side + (level + jnp.where(first, 1, jnp.where(last, 3, 0))) % 4
    send[...] = jnp.broadcast_to(jnp.where(iota(0, (8, W)) == 0, dots, 0.0)[None], (8, 8, W))
    send[level ^ 4, 4:8, :] = near

    @pl.when(jnp.logical_or(first, last))
    def _():
        send[goal, 4:8, :] = crossing


def final_kernel(theta_v, field, ui, ue, ki, ke, push_cols, k_cols, got, inc, res, inc_s, res_s, sems):
    theta = theta_v[0:1, :]
    block = jnp.sum(got[...], axis=0)
    row = block[0:1, :]
    lane1 = iota(1, (1, W))

    def total(k):
        value = jnp.sum(jnp.where(lane1 == k, row, 0.0), axis=1, keepdims=True)
        return jnp.broadcast_to(value, (1, W))

    norm0, curve0, zz, zaz = total(0), total(1), total(2), total(3)
    step0 = norm0 / curve0
    lead = 1.0 - step0 * theta
    norm1 = step0 * step0 * zz - lead * lead * norm0
    rz = curve0 - theta * norm0
    zw = zz + theta * rz
    a = lead + norm1 / norm0
    curve1 = a * a * curve0 - 2.0 * a * step0 * zw + step0 * step0 * zaz
    step1 = norm1 / curve1
    both = step0 + step1 * a
    cross = step1 * step0
    keep = 1.0 - theta * both
    columns = jnp.concatenate([block, jnp.zeros((W - 8, W), F32)], axis=0).T
    lane = iota(1)
    copies = []
    for x in range(PLANES):
        for c in range(3):
            r = field[c, x]
            v = ue[c, x // 3] if x in (0, 3) else ui[c, x - 1]
            k = ke[c, x // 3] if x in (0, 3) else ki[c, x - 1]
            low = k_cols[:, c * 4 + x : c * 4 + x + 1]
            if c == 2:
                v = v + jnp.where(
                    lane == 0,
                    k_cols[:, 48 + x : 49 + x],
                    jnp.where(lane == W - 1, push_cols[:, x : x + 1], 0.0),
                )
                low = low + columns[:, 4 + x : 5 + x]
            added = jnp.where(lane == 0, low, 0.0)
            for i, place in ((1, 1), (2, W - 2), (3, W - 1)):
                j = i * 12 + c * 4 + x
                added = jnp.where(lane == place, k_cols[:, j : j + 1], added)
            k = k + added
            inc_s[c, x] = both * r - cross * v
            res_s[c, x] = keep * r - both * v + cross * k
            for i, (source, target) in enumerate(((inc_s, inc), (res_s, res))):
                copy = pltpu.make_async_copy(source.at[c, x], target.at[c, x], sems.at[i, c, x])
                copy.start()
                copies.append(copy)
    for copy in copies:
        copy.wait()


def pairs(f):
    return [(i, f(i) % 256) for i in range(256)]


MATE = pairs(lambda i: i ^ 1)
FAR = pairs(lambda i: i + 1 if i % 2 else i - 1)
CROSS = pairs(lambda i: i ^ 128)
PLANE_GROUPS = [[32 * a + b for b in range(32)] for a in range(8)]
COLUMN_GROUPS = [[32 * a + b for a in range(8)] for b in range(32)]


def swap(x, table):
    return lax.ppermute(x, "slab", table)


def exchange(x, groups):
    return lax.all_to_all(x, "slab", 0, 0, tiled=True, axis_index_groups=groups)


def local(rhs, stiff, stencil, dual, mortar, partner, active):
    dev = lax.axis_index("slab").astype(jnp.int32).reshape(1)
    half = (3, 2, W, W)
    shape = rhs.shape
    stage = 8000000
    flat = f32(16, W)

    def whole(n):
        return [vmem()] * n

    def dma(*dims):
        return pltpu.SemaphoreType.DMA(dims)

    st = stencil.reshape(-1)
    meta = jnp.concatenate([(partner % 4).reshape(-1), active, dev, jnp.zeros((15,), jnp.int32)])
    a_mate, a_far = call(
        pack_kernel, "pack", [smem(), vmem()], (f32(HALO + 8, W), f32(HALO + 8, W))
    )(dev, rhs)
    g_far = swap(a_far, FAR)
    g_mate = swap(a_mate, MATE)
    ui, dots_ui, stiff_v, mortar_v, weights, theta = call(
        inner_first_kernel,
        "inner_first",
        [smem(), vmem(), vmem(), anywhere(), anywhere()],
        (
            f32(*half),
            flat,
            f32(PLANES, W, W),
            jax.ShapeDtypeStruct(mortar.shape, mortar.dtype),
            f32(W, W),
            f32(8, W),
        ),
        [pltpu.VMEM((3, 12, W, W), F32), dma(2)],
        stage,
    )(st, rhs, dual, stiff, mortar)
    own_faces = jnp.concatenate([a_mate[HALO : HALO + 4], g_mate[HALO : HALO + 4], g_far[HALO : HALO + 4]])
    own_faces, ui, meta = lax.optimization_barrier((own_faces, ui, meta))
    faces = swap(own_faces, CROSS)
    ue, dots_ue, b_mate, b_far = call(
        edge_first_kernel,
        "edge_first",
        [smem(), smem()] + whole(5),
        (f32(*half), flat, f32(HALO + 8, W), f32(HALO + 8, W)),
        [pltpu.VMEM((3, 18, W, W), F32)],
        stage,
    )(dev, st, rhs, g_mate, g_far, stiff_v, ui)
    items, push_cols, dots_c = call(
        contact0_kernel,
        "contact0",
        [smem()] + whole(5),
        (f32(16, W), f32(W, W), f32(8, W)),
        [pltpu.VMEM((16, W), F32)],
    )(meta, faces, g_far, rhs, weights, mortar_v)
    u_rows = b_mate[HALO : HALO + 8]
    h_mate = swap(jnp.concatenate([b_mate, items]), MATE)
    mate_back = h_mate[HALO + 8 : HALO + 20]
    h_far = swap(jnp.concatenate([b_far, items, mate_back]), FAR)
    ki, dots_ki, stiff_rows, coefs = call(
        inner_second_kernel,
        "inner_second",
        [smem()] + whole(3),
        (f32(*half), flat, f32(8, W), f32(88, W)),
        [pltpu.VMEM((3, 12, W, W), F32)],
        stage,
    )(st, ui, ue, stiff_v)
    h_far, ki = lax.optimization_barrier((h_far, ki))
    h_next = swap(h_far[HALO + 8 : HALO + 20], MATE)
    pack = call(gather_kernel, "gather", whole(5), f32(72, W))(u_rows, h_mate, h_far, h_next, items)
    cross = swap(pack, CROSS)
    ke, dots_ke, k_rows = call(
        edge_second_kernel,
        "edge_second",
        [smem(), smem()] + whole(6),
        (f32(*half), flat, f32(8, W)),
        [pltpu.VMEM((3, 18, W, W), F32)],
        stage,
    )(dev, st, ui, ue, h_mate, h_far, stiff_v, ki)
    send, k_cols = call(
        join_kernel,
        "join",
        [smem()] + whole(19),
        (f32(32, 8, W), f32(W, W)),
        [pltpu.VMEM((16, W), F32), pltpu.VMEM((16, W), F32)],
    )(
        meta, coefs, ui, ue, h_mate, h_far, pack, cross, items, push_cols, stiff_rows,
        u_rows, k_rows, weights, mortar_v, dots_ui, dots_ue, dots_c, dots_ki, dots_ke,
    )
    got = exchange(send, PLANE_GROUPS)
    relayed = call(relay_kernel, "relay", [smem(), vmem()], f32(8, 8, W))(dev, got)
    sums = exchange(relayed, COLUMN_GROUPS)
    return call(
        final_kernel,
        "final",
        whole(9),
        (f32(*shape), f32(*shape)),
        [pltpu.VMEM(shape, F32), pltpu.VMEM(shape, F32), dma(2, 3, 4)],
        out_specs=(anywhere(), anywhere()),
    )(theta, rhs, ui, ue, ki, ke, push_cols, k_cols, sums)


def solution(mesh):
    placed = (
        P(None, "slab", None, None),
        P("slab", None, None),
        P(),
        P("slab", None),
        P("slab", None, None, None),
        P("slab", None),
        P("slab"),
    )
    return jax.shard_map(
        local,
        mesh=mesh,
        in_specs=placed,
        out_specs=(P(None, "slab", None, None), P(None, "slab", None, None)),
        check_vma=False,
    )
```

time: 1320 us -> 76 us (0.06)
  waiting for transfers between devices: 497 us -> 5.93 us
  other arithmetic: 374 us -> 0.14 us
  blocking collectives: 377 us -> 21.8 us
  local copies, waits for them, and re-layouts: 39.3 us -> 4.62 us
  Pallas kernels: 0 us -> 20.6 us
  between operations: 18.7 us -> 0.75 us
  starting transfers between devices: 4.7 us -> 21.8 us
    unnamed x4 -> x0, waiting for transfers between devices: 496 us -> none
    add x9 -> x0, other arithmetic: 356 us -> none  [the longest x6 355 us: stencil_part(): outputs[out_comp]]
    psum x3 -> x0, blocking collectives: 229 us -> none  [the longest x2 151 us: residual_squares(): return lax.psum(jnp.sum(residual * residual), 'slab')]
    all_gather x2 -> x0, blocking collectives: 148 us -> none  [contact_gather(): all_faces = lax.all_gather(master, 'slab', axis=0, tiled=True)]
    slice x20 -> x6, local copies, waits for them, and re-layouts: 31 us -> 0.01 us  [the longest x1 0.01 us: local(): a_mate[HALO:HALO + 4]]
    all_to_all x0 -> x2, blocking collectives: none -> 21.8 us  [exchange(): return lax.all_to_all(x, 'slab', 0, 0, tiled=True, axis_index_groups=groups)]
    pallas_call x0 -> x10, Pallas kernels: none -> 20.6 us  [the longest x1 3.85 us: local(): call(inner_first_kernel, 'inner_first', [smem(), vmem(), vmem(), anywhere...]
    ppermute x4 -> x7, starting transfers between devices: 4.62 us -> 21.8 us  [swap(): return lax.ppermute(x, 'slab', table)]
  transfers between devices with their start and end apart: 6 -> 7, of which waited for: 2 -> 5; matrix products, arithmetic and copies ran while one was open for 3% -> 1% of each run, Pallas kernels for 0% -> 20%
where the time goes in v2:
time: 76 us; the launch traced here: 75.7 us
  starting transfers between devices  21.8 us (29%)
  blocking collectives  21.8 us (29%)
  Pallas kernels  20.6 us (27%)
  waiting for transfers between devices  5.93 us (8%)
  local copies, waits for them, and re-layouts  4.62 us (6%)
    ppermute x7, starting transfers between devices, swap(): return lax.ppermute(x, 'slab', table)  21.8 us
    all_to_all x2, blocking collectives, exchange(): return lax.all_to_all(x, 'slab', 0, 0, tiled=True, axis_index_groups=groups)  21.8 us
    ppermute x7, waiting for transfers between devices, swap(): return lax.ppermute(x, 'slab', table)  5.93 us
    unnamed x17, local copies, waits for them, and re-layouts  4.36 us
    pallas_call x1, Pallas kernels, local(): call(inner_first_kernel, 'inner_first', [smem(), vmem(), vmem(), anywhere...  3.85 us
    pallas_call x1, Pallas kernels, local(): call(edge_first_kernel, 'edge_first', [smem(), smem()] + whole(5), (f32(*...  3.85 us
    pallas_call x1, Pallas kernels, local(): call(edge_second_kernel, 'edge_second', [smem(), smem()] + whole(6), (f32...  3.82 us
    pallas_call x1, Pallas kernels, local(): call(inner_second_kernel, 'inner_second', [smem()] + whole(3), (f32(*half...  3.78 us
  transfers between devices with their start and end apart: 7, of which 5 were waited for; matrix products, arithmetic and copies ran while one was open for 1% of the time, Pallas kernels for 20%

profile of v2, /device:TPU:1, one launch (start us, length us, event | category | flops | bytes accessed | tf_op | source)
XLA Modules:
  0.0 75.7 jit_solution(17777515620636596749)
XLA Ops:
  0.6 1.1 %copy-done = f32[3,4,128,128]{3,2,1,0:T(8,128)S(1)} copy-done((f32[3,4,128,128]{3,2,1,0:T(8,128)S(1)}, f32[3,4,128,128]{3,2,1,0:T(8,128)}, u32[]{:S(2)}) %copy-start) | copy-done | bytes 786456
  1.9 2.7 %collective-permute-start.1 = (f32[392,128]{1,0:T(8,128)S(1)}, f32[392,128]{1,0:T(8,128)S(1)}, u32[]{:S(2)}, u32[]{:S(2)}) collective-permute-start(f32[392,128]{1,0:T(8,128)S(1)} %get-tuple-element.33), channel_id=1, source_target_pairs={{0,255},{1,2},{2,1},{3,4},{4,3},{5,6},{6,5},{7,8},{8,7},{9,10},{10... | collective-permute-start | bytes 602120 | tf_op jit(solution)/shard_map/ppermute | solution.py:521
  4.7 8.8 %collective-permute-start = (f32[392,128]{1,0:T(8,128)S(1)}, f32[392,128]{1,0:T(8,128)S(1)}, u32[]{:S(2)}, u32[]{:S(2)}) collective-permute-start(f32[392,128]{1,0:T(8,128)S(1)} %get-tuple-element.32), channel_id=1, source_target_pairs={{0,1},{1,0},{2,3},{3,2},{4,5},{5,4},{6,7},{7,6},{8,9},{9,8},{10,11... | collective-permute-start | bytes 602120 | tf_op jit(solution)/shard_map/ppermute | solution.py:521
  14.3 1.0 %copy-done.2 = bf16[4,3,128,128]{3,2,1,0:T(8,128)(2,1)S(1)} copy-done((bf16[4,3,128,128]{3,2,1,0:T(8,128)(2,1)S(1)}, bf16[4,3,128,128]{3,2,1,0:T(8,128)(2,1)}, u32[]{:S(2)}) %copy-start.2) | copy-done | bytes 393240
  15.3 0.9 %copy-done.3 = f32[4,128,128]{2,1,0:T(8,128)S(1)} copy-done((f32[4,128,128]{2,1,0:T(8,128)S(1)}, f32[4,128,128]{2,1,0:T(8,128)}, u32[]{:S(2)}) %copy-start.3) | copy-done | bytes 262168
  16.2 3.9 %inner_first.1 = (f32[3,2,128,128]{3,2,1,0:T(8,128)S(1)}, f32[16,128]{1,0:T(8,128)S(1)}, f32[4,128,128]{2,1,0:T(8,128)S(1)}, bf16[4,3,128,128]{3,2,1,0:T(8,128)(...) custom-call(f32[243]{0:T(256)S(1)} %reshape.13.st, f32[3,4,128,128]{3,2,1,0:T(8,128)S(1)} %copy-done.1, ...), custom_call_target="tpu_custom_call" | custom-call | flops 1000 | bytes 8000000 | tf_op jit(solution)/shard_map/inner_first/pallas_call | solution.py:548
  20.2 0.7 copy-done.7
  21.0 1.2 %collective-permute-start.2 = (f32[12,128]{1,0:T(8,128)S(1)}, f32[12,128]{1,0:T(8,128)S(1)}, u32[]{:S(2)}, u32[]{:S(2)}) collective-permute-start(f32[12,128]{1,0:T(8,128)S(1)} %pad_maximum_fusion.2), channel_id=1, source_target_pairs={{0,128},{1,129},{2,130},{3,131},{4,132},{5,133},{6,134},{7,135},{8... | collective-permute-start | bytes 18440 | tf_op jit(solution)/shard_map/ppermute | solution.py:521
  22.2 3.8 %edge_first.1 = (f32[3,2,128,128]{3,2,1,0:T(8,128)S(1)}, f32[16,128]{1,0:T(8,128)S(1)}, f32[392,128]{1,0:T(8,128)S(1)}, f32[392,128]{1,0:T(8,128)S(1)}) custom-call(s32[1]{0:T(128)} %bitcast.dev, f32[243]{0:T(256)S(1)} %reshape.13.st, f32[3,4,128,128]{3,2,1,0:T(8,128)S(1)} %copy-done.1, f32[392,128]{1,0:T(8,128)S(1)} %collective-permute-done.mate, ...), custom_call_target="tpu_custom_call" | custom-call | flops 1000 | bytes 8000000 | tf_op jit(solution)/shard_map/edge_first/pallas_call | solution.py:566
  26.1 1.4 %collective-permute-done.2.faces = f32[12,128]{1,0:T(8,128)S(1)} collective-permute-done((f32[12,128]{1,0:T(8,128)S(1)}, f32[12,128]{1,0:T(8,128)S(1)}, u32[]{:S(2)}, u32[]{:S(2)}) %collective-permute-start.2) | collective-permute-done | bytes 6176 | tf_op jit(solution)/shard_map/ppermute | solution.py:521
  27.5 1.3 %contact0.1 = (f32[16,128]{1,0:T(8,128)S(1)}, f32[128,128]{1,0:T(8,128)S(1)}, f32[8,128]{1,0:T(8,128)S(1)}) custom-call(s32[32]{0:T(128)S(1)} %pad_add_fusion.meta, f32[12,128]{1,0:T(8,128)S(1)} %collective-permute-done.2.faces, f32[392,128]{1,0:T(8,128)S(1)} %collective-permute-done.1.far, f32[3,4,128,128]{3,2,1,0:T(8,128)S(1)} %copy-done.1, ...), custom_call_target="tpu_custom_call" | custom-call | flops 1000 | bytes 1000000 | tf_op jit(solution)/shard_map/contact0/pallas_call | solution.py:574
  28.8 1.2 %collective-permute-start.3 = (f32[408,128]{1,0:T(8,128)S(1)}, f32[408,128]{1,0:T(8,128)S(1)}, u32[]{:S(2)}, u32[]{:S(2)}) collective-permute-start(f32[408,128]{1,0:T(8,128)S(1)} %pad_maximum_fusion.1), channel_id=1, source_target_pairs={{0,1},{1,0},{2,3},{3,2},{4,5},{5,4},{6,7},{7,6},{8,9},{9,8},{10,11... | collective-permute-start | bytes 626696 | tf_op jit(solution)/shard_map/ppermute | solution.py:521
  30.0 1.1 %collective-permute-done.3.mate = f32[408,128]{1,0:T(8,128)S(1)} collective-permute-done((f32[408,128]{1,0:T(8,128)S(1)}, f32[408,128]{1,0:T(8,128)S(1)}, u32[]{:S(2)}, u32[]{:S(2)}) %collective-permute-start.3) | collective-permute-done | bytes 208928 | tf_op jit(solution)/shard_map/ppermute | solution.py:521
  31.2 3.8 %inner_second.1 = (f32[3,2,128,128]{3,2,1,0:T(8,128)S(1)}, f32[16,128]{1,0:T(8,128)S(1)}, f32[8,128]{1,0:T(8,128)S(1)}, f32[88,128]{1,0:T(8,128)S(1)}) custom-call(f32[243]{0:T(256)S(1)} %reshape.13.st, f32[3,2,128,128]{3,2,1,0:T(8,128)S(1)} %get-tuple-element.35.ui, f32[3,2,128,128]{3,2,1,0:T(8,128)S(1)} %get-tuple-element.37.ue, ...), custom_call_target="tpu_custom_call" | custom-call | flops 1000 | bytes 8000000 | tf_op jit(solution)/shard_map/inner_second/pallas_call | solution.py:585
  35.0 1.5 %collective-permute-done.4.far = f32[420,128]{1,0:T(8,128)S(1)} collective-permute-done((f32[420,128]{1,0:T(8,128)S(1)}, f32[420,128]{1,0:T(8,128)S(1)}, u32[]{:S(2)}, u32[]{:S(2)}) %collective-permute-start.4) | collective-permute-done | bytes 215072 | tf_op jit(solution)/shard_map/ppermute | solution.py:521
  36.5 5.8 %collective-permute-start.5 = (f32[12,128]{1,0:T(8,128)S(1)}, f32[12,128]{1,0:T(8,128)S(1)}, u32[]{:S(2)}, u32[]{:S(2)}) collective-permute-start(f32[12,128]{1,0:T(8,128)S(1)} %slice.23), channel_id=1, source_target_pairs={{0,1},{1,0},{2,3},{3,2},{4,5},{5,4},{6,7},{7,6},{8,9},{9,8},{10,11... | collective-permute-start | bytes 18440 | tf_op jit(solution)/shard_map/ppermute | solution.py:521
  42.3 0.8 %collective-permute-done.5.following = f32[12,128]{1,0:T(8,128)S(1)} collective-permute-done((f32[12,128]{1,0:T(8,128)S(1)}, f32[12,128]{1,0:T(8,128)S(1)}, u32[]{:S(2)}, u32[]{:S(2)}) %collective-permute-start.5) | collective-permute-done | bytes 6176 | tf_op jit(solution)/shard_map/ppermute | solution.py:521
  43.1 2.0 %collective-permute-start.6 = (f32[72,128]{1,0:T(8,128)S(1)}, f32[72,128]{1,0:T(8,128)S(1)}, u32[]{:S(2)}, u32[]{:S(2)}) collective-permute-start(f32[72,128]{1,0:T(8,128)S(1)} %gather.1.pack), channel_id=1, source_target_pairs={{0,128},{1,129},{2,130},{3,131},{4,132},{5,133},{6,134},{7,135},{8... | collective-permute-start | bytes 110600 | tf_op jit(solution)/shard_map/ppermute | solution.py:521
  45.1 3.8 %edge_second.1 = (f32[3,2,128,128]{3,2,1,0:T(8,128)S(1)}, f32[16,128]{1,0:T(8,128)S(1)}, f32[8,128]{1,0:T(8,128)S(1)}) custom-call(s32[1]{0:T(128)} %bitcast.dev, f32[243]{0:T(256)S(1)} %reshape.13.st, f32[3,2,128,128]{3,2,1,0:T(8,128)S(1)} %get-tuple-element.35.ui, f32[3,2,128,128]{3,2,1,0:T(8,128)S(1)} %get-tuple-element.37.ue, ...), custom_call_target="tpu_custom_call" | custom-call | flops 1000 | bytes 8000000 | tf_op jit(solution)/shard_map/edge_second/pallas_call | solution.py:597
  48.9 1.1 %collective-permute-done.6.cross = f32[72,128]{1,0:T(8,128)S(1)} collective-permute-done((f32[72,128]{1,0:T(8,128)S(1)}, f32[72,128]{1,0:T(8,128)S(1)}, u32[]{:S(2)}, u32[]{:S(2)}) %collective-permute-start.6) | collective-permute-done | bytes 36896 | tf_op jit(solution)/shard_map/ppermute | solution.py:521
  50.0 1.7 %join.1 = (f32[32,8,128]{2,1,0:T(8,128)S(1)}, f32[128,128]{1,0:T(8,128)S(1)}) custom-call(s32[32]{0:T(128)S(1)} %pad_add_fusion.meta, f32[88,128]{1,0:T(8,128)S(1)} %get-tuple-element.50.coefs, f32[3,2,128,128]{3,2,1,0:T(8,128)S(1)} %get-tuple-element.35.ui, f32[3,2,128,128]{3,2,1,0:T(8,128)S(1)} %get-tuple-element.37.ue, ...), custom_call_target="tpu_custom_call" | custom-call | flops 1000 | bytes 1000000 | tf_op jit(solution)/shard_map/join/pallas_call | solution.py:605
  51.7 11.9 %all_to_all.10.got = f32[32,8,128]{2,1,0:T(8,128)S(1)} all-to-all(f32[32,8,128]{2,1,0:T(8,128)S(1)} %get-tuple-element.59), channel_id=1, replica_groups={{0,1,2,3,4,5,6,7,8,9,10,11,12,13,14,15,16,17,18,19,20,21,22,23,24,25,26..., dimensions={0} | all-to-all | bytes 262144 | tf_op jit(solution)/shard_map/all_to_all | solution.py:525
  63.6 9.9 %all_to_all.11.got = f32[8,8,128]{2,1,0:T(8,128)S(1)} all-to-all(f32[8,8,128]{2,1,0:T(8,128)S(1)} %relay.1), channel_id=1, replica_groups={{0,32,64,96,128,160,192,224},{1,33,65,97,129,161,193,225},{2,34,66,98,1..., dimensions={0} | all-to-all | bytes 65536 | tf_op jit(solution)/shard_map/all_to_all | solution.py:525
  73.6 2.1 %final.1 = (f32[3,4,128,128]{3,2,1,0:T(8,128)}, f32[3,4,128,128]{3,2,1,0:T(8,128)}) custom-call(f32[8,128]{1,0:T(8,128)S(1)} %get-tuple-element.31.theta_v, f32[3,4,128,128]{3,2,1,0:T(8,128)S(1)} %copy-done.1, f32[3,2,128,128]{3,2,1,0:T(8,128)S(1)} %get-tuple-element.35.ui, f32[3,2,128,128]{3,2,1,0:T(8,128)S(1)} %get-tuple-element.37.ue, ...), custom_call_target="tpu_custom_call" | custom-call | flops 1000 | bytes 1000000 | tf_op jit(solution)/shard_map/final/pallas_call | solution.py:618
  (33 shorter events, 1.4 us)
Async XLA Ops:
  0.6 1.1 %copy-start = (f32[3,4,128,128]{3,2,1,0:T(8,128)S(1)}, f32[3,4,128,128]{3,2,1,0:T(8,128)}, u32[]{:S(2)}) copy-start(f32[3,4,128,128]{3,2,1,0:T(8,128)} %field.9) | copy-start | bytes 2359300
  1.8 11.7 %copy-start.6 = (s32[4,3]{1,0:T(4,128)S(1)}, s32[4,3]{1,0:T(4,128)}, u32[]{:S(2)}) copy-start(s32[4,3]{1,0:T(4,128)} %param.12) | copy-start | bytes 148
  1.8 12.0 %copy-start.1 = (f32[3,4,128,128]{3,2,1,0:T(8,128)S(1)}, f32[3,4,128,128]{3,2,1,0:T(8,128)}, u32[]{:S(2)}) copy-start(f32[3,4,128,128]{3,2,1,0:T(8,128)} %field.9) | copy-start | bytes 2359300
  1.9 11.5 %copy-start.5 = (f32[27,3,3]{0,2,1:T(4,128)S(1)}, f32[27,3,3]{0,2,1:T(4,128)}, u32[]{:S(2)}) copy-start(f32[27,3,3]{0,2,1:T(4,128)} %param.9) | copy-start | bytes 2920
  1.9 19.0 %collective-permute-start.1 = (f32[392,128]{1,0:T(8,128)S(1)}, f32[392,128]{1,0:T(8,128)S(1)}, u32[]{:S(2)}, u32[]{:S(2)}) collective-permute-start(f32[392,128]{1,0:T(8,128)S(1)} %get-tuple-element.33), channel_id=1, source_target_pairs={{0,255},{1,2},{2,1},{3,4},{4,3},{5,6},{6,5},{7,8},{8,7},{9,10},{10... | collective-permute-start | bytes 602120 | tf_op jit(solution)/shard_map/ppermute | solution.py:521
  4.7 16.2 %collective-permute-start = (f32[392,128]{1,0:T(8,128)S(1)}, f32[392,128]{1,0:T(8,128)S(1)}, u32[]{:S(2)}, u32[]{:S(2)}) collective-permute-start(f32[392,128]{1,0:T(8,128)S(1)} %get-tuple-element.32), channel_id=1, source_target_pairs={{0,1},{1,0},{2,3},{3,2},{4,5},{5,4},{6,7},{7,6},{8,9},{9,8},{10,11... | collective-permute-start | bytes 602120 | tf_op jit(solution)/shard_map/ppermute | solution.py:521
  13.6 0.7 copy-start.4
  14.3 1.0 %copy-start.2 = (bf16[4,3,128,128]{3,2,1,0:T(8,128)(2,1)S(1)}, bf16[4,3,128,128]{3,2,1,0:T(8,128)(2,1)}, u32[]{:S(2)}) copy-start(bf16[4,3,128,128]{3,2,1,0:T(8,128)(2,1)} %mortar.1) | copy-start | bytes 1179652
  15.3 0.9 %copy-start.3 = (f32[4,128,128]{2,1,0:T(8,128)S(1)}, f32[4,128,128]{2,1,0:T(8,128)}, u32[]{:S(2)}) copy-start(f32[4,128,128]{2,1,0:T(8,128)} %stiff.1) | copy-start | bytes 786436
  20.2 0.7 copy-start.7
  21.0 6.5 %collective-permute-start.2 = (f32[12,128]{1,0:T(8,128)S(1)}, f32[12,128]{1,0:T(8,128)S(1)}, u32[]{:S(2)}, u32[]{:S(2)}) collective-permute-start(f32[12,128]{1,0:T(8,128)S(1)} %pad_maximum_fusion.2), channel_id=1, source_target_pairs={{0,128},{1,129},{2,130},{3,131},{4,132},{5,133},{6,134},{7,135},{8... | collective-permute-start | bytes 18440 | tf_op jit(solution)/shard_map/ppermute | solution.py:521
  28.8 2.3 %collective-permute-start.3 = (f32[408,128]{1,0:T(8,128)S(1)}, f32[408,128]{1,0:T(8,128)S(1)}, u32[]{:S(2)}, u32[]{:S(2)}) collective-permute-start(f32[408,128]{1,0:T(8,128)S(1)} %pad_maximum_fusion.1), channel_id=1, source_target_pairs={{0,1},{1,0},{2,3},{3,2},{4,5},{5,4},{6,7},{7,6},{8,9},{9,8},{10,11... | collective-permute-start | bytes 626696 | tf_op jit(solution)/shard_map/ppermute | solution.py:521
  31.1 5.4 %collective-permute-start.4 = (f32[420,128]{1,0:T(8,128)S(1)}, f32[420,128]{1,0:T(8,128)S(1)}, u32[]{:S(2)}, u32[]{:S(2)}) collective-permute-start(f32[420,128]{1,0:T(8,128)S(1)} %pad_maximum_fusion), channel_id=1, source_target_pairs={{0,255},{1,2},{2,1},{3,4},{4,3},{5,6},{6,5},{7,8},{8,7},{9,10},{10... | collective-permute-start | bytes 645128 | tf_op jit(solution)/shard_map/ppermute | solution.py:521
  36.5 6.6 %collective-permute-start.5 = (f32[12,128]{1,0:T(8,128)S(1)}, f32[12,128]{1,0:T(8,128)S(1)}, u32[]{:S(2)}, u32[]{:S(2)}) collective-permute-start(f32[12,128]{1,0:T(8,128)S(1)} %slice.23), channel_id=1, source_target_pairs={{0,1},{1,0},{2,3},{3,2},{4,5},{5,4},{6,7},{7,6},{8,9},{9,8},{10,11... | collective-permute-start | bytes 18440 | tf_op jit(solution)/shard_map/ppermute | solution.py:521
  43.1 6.9 %collective-permute-start.6 = (f32[72,128]{1,0:T(8,128)S(1)}, f32[72,128]{1,0:T(8,128)S(1)}, u32[]{:S(2)}, u32[]{:S(2)}) collective-permute-start(f32[72,128]{1,0:T(8,128)S(1)} %gather.1.pack), channel_id=1, source_target_pairs={{0,128},{1,129},{2,130},{3,131},{4,132},{5,133},{6,134},{7,135},{8... | collective-permute-start | bytes 110600 | tf_op jit(solution)/shard_map/ppermute | solution.py:521

commit v3 on v2

--- a/solution.py
+++ b/solution.py
@@ -55,12 +55,15 @@
     return trace * F32(1.0 / 3.0) + F32(2.125)
 
 
-def columns_to_rows(columns):
+def face_rows(planes):
     lane = iota(1)
     block = jnp.zeros((W, W), F32)
-    for k, column in enumerate(columns):
-        block = jnp.where(lane == k, column, block)
-    return block.T
+    for k, plane in enumerate(planes):
+        moved = pltpu.roll(plane, 2 * k + 1, 1)
+        block = jnp.where(lane // 2 == k, moved, block)
+    rows = block.T[0:8, :]
+    order = [1, 3, 5, 7, 0, 2, 4, 6]
+    return jnp.concatenate([rows[i : i + 1] for i in order], axis=0)
 
 
 def pick(flag, yes, no):
@@ -85,15 +88,17 @@
     return jnp.logical_or(place == 0, place == 127)
 
 
-def pack_kernel(dev, field, mate, far):
+def load_kernel(dev, rhs, field, mate, far, faces):
     odd, _ = place_of(dev)
     for c in range(3):
-        low, high = field[c, 0], field[c, PLANES - 1]
+        low, high = rhs[c, 0], rhs[c, PLANES - 1]
         mate[c * W : (c + 1) * W, :] = pick(odd, low, high)
         far[c * W : (c + 1) * W, :] = pick(odd, high, low)
-    rows = columns_to_rows([field[2, t, :, 0:1] for t in range(PLANES)])[0:8, :]
+    rows = face_rows([rhs[2, t] for t in range(PLANES)])
+    faces[...] = rows
     mate[HALO : HALO + 8, :] = rows
     far[HALO : HALO + 8, :] = rows
+    field[...] = rhs[...]
 
 
 BLOCK = 32
@@ -177,19 +182,28 @@
     return 3 * x
 
 
-def inner_first_kernel(st, field, dual, stiff, mortar, ui, dots, stiff_v, mortar_v, weights, theta, s, sems):
+def inner_first_kernel(
+    dev, st, partner, active, field, dual, stiff, mortar,
+    ui, dots, theta, stiff_v, mortar_v, dual_v, meta, s, sems,
+):
     stiff_copy = pltpu.make_async_copy(stiff, stiff_v, sems.at[0])
     mortar_copy = pltpu.make_async_copy(mortar, mortar_v, sems.at[1])
     stiff_copy.start()
     mortar_copy.start()
+    dual_v[...] = dual[...]
+    for t in range(PLANES):
+        for slot in range(3):
+            meta[3 * t + slot] = partner[t, slot] % 4
+        meta[12 + t] = active[t]
+    meta[16] = dev[0]
+    for i in range(17, 32):
+        meta[i] = 0
     for c in range(3):
         for x in range(PLANES):
             s[1, c * 4 + x] = field[c, x]
     fill_shifted(s, 4)
-    block = jnp.concatenate([dual[...], jnp.zeros((W - PLANES, W), F32)], axis=0)
-    weights[...] = block.T
+    theta[...] = jnp.full((8, W), shift_of(st), F32)
     stiff_copy.wait()
-    theta[...] = jnp.full((8, W), shift_of(st), F32)
     store_dots(dots, sweep(s, st, 4, inner, emitter(ui, stiff_v, inner, shift_of(st))))
     mortar_copy.wait()
 
@@ -209,11 +223,6 @@
     fill_shifted(s, 6)
 
 
-def face_rows(edge, mid):
-    planes = (edge.at[2, 0], mid.at[2, 0], mid.at[2, 1], edge.at[2, 1])
-    return columns_to_rows([p[:, 0:1] for p in planes] + [p[:, W - 1 : W] for p in planes])[0:8, :]
-
-
 def centre6(x):
     return 3 * x + 1
 
@@ -226,7 +235,7 @@
         low, high = ue[c, 0], ue[c, 1]
         to_mate[c * W : (c + 1) * W, :] = pick(odd, low, high)
         to_far[c * W : (c + 1) * W, :] = pick(odd, high, low)
-    rows = face_rows(ue, ui)
+    rows = face_rows([ue[2, 0], ui[2, 0], ui[2, 1], ue[2, 1]])
     to_mate[HALO : HALO + 8, :] = rows
     to_far[HALO : HALO + 8, :] = rows
 
@@ -239,8 +248,7 @@
         s[1, c * 4 + 3] = ue[c, 1]
     fill_shifted(s, 4)
     store_dots(dots, sweep(s, st, 4, inner, emitter(ki, stiff, inner, None)))
-    faces = [stiff[t, :, 0:1] for t in range(PLANES)] + [stiff[t, :, W - 1 : W] for t in range(PLANES)]
-    stiff_rows[...] = columns_to_rows(faces)[0:8, :]
+    stiff_rows[...] = face_rows([stiff[t] for t in range(PLANES)])
     for i, (k, c) in enumerate(FACE_TERMS):
         coefs[i : i + 1, :] = jnp.full((1, W), coefficient(st, k, c, 2), F32)
 
@@ -248,59 +256,69 @@
 def edge_second_kernel(dev, st, ui, ue, mate, far, stiff, ki, ke, dots, rows, s):
     fill_halo(dev, s, mate, far, lambda c, i: ue[c, i], lambda c, i: ui[c, i])
     store_dots(dots, sweep(s, st, 6, centre6, emitter(ke, stiff, outer, None)))
-    rows[...] = face_rows(ke, ki)
-
-
-def contact(meta, slave, table, weights, mortar, back):
-    energy = jnp.zeros((W, 1), F32)
-    columns, pushes, slots = [], [], []
+    rows[...] = face_rows([ke[2, 0], ki[2, 0], ki[2, 1], ke[2, 1]])
+
+
+def thirds(v):
+    a = v.astype(jnp.bfloat16)
+    rest = v - a.astype(F32)
+    b = rest.astype(jnp.bfloat16)
+    c = (rest - b.astype(F32)).astype(jnp.bfloat16)
+    return jnp.concatenate([a, b, c], axis=0)
+
+
+def contact(meta, slave, table, dual, mortar, back, picked):
+    for t in range(PLANES):
+        for s in range(3):
+            picked[3 * t + s : 3 * t + s + 1, :] = table[pl.ds(4 * s + meta[3 * t + s], 1), :]
+    picked[12:16, :] = jnp.zeros((4, W), F32)
+    parts = thirds(picked[...])
+    pulled = []
     for t in range(PLANES):
         total = None
         for s in range(3):
-            row = table[pl.ds(4 * s + meta[3 * t + s], 1), :]
-            term = mortar[t, s].astype(F32) * row
-            total = term if total is None else total + term
-        pulled = jnp.sum(total, axis=1, keepdims=True)
-        weight = weights[:, t : t + 1]
-        gap = weight * slave(t) - pulled
-        push = (F32(4.0) * meta[12 + t].astype(F32)) * gap
-        energy += push * gap
-        columns.append(weight * push)
-        pushes.append(push)
+            got = lax.dot_general(
+                parts, mortar[t, s], (((1,), (1,)), ((), ())), preferred_element_type=F32
+            )
+            r = 3 * t + s
+            row = got[r : r + 1] + (got[16 + r : 17 + r] + got[32 + r : 33 + r])
+            total = row if total is None else total + row
+        pulled.append(total)
+    gap = dual * slave - jnp.concatenate(pulled, axis=0)
+    which = iota(0, (PLANES, W))
+    scale = jnp.zeros((PLANES, W), F32)
+    for t in range(PLANES):
+        scale = jnp.where(which == t, F32(4.0) * meta[12 + t].astype(F32), scale)
+    push = scale * gap
+    parts = thirds(jnp.concatenate([push, jnp.zeros((16 - PLANES, W), F32)], axis=0))
     for s in range(3):
-        rows = [
-            jnp.sum(mortar[t, s].astype(F32) * pushes[t], axis=0, keepdims=True) for t in range(PLANES)
-        ]
+        rows = []
+        for t in range(PLANES):
+            got = jnp.dot(parts, mortar[t, s], preferred_element_type=F32)
+            rows.append(got[t : t + 1] + (got[16 + t : 17 + t] + got[32 + t : 33 + t]))
         for k in range(4):
             total = None
             for t in range(PLANES):
                 term = jnp.where(meta[3 * t + s] == k, rows[t], 0.0)
                 total = term if total is None else total + term
             back[4 * s + k : 4 * s + k + 1, :] = -total
-    return energy, columns
-
-
-def fold_column(column):
-    return jnp.where(iota(1, (8, W)) == 0, jnp.sum(column.reshape(W // 8, 8, 1), axis=0), 0.0)
-
-
-def contact0_kernel(meta, faces, far, field, weights, mortar, items, push_cols, dots, table):
+    return push * gap, dual * push
+
+
+def pad8(rows):
+    return jnp.concatenate([rows, jnp.zeros((8 - PLANES, W), F32)], axis=0)
+
+
+def contact0_kernel(meta, faces, far, r_rows, dual, mortar, items, dots, table, picked):
     odd, place = place_of(meta, 16)
     own, mate = faces[0:4, :], faces[4:8, :]
     other = pick(is_wrap(place), far[HALO : HALO + 4, :], faces[8:12, :])
     table[0:4, :] = pick(odd, mate, other)
     table[4:8, :] = own
     table[8:12, :] = pick(odd, other, mate)
-    energy, columns = contact(
-        meta, lambda t: field[2, t, :, W - 1 : W], table, weights, mortar, items
-    )
-    lane = iota(1)
-    block = jnp.zeros((W, W), F32)
-    for k, column in enumerate(columns):
-        block = jnp.where(lane == k, column, block)
-    push_cols[...] = block
-    items[12:16, :] = block.T[0:4, :]
-    dots[...] = fold_column(energy)
+    energy, pushed = contact(meta, r_rows[4:8, :], table, dual[...], mortar, items, picked)
+    items[12:16, :] = pushed
+    dots[...] = pad8(energy)
 
 
 def lists(pack, other, odd, swap_far, swap_next):
@@ -325,9 +343,9 @@
 
 
 def join_kernel(
-    meta, coefs, ui, ue, mate, far, pack, cross, items, push_cols, stiff_rows, u_rows, k_rows,
-    weights, mortar, dots_ui, dots_ue, dots_c, dots_ki, dots_ke,
-    send, k_cols, table, back,
+    meta, coefs, mate, far, pack, cross, items, stiff_rows, u_rows, k_rows,
+    dual, mortar, dots_ui, dots_ue, dots_c, dots_ki, dots_ke,
+    send, rows, table, back, picked,
 ):
     odd, place = place_of(meta, 16)
     cut, swap_far = is_cut(place), is_wrap(place)
@@ -340,11 +358,7 @@
     table[4:8, :] = cross[0:4, :] + slave[1]
     table[8:12, :] = pick(odd, other, cross[4:8, :]) + slave[2]
 
-    def slave_column(t):
-        plane = ue.at[2, t // 3] if t in (0, 3) else ui.at[2, t - 1]
-        return plane[:, W - 1 : W] + push_cols[:, t : t + 1]
-
-    energy, columns = contact(meta, slave_column, table, weights, mortar, back)
+    energy, pushed = contact(meta, u_rows[4:8, :] + items[12:16, :], table, dual[...], mortar, back, picked)
 
     low = jnp.logical_and(cut, even)
     high = jnp.logical_and(cut, odd)
@@ -385,23 +399,25 @@
             lines[k, c] = total
     lines[0, 2] = lines[0, 2] + stiff_rows[0:4, :] * own_total
     lines[3, 2] = lines[3, 2] + stiff_rows[4:8, :] * own_push
-    block = jnp.concatenate(
-        [lines[k, c] for k in range(4) for c in range(3)] + [own_total, jnp.zeros((W - 52, W), F32)], axis=0
-    )
-    cols = block.T
-    wide = iota(1)
-    for t in range(PLANES):
-        cols = jnp.where(wide == 44 + t, cols + columns[t], cols)
-    k_cols[...] = cols
-
+    bend = lines[3, 2]
+    lines[3, 2] = bend + pushed
+    for c in range(3):
+        for x in range(PLANES):
+            for i, k in enumerate((2, 3, 0, 1)):
+                j = 4 * (4 * c + x) + i
+                rows[j : j + 1, :] = lines[k, c][x : x + 1]
+    rows[48:64, :] = jnp.zeros((16, W), F32)
+    for x in range(PLANES):
+        rows[4 * x + 49 : 4 * x + 50, :] = own_push[x : x + 1]
+        rows[4 * x + 50 : 4 * x + 51, :] = own_total[x : x + 1]
     face = own_total * u_rows[0:4, :] + own_push * u_rows[4:8, :]
     square = own_total * own_total + own_push * own_push
-    image = own_total * (2.0 * k_rows[0:4, :] + lines[0, 2]) + own_push * (2.0 * k_rows[4:8, :] + lines[3, 2])
+    image = own_total * (2.0 * k_rows[0:4, :] + lines[0, 2]) + own_push * (2.0 * k_rows[4:8, :] + bend)
     values = (
         dots_ui[0:8, :] + dots_ue[0:8, :],
         dots_ui[8:16, :] + dots_ue[8:16, :] + dots_c[...],
         dots_ki[0:8, :] + dots_ke[0:8, :],
-        dots_ki[8:16, :] + dots_ke[8:16, :] + fold_column(energy),
+        dots_ki[8:16, :] + dots_ke[8:16, :] + pad8(energy),
     )
     extra = (None, None, 2.0 * face + square, image)
     wide8 = iota(1, (8, W))
@@ -453,7 +469,7 @@
         send[goal, 4:8, :] = crossing
 
 
-def final_kernel(theta_v, field, ui, ue, ki, ke, push_cols, k_cols, got, inc, res, inc_s, res_s, sems):
+def final_kernel(theta_v, field, ui, ue, ki, ke, rows, got, inc, res, inc_s, res_s, work, sems):
     theta = theta_v[0:1, :]
     block = jnp.sum(got[...], axis=0)
     row = block[0:1, :]
@@ -475,29 +491,34 @@
     both = step0 + step1 * a
     cross = step1 * step0
     keep = 1.0 - theta * both
-    columns = jnp.concatenate([block, jnp.zeros((W - 8, W), F32)], axis=0).T
+    work[0:48, :] = cross * rows[0:48, :]
+    for x in range(PLANES):
+        j = 4 * (8 + x)
+        work[j + 1 : j + 2, :] = work[j + 1 : j + 2, :] - both * rows[49 + 4 * x : 50 + 4 * x, :]
+        work[j + 2 : j + 3, :] = (
+            work[j + 2 : j + 3, :]
+            - both * rows[50 + 4 * x : 51 + 4 * x, :]
+            + cross * block[4 + x : 5 + x]
+        )
+    work[48:64, :] = -cross * rows[48:64, :]
+    work[64:W, :] = jnp.zeros((W - 64, W), F32)
+    columns = work[...].T
     lane = iota(1)
+    rim = jnp.logical_or(lane < 2, lane >= W - 2)
+
+    def on_rim(q):
+        return jnp.where(rim, pltpu.roll(columns, (W - 4 * q - 2) % W, 1), 0.0)
+
     copies = []
     for x in range(PLANES):
         for c in range(3):
             r = field[c, x]
             v = ue[c, x // 3] if x in (0, 3) else ui[c, x - 1]
             k = ke[c, x // 3] if x in (0, 3) else ki[c, x - 1]
-            low = k_cols[:, c * 4 + x : c * 4 + x + 1]
-            if c == 2:
-                v = v + jnp.where(
-                    lane == 0,
-                    k_cols[:, 48 + x : 49 + x],
-                    jnp.where(lane == W - 1, push_cols[:, x : x + 1], 0.0),
-                )
-                low = low + columns[:, 4 + x : 5 + x]
-            added = jnp.where(lane == 0, low, 0.0)
-            for i, place in ((1, 1), (2, W - 2), (3, W - 1)):
-                j = i * 12 + c * 4 + x
-                added = jnp.where(lane == place, k_cols[:, j : j + 1], added)
-            k = k + added
-            inc_s[c, x] = both * r - cross * v
-            res_s[c, x] = keep * r - both * v + cross * k
+            grown = both * r - cross * v
+            left = keep * r - both * v + cross * k + on_rim(4 * c + x)
+            inc_s[c, x] = grown + on_rim(12 + x) if c == 2 else grown
+            res_s[c, x] = left
             for i, (source, target) in enumerate(((inc_s, inc), (res_s, res))):
                 copy = pltpu.make_async_copy(source.at[c, x], target.at[c, x], sems.at[i, c, x])
                 copy.start()
@@ -539,29 +560,33 @@
         return pltpu.SemaphoreType.DMA(dims)
 
     st = stencil.reshape(-1)
-    meta = jnp.concatenate([(partner % 4).reshape(-1), active, dev, jnp.zeros((15,), jnp.int32)])
-    a_mate, a_far = call(
-        pack_kernel, "pack", [smem(), vmem()], (f32(HALO + 8, W), f32(HALO + 8, W))
+    field, a_mate, a_far, r_rows = call(
+        load_kernel,
+        "load",
+        [smem(), vmem()],
+        (f32(*shape), f32(HALO + 8, W), f32(HALO + 8, W), f32(8, W)),
     )(dev, rhs)
     g_far = swap(a_far, FAR)
     g_mate = swap(a_mate, MATE)
-    ui, dots_ui, stiff_v, mortar_v, weights, theta = call(
+    ui, dots_ui, theta, stiff_v, mortar_v, dual_v, meta = call(
         inner_first_kernel,
         "inner_first",
-        [smem(), vmem(), vmem(), anywhere(), anywhere()],
+        [smem()] * 4 + whole(2) + [anywhere()] * 2,
         (
             f32(*half),
             flat,
+            f32(8, W),
             f32(PLANES, W, W),
             jax.ShapeDtypeStruct(mortar.shape, mortar.dtype),
-            f32(W, W),
-            f32(8, W),
+            f32(PLANES, W),
+            jax.ShapeDtypeStruct((32,), jnp.int32),
         ),
         [pltpu.VMEM((3, 12, W, W), F32), dma(2)],
         stage,
-    )(st, rhs, dual, stiff, mortar)
+        out_specs=(vmem(),) * 6 + (smem(),),
+    )(dev, st, partner, active, field, dual, stiff, mortar)
     own_faces = jnp.concatenate([a_mate[HALO : HALO + 4], g_mate[HALO : HALO + 4], g_far[HALO : HALO + 4]])
-    own_faces, ui, meta = lax.optimization_barrier((own_faces, ui, meta))
+    own_faces, ui = lax.optimization_barrier((own_faces, ui))
     faces = swap(own_faces, CROSS)
     ue, dots_ue, b_mate, b_far = call(
         edge_first_kernel,
@@ -570,14 +595,14 @@
         (f32(*half), flat, f32(HALO + 8, W), f32(HALO + 8, W)),
         [pltpu.VMEM((3, 18, W, W), F32)],
         stage,
-    )(dev, st, rhs, g_mate, g_far, stiff_v, ui)
-    items, push_cols, dots_c = call(
+    )(dev, st, field, g_mate, g_far, stiff_v, ui)
+    items, dots_c = call(
         contact0_kernel,
         "contact0",
         [smem()] + whole(5),
-        (f32(16, W), f32(W, W), f32(8, W)),
-        [pltpu.VMEM((16, W), F32)],
-    )(meta, faces, g_far, rhs, weights, mortar_v)
+        (f32(16, W), f32(8, W)),
+        [pltpu.VMEM((16, W), F32), pltpu.VMEM((16, W), F32)],
+    )(meta, faces, g_far, r_rows, dual_v, mortar_v)
     u_rows = b_mate[HALO : HALO + 8]
     h_mate = swap(jnp.concatenate([b_mate, items]), MATE)
     mate_back = h_mate[HALO + 8 : HALO + 20]
@@ -602,15 +627,15 @@
         [pltpu.VMEM((3, 18, W, W), F32)],
         stage,
     )(dev, st, ui, ue, h_mate, h_far, stiff_v, ki)
-    send, k_cols = call(
+    send, rows = call(
         join_kernel,
         "join",
-        [smem()] + whole(19),
-        (f32(32, 8, W), f32(W, W)),
-        [pltpu.VMEM((16, W), F32), pltpu.VMEM((16, W), F32)],
+        [smem()] + whole(16),
+        (f32(32, 8, W), f32(64, W)),
+        [pltpu.VMEM((16, W), F32), pltpu.VMEM((16, W), F32), pltpu.VMEM((16, W), F32)],
     )(
-        meta, coefs, ui, ue, h_mate, h_far, pack, cross, items, push_cols, stiff_rows,
-        u_rows, k_rows, weights, mortar_v, dots_ui, dots_ue, dots_c, dots_ki, dots_ke,
+        meta, coefs, h_mate, h_far, pack, cross, items, stiff_rows,
+        u_rows, k_rows, dual_v, mortar_v, dots_ui, dots_ue, dots_c, dots_ki, dots_ke,
     )
     got = exchange(send, PLANE_GROUPS)
     relayed = call(relay_kernel, "relay", [smem(), vmem()], f32(8, 8, W))(dev, got)
@@ -618,11 +643,11 @@
     return call(
         final_kernel,
         "final",
-        whole(9),
+        whole(8),
         (f32(*shape), f32(*shape)),
-        [pltpu.VMEM(shape, F32), pltpu.VMEM(shape, F32), dma(2, 3, 4)],
+        [pltpu.VMEM(shape, F32), pltpu.VMEM(shape, F32), pltpu.VMEM((W, W), F32), dma(2, 3, 4)],
         out_specs=(anywhere(), anywhere()),
-    )(theta, rhs, ui, ue, ki, ke, push_cols, k_cols, sums)
+    )(theta, field, ui, ue, ki, ke, rows, sums)
 
 
 def solution(mesh):

time: 76 us -> 74 us (0.974)
  local copies, waits for them, and re-layouts: 4.62 us -> 2.07 us
  blocking collectives: 21.8 us -> 23 us
    unnamed x17 -> x15, local copies, waits for them, and re-layouts: 4.36 us -> 1.89 us
    all_to_all x2, blocking collectives: 21.8 us -> 23 us  [exchange(): return lax.all_to_all(x, 'slab', 0, 0, tiled=True, axis_index_groups=groups)]
  transfers between devices with their start and end apart: 7 -> 7, of which waited for: 5 -> 5; matrix products, arithmetic and copies ran while one was open for 1% -> 0% of each run, Pallas kernels for 20% -> 21%
where the time goes in v3:
time: 74 us; the launch traced here: 73.8 us
  blocking collectives  23 us (31%)
  starting transfers between devices  22 us (30%)
  Pallas kernels  20 us (27%)
  waiting for transfers between devices  5.96 us (8%)
  local copies, waits for them, and re-layouts  2.07 us (3%)
  between operations  0.78 us (1%)
    all_to_all x2, blocking collectives, exchange(): return lax.all_to_all(x, 'slab', 0, 0, tiled=True, axis_index_groups=groups)  23 us
    ppermute x7, starting transfers between devices, swap(): return lax.ppermute(x, 'slab', table)  22 us
    ppermute x7, waiting for transfers between devices, swap(): return lax.ppermute(x, 'slab', table)  5.96 us
    pallas_call x1, Pallas kernels, local(): call(inner_first_kernel, 'inner_first', [smem()] * 4 + whole(2) + [anywhe...  4.41 us
    pallas_call x1, Pallas kernels, local(): call(edge_first_kernel, 'edge_first', [smem(), smem()] + whole(5), (f32(*...  3.77 us
    pallas_call x1, Pallas kernels, local(): call(edge_second_kernel, 'edge_second', [smem(), smem()] + whole(6), (f32...  3.71 us
    pallas_call x1, Pallas kernels, local(): call(inner_second_kernel, 'inner_second', [smem()] + whole(3), (f32(*half...  3.71 us
    unnamed x15, local copies, waits for them, and re-layouts  1.89 us
  transfers between devices with their start and end apart: 7, of which 5 were waited for; matrix products, arithmetic and copies ran while one was open for 0% of the time, Pallas kernels for 21%

profile of v3, /device:TPU:1, one launch (start us, length us, event | category | flops | bytes accessed | tf_op | source)
XLA Modules:
  0.0 73.8 jit_solution(16708605869560537961)
XLA Ops:
  0.6 1.1 %copy-done = f32[3,4,128,128]{3,2,1,0:T(8,128)S(1)} copy-done((f32[3,4,128,128]{3,2,1,0:T(8,128)S(1)}, f32[3,4,128,128]{3,2,1,0:T(8,128)}, u32[]{:S(2)}) %copy-start) | copy-done | bytes 786456
  1.8 0.2 load.1
  2.0 2.7 %collective-permute-start.1 = (f32[392,128]{1,0:T(8,128)S(1)}, f32[392,128]{1,0:T(8,128)S(1)}, u32[]{:S(2)}, u32[]{:S(2)}) collective-permute-start(f32[392,128]{1,0:T(8,128)S(1)} %get-tuple-element.35), channel_id=1, source_target_pairs={{0,255},{1,2},{2,1},{3,4},{4,3},{5,6},{6,5},{7,8},{8,7},{9,10},{10... | collective-permute-start | bytes 602120 | tf_op jit(solution)/shard_map/ppermute | solution.py:542
  4.7 8.8 %collective-permute-start = (f32[392,128]{1,0:T(8,128)S(1)}, f32[392,128]{1,0:T(8,128)S(1)}, u32[]{:S(2)}, u32[]{:S(2)}) collective-permute-start(f32[392,128]{1,0:T(8,128)S(1)} %get-tuple-element.34), channel_id=1, source_target_pairs={{0,1},{1,0},{2,3},{3,2},{4,5},{5,4},{6,7},{7,6},{8,9},{9,8},{10,11... | collective-permute-start | bytes 602120 | tf_op jit(solution)/shard_map/ppermute | solution.py:542
  13.6 0.2 reshape.11.st
  13.8 0.5 copy-done.3
  14.4 4.4 %inner_first.1 = (f32[3,2,128,128]{3,2,1,0:T(8,128)S(1)}, f32[16,128]{1,0:T(8,128)S(1)}, f32[8,128]{1,0:T(8,128)S(1)}, f32[4,128,128]{2,1,0:T(8,128)S(1)}, bf16[...) custom-call(s32[1]{0:T(128)} %bitcast.dev, f32[243]{0:T(256)S(1)} %reshape.11.st, ...), custom_call_target="tpu_custom_call" | custom-call | flops 1000 | bytes 8000000 | tf_op jit(solution)/shard_map/inner_first/pallas_call | solution.py:571
  18.9 1.2 %collective-permute-start.2 = (f32[12,128]{1,0:T(8,128)S(1)}, f32[12,128]{1,0:T(8,128)S(1)}, u32[]{:S(2)}, u32[]{:S(2)}) collective-permute-start(f32[12,128]{1,0:T(8,128)S(1)} %pad_maximum_fusion.2), channel_id=1, source_target_pairs={{0,128},{1,129},{2,130},{3,131},{4,132},{5,133},{6,134},{7,135},{8... | collective-permute-start | bytes 18440 | tf_op jit(solution)/shard_map/ppermute | solution.py:542
  20.2 3.8 %edge_first.1 = (f32[3,2,128,128]{3,2,1,0:T(8,128)S(1)}, f32[16,128]{1,0:T(8,128)S(1)}, f32[392,128]{1,0:T(8,128)S(1)}, f32[392,128]{1,0:T(8,128)S(1)}) custom-call(s32[1]{0:T(128)} %bitcast.dev, f32[243]{0:T(256)S(1)} %reshape.11.st, f32[3,4,128,128]{3,2,1,0:T(8,128)S(1)} %get-tuple-element.32.field, f32[392,128]{1,0:T(8,128)S(1)} %collective-permute-done.mate, ...), custom_call_target="tpu_custom_call" | custom-call | flops 1000 | bytes 8000000 | tf_op jit(solution)/shard_map/edge_first/pallas_call | solution.py:591
  23.9 1.5 %collective-permute-done.2.faces = f32[12,128]{1,0:T(8,128)S(1)} collective-permute-done((f32[12,128]{1,0:T(8,128)S(1)}, f32[12,128]{1,0:T(8,128)S(1)}, u32[]{:S(2)}, u32[]{:S(2)}) %collective-permute-start.2) | collective-permute-done | bytes 6176 | tf_op jit(solution)/shard_map/ppermute | solution.py:542
  25.4 1.2 %contact0.1 = (f32[16,128]{1,0:T(8,128)S(1)}, f32[8,128]{1,0:T(8,128)S(1)}) custom-call(s32[32]{0:T(128)S(1)} %get-tuple-element.41.meta, f32[12,128]{1,0:T(8,128)S(1)} %collective-permute-done.2.faces, f32[392,128]{1,0:T(8,128)S(1)} %collective-permute-done.1.far, f32[8,128]{1,0:T(8,128)S(1)} %get-tuple-element.43.r_rows, ...), custom_call_target="tpu_custom_call" | custom-call | flops 1000 | bytes 1000000 | tf_op jit(solution)/shard_map/contact0/pallas_call | solution.py:599
  26.6 1.2 %collective-permute-start.3 = (f32[408,128]{1,0:T(8,128)S(1)}, f32[408,128]{1,0:T(8,128)S(1)}, u32[]{:S(2)}, u32[]{:S(2)}) collective-permute-start(f32[408,128]{1,0:T(8,128)S(1)} %pad_maximum_fusion.1), channel_id=1, source_target_pairs={{0,1},{1,0},{2,3},{3,2},{4,5},{5,4},{6,7},{7,6},{8,9},{9,8},{10,11... | collective-permute-start | bytes 626696 | tf_op jit(solution)/shard_map/ppermute | solution.py:542
  27.8 1.1 %collective-permute-done.3.mate = f32[408,128]{1,0:T(8,128)S(1)} collective-permute-done((f32[408,128]{1,0:T(8,128)S(1)}, f32[408,128]{1,0:T(8,128)S(1)}, u32[]{:S(2)}, u32[]{:S(2)}) %collective-permute-start.3) | collective-permute-done | bytes 208928 | tf_op jit(solution)/shard_map/ppermute | solution.py:542
  29.1 3.7 %inner_second.1 = (f32[3,2,128,128]{3,2,1,0:T(8,128)S(1)}, f32[16,128]{1,0:T(8,128)S(1)}, f32[8,128]{1,0:T(8,128)S(1)}, f32[88,128]{1,0:T(8,128)S(1)}) custom-call(f32[243]{0:T(256)S(1)} %reshape.11.st, f32[3,2,128,128]{3,2,1,0:T(8,128)S(1)} %get-tuple-element.37.ui, f32[3,2,128,128]{3,2,1,0:T(8,128)S(1)} %get-tuple-element.39.ue, ...), custom_call_target="tpu_custom_call" | custom-call | flops 1000 | bytes 8000000 | tf_op jit(solution)/shard_map/inner_second/pallas_call | solution.py:610
  32.8 1.6 %collective-permute-done.4.far = f32[420,128]{1,0:T(8,128)S(1)} collective-permute-done((f32[420,128]{1,0:T(8,128)S(1)}, f32[420,128]{1,0:T(8,128)S(1)}, u32[]{:S(2)}, u32[]{:S(2)}) %collective-permute-start.4) | collective-permute-done | bytes 215072 | tf_op jit(solution)/shard_map/ppermute | solution.py:542
  34.4 5.8 %collective-permute-start.5 = (f32[12,128]{1,0:T(8,128)S(1)}, f32[12,128]{1,0:T(8,128)S(1)}, u32[]{:S(2)}, u32[]{:S(2)}) collective-permute-start(f32[12,128]{1,0:T(8,128)S(1)} %slice.23), channel_id=1, source_target_pairs={{0,1},{1,0},{2,3},{3,2},{4,5},{5,4},{6,7},{7,6},{8,9},{9,8},{10,11... | collective-permute-start | bytes 18440 | tf_op jit(solution)/shard_map/ppermute | solution.py:542
  40.2 0.8 %collective-permute-done.5.following = f32[12,128]{1,0:T(8,128)S(1)} collective-permute-done((f32[12,128]{1,0:T(8,128)S(1)}, f32[12,128]{1,0:T(8,128)S(1)}, u32[]{:S(2)}, u32[]{:S(2)}) %collective-permute-start.5) | collective-permute-done | bytes 6176 | tf_op jit(solution)/shard_map/ppermute | solution.py:542
  41.0 2.1 %collective-permute-start.6 = (f32[72,128]{1,0:T(8,128)S(1)}, f32[72,128]{1,0:T(8,128)S(1)}, u32[]{:S(2)}, u32[]{:S(2)}) collective-permute-start(f32[72,128]{1,0:T(8,128)S(1)} %gather.1.pack), channel_id=1, source_target_pairs={{0,128},{1,129},{2,130},{3,131},{4,132},{5,133},{6,134},{7,135},{8... | collective-permute-start | bytes 110600 | tf_op jit(solution)/shard_map/ppermute | solution.py:542
  43.1 3.7 %edge_second.1 = (f32[3,2,128,128]{3,2,1,0:T(8,128)S(1)}, f32[16,128]{1,0:T(8,128)S(1)}, f32[8,128]{1,0:T(8,128)S(1)}) custom-call(s32[1]{0:T(128)} %bitcast.dev, f32[243]{0:T(256)S(1)} %reshape.11.st, f32[3,2,128,128]{3,2,1,0:T(8,128)S(1)} %get-tuple-element.37.ui, f32[3,2,128,128]{3,2,1,0:T(8,128)S(1)} %get-tuple-element.39.ue, ...), custom_call_target="tpu_custom_call" | custom-call | flops 1000 | bytes 8000000 | tf_op jit(solution)/shard_map/edge_second/pallas_call | solution.py:622
  46.8 1.0 %collective-permute-done.6.cross = f32[72,128]{1,0:T(8,128)S(1)} collective-permute-done((f32[72,128]{1,0:T(8,128)S(1)}, f32[72,128]{1,0:T(8,128)S(1)}, u32[]{:S(2)}, u32[]{:S(2)}) %collective-permute-start.6) | collective-permute-done | bytes 36896 | tf_op jit(solution)/shard_map/ppermute | solution.py:542
  47.8 1.2 %join.1 = (f32[32,8,128]{2,1,0:T(8,128)S(1)}, f32[64,128]{1,0:T(8,128)S(1)}) custom-call(s32[32]{0:T(128)S(1)} %get-tuple-element.41.meta, f32[88,128]{1,0:T(8,128)S(1)} %get-tuple-element.52.coefs, f32[408,128]{1,0:T(8,128)S(1)} %collective-permute-done.3.mate, f32[420,128]{1,0:T(8,128)S(1)} %collective-permute-done.4.far, f32[72,128]{1,0:T(8,128)S(1)} %gather.1.pack, ...), custom_call_target="tpu_custom_call" | custom-call | flops 1000 | bytes 1000000 | tf_op jit(solution)/shard_map/join/pallas_call | solution.py:630
  48.9 11.9 %all_to_all.10.got = f32[32,8,128]{2,1,0:T(8,128)S(1)} all-to-all(f32[32,8,128]{2,1,0:T(8,128)S(1)} %get-tuple-element.61), channel_id=1, replica_groups={{0,1,2,3,4,5,6,7,8,9,10,11,12,13,14,15,16,17,18,19,20,21,22,23,24,25,26..., dimensions={0} | all-to-all | bytes 262144 | tf_op jit(solution)/shard_map/all_to_all | solution.py:546
  60.9 11.1 %all_to_all.11.got = f32[8,8,128]{2,1,0:T(8,128)S(1)} all-to-all(f32[8,8,128]{2,1,0:T(8,128)S(1)} %relay.1), channel_id=1, replica_groups={{0,32,64,96,128,160,192,224},{1,33,65,97,129,161,193,225},{2,34,66,98,1..., dimensions={0} | all-to-all | bytes 65536 | tf_op jit(solution)/shard_map/all_to_all | solution.py:546
  72.0 1.8 %final.1 = (f32[3,4,128,128]{3,2,1,0:T(8,128)}, f32[3,4,128,128]{3,2,1,0:T(8,128)}) custom-call(f32[8,128]{1,0:T(8,128)S(1)} %get-tuple-element.33.theta_v, f32[3,4,128,128]{3,2,1,0:T(8,128)S(1)} %get-tuple-element.32.field, f32[3,2,128,128]{3,2,1,0:T(8,128)S(1)} %get-tuple-element.37.ui, f32[3,2,128,128]{3,2,1,0:T(8,128)S(1)} %get-tuple-element.39.ue, ...), custom_call_target="tpu_custom_call" | custom-call | flops 1000 | bytes 1000000 | tf_op jit(solution)/shard_map/final/pallas_call | solution.py:643
  (27 shorter events, 0.5 us)
Async XLA Ops:
  0.6 1.1 %copy-start = (f32[3,4,128,128]{3,2,1,0:T(8,128)S(1)}, f32[3,4,128,128]{3,2,1,0:T(8,128)}, u32[]{:S(2)}) copy-start(f32[3,4,128,128]{3,2,1,0:T(8,128)} %rhs.1) | copy-start | bytes 2359300
  1.8 11.7 %copy-start.6 = (f32[27,3,3]{0,2,1:T(4,128)S(1)}, f32[27,3,3]{0,2,1:T(4,128)}, u32[]{:S(2)}) copy-start(f32[27,3,3]{0,2,1:T(4,128)} %param.9) | copy-start | bytes 2920
  1.8 12.0 %copy-start.1 = (bf16[4,3,128,128]{3,2,1,0:T(8,128)(2,1)S(1)}, bf16[4,3,128,128]{3,2,1,0:T(8,128)(2,1)}, u32[]{:S(2)}) copy-start(bf16[4,3,128,128]{3,2,1,0:T(8,128)(2,1)} %mortar.1) | copy-start | bytes 1179652
  1.8 12.0 %copy-start.2 = (f32[4,128,128]{2,1,0:T(8,128)S(1)}, f32[4,128,128]{2,1,0:T(8,128)}, u32[]{:S(2)}) copy-start(f32[4,128,128]{2,1,0:T(8,128)} %stiff.1) | copy-start | bytes 786436
  2.0 16.9 %collective-permute-start.1 = (f32[392,128]{1,0:T(8,128)S(1)}, f32[392,128]{1,0:T(8,128)S(1)}, u32[]{:S(2)}, u32[]{:S(2)}) collective-permute-start(f32[392,128]{1,0:T(8,128)S(1)} %get-tuple-element.35), channel_id=1, source_target_pairs={{0,255},{1,2},{2,1},{3,4},{4,3},{5,6},{6,5},{7,8},{8,7},{9,10},{10... | collective-permute-start | bytes 602120 | tf_op jit(solution)/shard_map/ppermute | solution.py:542
  4.7 14.2 %collective-permute-start = (f32[392,128]{1,0:T(8,128)S(1)}, f32[392,128]{1,0:T(8,128)S(1)}, u32[]{:S(2)}, u32[]{:S(2)}) collective-permute-start(f32[392,128]{1,0:T(8,128)S(1)} %get-tuple-element.34), channel_id=1, source_target_pairs={{0,1},{1,0},{2,3},{3,2},{4,5},{5,4},{6,7},{7,6},{8,9},{9,8},{10,11... | collective-permute-start | bytes 602120 | tf_op jit(solution)/shard_map/ppermute | solution.py:542
  13.6 0.7 copy-start.3
  13.6 0.7 copy-start.4
  13.8 0.7 copy-start.5
  18.9 6.5 %collective-permute-start.2 = (f32[12,128]{1,0:T(8,128)S(1)}, f32[12,128]{1,0:T(8,128)S(1)}, u32[]{:S(2)}, u32[]{:S(2)}) collective-permute-start(f32[12,128]{1,0:T(8,128)S(1)} %pad_maximum_fusion.2), channel_id=1, source_target_pairs={{0,128},{1,129},{2,130},{3,131},{4,132},{5,133},{6,134},{7,135},{8... | collective-permute-start | bytes 18440 | tf_op jit(solution)/shard_map/ppermute | solution.py:542
  26.6 2.3 %collective-permute-start.3 = (f32[408,128]{1,0:T(8,128)S(1)}, f32[408,128]{1,0:T(8,128)S(1)}, u32[]{:S(2)}, u32[]{:S(2)}) collective-permute-start(f32[408,128]{1,0:T(8,128)S(1)} %pad_maximum_fusion.1), channel_id=1, source_target_pairs={{0,1},{1,0},{2,3},{3,2},{4,5},{5,4},{6,7},{7,6},{8,9},{9,8},{10,11... | collective-permute-start | bytes 626696 | tf_op jit(solution)/shard_map/ppermute | solution.py:542
  29.0 5.4 %collective-permute-start.4 = (f32[420,128]{1,0:T(8,128)S(1)}, f32[420,128]{1,0:T(8,128)S(1)}, u32[]{:S(2)}, u32[]{:S(2)}) collective-permute-start(f32[420,128]{1,0:T(8,128)S(1)} %pad_maximum_fusion), channel_id=1, source_target_pairs={{0,255},{1,2},{2,1},{3,4},{4,3},{5,6},{6,5},{7,8},{8,7},{9,10},{10... | collective-permute-start | bytes 645128 | tf_op jit(solution)/shard_map/ppermute | solution.py:542
  34.4 6.6 %collective-permute-start.5 = (f32[12,128]{1,0:T(8,128)S(1)}, f32[12,128]{1,0:T(8,128)S(1)}, u32[]{:S(2)}, u32[]{:S(2)}) collective-permute-start(f32[12,128]{1,0:T(8,128)S(1)} %slice.23), channel_id=1, source_target_pairs={{0,1},{1,0},{2,3},{3,2},{4,5},{5,4},{6,7},{7,6},{8,9},{9,8},{10,11... | collective-permute-start | bytes 18440 | tf_op jit(solution)/shard_map/ppermute | solution.py:542
  41.0 6.8 %collective-permute-start.6 = (f32[72,128]{1,0:T(8,128)S(1)}, f32[72,128]{1,0:T(8,128)S(1)}, u32[]{:S(2)}, u32[]{:S(2)}) collective-permute-start(f32[72,128]{1,0:T(8,128)S(1)} %gather.1.pack), channel_id=1, source_target_pairs={{0,128},{1,129},{2,130},{3,131},{4,132},{5,133},{6,134},{7,135},{8... | collective-permute-start | bytes 110600 | tf_op jit(solution)/shard_map/ppermute | solution.py:542

commit v4 on v3

--- a/solution.py
+++ b/solution.py
@@ -260,46 +260,42 @@
 
 
 def thirds(v):
-    a = v.astype(jnp.bfloat16)
-    rest = v - a.astype(F32)
-    b = rest.astype(jnp.bfloat16)
-    c = (rest - b.astype(F32)).astype(jnp.bfloat16)
-    return jnp.concatenate([a, b, c], axis=0)
+    a = v.astype(jnp.bfloat16).astype(F32)
+    rest = v - a
+    b = rest.astype(jnp.bfloat16).astype(F32)
+    return jnp.concatenate([a, b, rest - b, jnp.zeros_like(a)], axis=0).astype(jnp.bfloat16)
 
 
 def contact(meta, slave, table, dual, mortar, back, picked):
-    for t in range(PLANES):
-        for s in range(3):
-            picked[3 * t + s : 3 * t + s + 1, :] = table[pl.ds(4 * s + meta[3 * t + s], 1), :]
-    picked[12:16, :] = jnp.zeros((4, W), F32)
-    parts = thirds(picked[...])
+    parts = []
+    for s in range(3):
+        for t in range(PLANES):
+            picked[8 * s + t : 8 * s + t + 1, :] = table[pl.ds(4 * s + meta[3 * t + s], 1), :]
+        parts.append(thirds(picked[8 * s : 8 * s + PLANES, :]))
+    left = jnp.concatenate(parts, axis=1)
+    blocks = [jnp.concatenate([mortar[t, s] for s in range(3)], axis=1) for t in range(PLANES)]
     pulled = []
     for t in range(PLANES):
-        total = None
-        for s in range(3):
-            got = lax.dot_general(
-                parts, mortar[t, s], (((1,), (1,)), ((), ())), preferred_element_type=F32
-            )
-            r = 3 * t + s
-            row = got[r : r + 1] + (got[16 + r : 17 + r] + got[32 + r : 33 + r])
-            total = row if total is None else total + row
-        pulled.append(total)
+        got = lax.dot_general(
+            left, blocks[t], (((1,), (1,)), ((), ())), preferred_element_type=F32
+        )
+        pulled.append(got[t : t + 1] + (got[4 + t : 5 + t] + got[8 + t : 9 + t]))
     gap = dual * slave - jnp.concatenate(pulled, axis=0)
     which = iota(0, (PLANES, W))
     scale = jnp.zeros((PLANES, W), F32)
     for t in range(PLANES):
         scale = jnp.where(which == t, F32(4.0) * meta[12 + t].astype(F32), scale)
     push = scale * gap
-    parts = thirds(jnp.concatenate([push, jnp.zeros((16 - PLANES, W), F32)], axis=0))
+    left = thirds(push)
+    rows = []
+    for t in range(PLANES):
+        got = jnp.dot(left, blocks[t], preferred_element_type=F32)
+        rows.append(got[t : t + 1] + (got[4 + t : 5 + t] + got[8 + t : 9 + t]))
     for s in range(3):
-        rows = []
-        for t in range(PLANES):
-            got = jnp.dot(parts, mortar[t, s], preferred_element_type=F32)
-            rows.append(got[t : t + 1] + (got[16 + t : 17 + t] + got[32 + t : 33 + t]))
         for k in range(4):
             total = None
             for t in range(PLANES):
-                term = jnp.where(meta[3 * t + s] == k, rows[t], 0.0)
+                term = jnp.where(meta[3 * t + s] == k, rows[t][:, s * W : (s + 1) * W], 0.0)
                 total = term if total is None else total + term
             back[4 * s + k : 4 * s + k + 1, :] = -total
     return push * gap, dual * push
@@ -343,7 +339,7 @@
 
 
 def join_kernel(
-    meta, coefs, mate, far, pack, cross, items, stiff_rows, u_rows, k_rows,
+    meta, coefs, mate_items, far, pack, cross, items, stiff_rows, u_rows, k_rows,
     dual, mortar, dots_ui, dots_ue, dots_c, dots_ki, dots_ke,
     send, rows, table, back, picked,
 ):
@@ -365,7 +361,7 @@
     own_total, own_push = master[1], items[12:16, :]
     before = pick(place == 0, slave[0], master[0])[3:4]
     after = pick(place == 127, slave[2], master[2])[0:1]
-    mate_push = mate[HALO + 20 : HALO + 24, :]
+    mate_push = mate_items[12:16, :]
     far_push = far[HALO + 20 : HALO + 24, :]
     push_before = pick(odd, mate_push, far_push)[3:4]
     push_after = pick(odd, far_push, mate_push)[0:1]
@@ -435,14 +431,14 @@
     send[(column + 1) % 32, 4:8, :] = back[8:12, :]
 
 
-def gather_kernel(u_rows, mate, far, following, items, pack):
+def gather_kernel(u_rows, mate, mate_items, far, following, items, pack):
     start = HALO + 8
     parts = [
         u_rows[0:4, :],
         mate[HALO : HALO + 4, :],
         far[HALO : HALO + 4, :],
         items[0:12, :],
-        mate[start : start + 12, :],
+        mate_items[0:12, :],
         far[start : start + 12, :],
         far[start + 16 : start + 28, :],
         following[0:12, :],
@@ -502,29 +498,43 @@
         )
     work[48:64, :] = -cross * rows[48:64, :]
     work[64:W, :] = jnp.zeros((W - 64, W), F32)
-    columns = work[...].T
-    lane = iota(1)
+    work[...] = work[...].T
+    lane = iota(1, (BLOCK, W))
     rim = jnp.logical_or(lane < 2, lane >= W - 2)
 
-    def on_rim(q):
-        return jnp.where(rim, pltpu.roll(columns, (W - 4 * q - 2) % W, 1), 0.0)
-
-    copies = []
+    def copies(c, x):
+        return [
+            pltpu.make_async_copy(source.at[c, x], target.at[c, x], sems.at[i, c, x])
+            for i, (source, target) in enumerate(((inc_s, inc), (res_s, res)))
+        ]
+
+    def body(i, _):
+        for v_from, k_from, x in ((ue, ke, 3 * i), (ui, ki, 1 + i)):
+            for c in range(3):
+
+                def block_of(b, _):
+                    rows_y = pl.ds(pl.multiple_of(b * BLOCK, BLOCK), BLOCK)
+                    columns = work[rows_y, :]
+
+                    def on_rim(q):
+                        return jnp.where(rim, pltpu.roll(columns, W - 2 - 4 * q, 1), 0.0)
+
+                    r, v, k = field[c, x, rows_y, :], v_from[c, i, rows_y, :], k_from[c, i, rows_y, :]
+                    grown = both * r - cross * v
+                    inc_s[c, x, rows_y, :] = grown + on_rim(12 + x) if c == 2 else grown
+                    res_s[c, x, rows_y, :] = keep * r - both * v + (cross * k + on_rim(4 * c + x))
+                    return 0
+
+                lax.fori_loop(0, W // BLOCK, block_of, 0, unroll=True)
+                for copy in copies(c, x):
+                    copy.start()
+        return 0
+
+    lax.fori_loop(0, 2, body, 0)
     for x in range(PLANES):
         for c in range(3):
-            r = field[c, x]
-            v = ue[c, x // 3] if x in (0, 3) else ui[c, x - 1]
-            k = ke[c, x // 3] if x in (0, 3) else ki[c, x - 1]
-            grown = both * r - cross * v
-            left = keep * r - both * v + cross * k + on_rim(4 * c + x)
-            inc_s[c, x] = grown + on_rim(12 + x) if c == 2 else grown
-            res_s[c, x] = left
-            for i, (source, target) in enumerate(((inc_s, inc), (res_s, res))):
-                copy = pltpu.make_async_copy(source.at[c, x], target.at[c, x], sems.at[i, c, x])
-                copy.start()
-                copies.append(copy)
-    for copy in copies:
-        copy.wait()
+            for copy in copies(c, x):
+                copy.wait()
 
 
 def pairs(f):
@@ -596,17 +606,18 @@
         [pltpu.VMEM((3, 18, W, W), F32)],
         stage,
     )(dev, st, field, g_mate, g_far, stiff_v, ui)
+    faces, b_mate, b_far = lax.optimization_barrier((faces, b_mate, b_far))
     items, dots_c = call(
         contact0_kernel,
         "contact0",
         [smem()] + whole(5),
         (f32(16, W), f32(8, W)),
-        [pltpu.VMEM((16, W), F32), pltpu.VMEM((16, W), F32)],
+        [pltpu.VMEM((16, W), F32), pltpu.VMEM((24, W), F32)],
     )(meta, faces, g_far, r_rows, dual_v, mortar_v)
     u_rows = b_mate[HALO : HALO + 8]
-    h_mate = swap(jnp.concatenate([b_mate, items]), MATE)
-    mate_back = h_mate[HALO + 8 : HALO + 20]
-    h_far = swap(jnp.concatenate([b_far, items, mate_back]), FAR)
+    h_mate = swap(b_mate, MATE)
+    mate_items = swap(items, MATE)
+    h_far = swap(jnp.concatenate([b_far, items, mate_items[0:12]]), FAR)
     ki, dots_ki, stiff_rows, coefs = call(
         inner_second_kernel,
         "inner_second",
@@ -617,7 +628,7 @@
     )(st, ui, ue, stiff_v)
     h_far, ki = lax.optimization_barrier((h_far, ki))
     h_next = swap(h_far[HALO + 8 : HALO + 20], MATE)
-    pack = call(gather_kernel, "gather", whole(5), f32(72, W))(u_rows, h_mate, h_far, h_next, items)
+    pack = call(gather_kernel, "gather", whole(6), f32(72, W))(u_rows, h_mate, mate_items, h_far, h_next, items)
     cross = swap(pack, CROSS)
     ke, dots_ke, k_rows = call(
         edge_second_kernel,
@@ -632,9 +643,9 @@
         "join",
         [smem()] + whole(16),
         (f32(32, 8, W), f32(64, W)),
-        [pltpu.VMEM((16, W), F32), pltpu.VMEM((16, W), F32), pltpu.VMEM((16, W), F32)],
+        [pltpu.VMEM((16, W), F32), pltpu.VMEM((16, W), F32), pltpu.VMEM((24, W), F32)],
     )(
-        meta, coefs, h_mate, h_far, pack, cross, items, stiff_rows,
+        meta, coefs, mate_items, h_far, pack, cross, items, stiff_rows,
         u_rows, k_rows, dual_v, mortar_v, dots_ui, dots_ue, dots_c, dots_ki, dots_ke,
     )
     got = exchange(send, PLANE_GROUPS)

time: 74 us -> 73.3 us (level)
  waiting for transfers between devices: 5.96 us -> 4.11 us
  starting transfers between devices: 22 us -> 23.5 us
    ppermute x7 -> x8, waiting for transfers between devices: 5.96 us -> 4.11 us  [swap(): return lax.ppermute(x, 'slab', table)]
    ppermute x7 -> x8, starting transfers between devices: 22 us -> 23.5 us  [swap(): return lax.ppermute(x, 'slab', table)]
  transfers between devices with their start and end apart: 7 -> 8, of which waited for: 5 -> 4; matrix products, arithmetic and copies ran while one was open for 0% -> 0% of each run, Pallas kernels for 21% -> 21%
where the time goes in v4:
time: 73.3 us; the launch traced here: 73 us
  starting transfers between devices  23.5 us (32%)
  blocking collectives  23 us (31%)
  Pallas kernels  19.5 us (27%)
  waiting for transfers between devices  4.11 us (6%)
  local copies, waits for them, and re-layouts  2.06 us (3%)
  between operations  0.79 us (1%)
    ppermute x8, starting transfers between devices, swap(): return lax.ppermute(x, 'slab', table)  23.5 us
    all_to_all x2, blocking collectives, exchange(): return lax.all_to_all(x, 'slab', 0, 0, tiled=True, axis_index_groups=groups)  23 us
    pallas_call x1, Pallas kernels, local(): call(inner_first_kernel, 'inner_first', [smem()] * 4 + whole(2) + [anywhe...  4.41 us
    ppermute x8, waiting for transfers between devices, swap(): return lax.ppermute(x, 'slab', table)  4.11 us
    pallas_call x1, Pallas kernels, local(): call(edge_first_kernel, 'edge_first', [smem(), smem()] + whole(5), (f32(*...  3.77 us
    pallas_call x1, Pallas kernels, local(): call(edge_second_kernel, 'edge_second', [smem(), smem()] + whole(6), (f32...  3.72 us
    pallas_call x1, Pallas kernels, local(): call(inner_second_kernel, 'inner_second', [smem()] + whole(3), (f32(*half...  3.71 us
    unnamed x15, local copies, waits for them, and re-layouts  1.89 us
  transfers between devices with their start and end apart: 8, of which 4 were waited for; matrix products, arithmetic and copies ran while one was open for 0% of the time, Pallas kernels for 21%

profile of v4, /device:TPU:1, one launch (start us, length us, event | category | flops | bytes accessed | tf_op | source)
XLA Modules:
  0.0 73.0 jit_solution(9110508602148846123)
XLA Ops:
  0.6 1.1 %copy-done = f32[3,4,128,128]{3,2,1,0:T(8,128)S(1)} copy-done((f32[3,4,128,128]{3,2,1,0:T(8,128)S(1)}, f32[3,4,128,128]{3,2,1,0:T(8,128)}, u32[]{:S(2)}) %copy-start) | copy-done | bytes 786456
  1.8 0.2 load.1
  2.0 2.7 %collective-permute-start.1 = (f32[392,128]{1,0:T(8,128)S(1)}, f32[392,128]{1,0:T(8,128)S(1)}, u32[]{:S(2)}, u32[]{:S(2)}) collective-permute-start(f32[392,128]{1,0:T(8,128)S(1)} %get-tuple-element.38), channel_id=1, source_target_pairs={{0,255},{1,2},{2,1},{3,4},{4,3},{5,6},{6,5},{7,8},{8,7},{9,10},{10... | collective-permute-start | bytes 602120 | tf_op jit(solution)/shard_map/ppermute | solution.py:552
  4.7 8.8 %collective-permute-start = (f32[392,128]{1,0:T(8,128)S(1)}, f32[392,128]{1,0:T(8,128)S(1)}, u32[]{:S(2)}, u32[]{:S(2)}) collective-permute-start(f32[392,128]{1,0:T(8,128)S(1)} %get-tuple-element.37), channel_id=1, source_target_pairs={{0,1},{1,0},{2,3},{3,2},{4,5},{5,4},{6,7},{7,6},{8,9},{9,8},{10,11... | collective-permute-start | bytes 602120 | tf_op jit(solution)/shard_map/ppermute | solution.py:552
  13.6 0.2 reshape.11.st
  13.8 0.5 copy-done.3
  14.4 4.4 %inner_first.1 = (f32[3,2,128,128]{3,2,1,0:T(8,128)S(1)}, f32[16,128]{1,0:T(8,128)S(1)}, f32[8,128]{1,0:T(8,128)S(1)}, f32[4,128,128]{2,1,0:T(8,128)S(1)}, bf16[...) custom-call(s32[1]{0:T(128)} %bitcast.dev, f32[243]{0:T(256)S(1)} %reshape.11.st, ...), custom_call_target="tpu_custom_call" | custom-call | flops 1000 | bytes 8000000 | tf_op jit(solution)/shard_map/inner_first/pallas_call | solution.py:581
  18.9 1.2 %collective-permute-start.2 = (f32[12,128]{1,0:T(8,128)S(1)}, f32[12,128]{1,0:T(8,128)S(1)}, u32[]{:S(2)}, u32[]{:S(2)}) collective-permute-start(f32[12,128]{1,0:T(8,128)S(1)} %pad_maximum_fusion.1), channel_id=1, source_target_pairs={{0,128},{1,129},{2,130},{3,131},{4,132},{5,133},{6,134},{7,135},{8... | collective-permute-start | bytes 18440 | tf_op jit(solution)/shard_map/ppermute | solution.py:552
  20.2 3.8 %edge_first.1 = (f32[3,2,128,128]{3,2,1,0:T(8,128)S(1)}, f32[16,128]{1,0:T(8,128)S(1)}, f32[392,128]{1,0:T(8,128)S(1)}, f32[392,128]{1,0:T(8,128)S(1)}) custom-call(s32[1]{0:T(128)} %bitcast.dev, f32[243]{0:T(256)S(1)} %reshape.11.st, f32[3,4,128,128]{3,2,1,0:T(8,128)S(1)} %get-tuple-element.35.field, f32[392,128]{1,0:T(8,128)S(1)} %collective-permute-done.mate, ...), custom_call_target="tpu_custom_call" | custom-call | flops 1000 | bytes 8000000 | tf_op jit(solution)/shard_map/edge_first/pallas_call | solution.py:601
  23.9 1.5 %collective-permute-done.2.faces = f32[12,128]{1,0:T(8,128)S(1)} collective-permute-done((f32[12,128]{1,0:T(8,128)S(1)}, f32[12,128]{1,0:T(8,128)S(1)}, u32[]{:S(2)}, u32[]{:S(2)}) %collective-permute-start.2) | collective-permute-done | bytes 6176 | tf_op jit(solution)/shard_map/ppermute | solution.py:552
  25.4 1.0 %contact0.1 = (f32[16,128]{1,0:T(8,128)S(1)}, f32[8,128]{1,0:T(8,128)S(1)}) custom-call(s32[32]{0:T(128)S(1)} %get-tuple-element.47.meta, f32[12,128]{1,0:T(8,128)S(1)} %collective-permute-done.2.faces, f32[392,128]{1,0:T(8,128)S(1)} %collective-permute-done.1.far, f32[8,128]{1,0:T(8,128)S(1)} %get-tuple-element.49.r_rows, ...), custom_call_target="tpu_custom_call" | custom-call | flops 1000 | bytes 1000000 | tf_op jit(solution)/shard_map/contact0/pallas_call | solution.py:610
  26.4 1.2 %collective-permute-start.3 = (f32[16,128]{1,0:T(8,128)S(1)}, f32[16,128]{1,0:T(8,128)S(1)}, u32[]{:S(2)}, u32[]{:S(2)}) collective-permute-start(f32[16,128]{1,0:T(8,128)S(1)} %get-tuple-element.52.items), channel_id=1, source_target_pairs={{0,1},{1,0},{2,3},{3,2},{4,5},{5,4},{6,7},{7,6},{8,9},{9,8},{10,11... | collective-permute-start | bytes 24584 | tf_op jit(solution)/shard_map/ppermute | solution.py:552
  27.7 0.8 %collective-permute-done.3.mate_items = f32[16,128]{1,0:T(8,128)S(1)} collective-permute-done((f32[16,128]{1,0:T(8,128)S(1)}, f32[16,128]{1,0:T(8,128)S(1)}, u32[]{:S(2)}, u32[]{:S(2)}) %collective-permute-start.3) | collective-permute-done | bytes 8224 | tf_op jit(solution)/shard_map/ppermute | solution.py:552
  28.6 4.3 %collective-permute-start.5 = (f32[392,128]{1,0:T(8,128)S(1)}, f32[392,128]{1,0:T(8,128)S(1)}, u32[]{:S(2)}, u32[]{:S(2)}) collective-permute-start(f32[392,128]{1,0:T(8,128)S(1)} %get-tuple-element.55), channel_id=1, source_target_pairs={{0,1},{1,0},{2,3},{3,2},{4,5},{5,4},{6,7},{7,6},{8,9},{9,8},{10,11... | collective-permute-start | bytes 602120 | tf_op jit(solution)/shard_map/ppermute | solution.py:552
  32.9 3.7 %inner_second.1 = (f32[3,2,128,128]{3,2,1,0:T(8,128)S(1)}, f32[16,128]{1,0:T(8,128)S(1)}, f32[8,128]{1,0:T(8,128)S(1)}, f32[88,128]{1,0:T(8,128)S(1)}) custom-call(f32[243]{0:T(256)S(1)} %reshape.11.st, f32[3,2,128,128]{3,2,1,0:T(8,128)S(1)} %get-tuple-element.40.ui, f32[3,2,128,128]{3,2,1,0:T(8,128)S(1)} %get-tuple-element.42.ue, ...), custom_call_target="tpu_custom_call" | custom-call | flops 1000 | bytes 8000000 | tf_op jit(solution)/shard_map/inner_second/pallas_call | solution.py:621
  36.6 3.0 %collective-permute-start.6 = (f32[12,128]{1,0:T(8,128)S(1)}, f32[12,128]{1,0:T(8,128)S(1)}, u32[]{:S(2)}, u32[]{:S(2)}) collective-permute-start(f32[12,128]{1,0:T(8,128)S(1)} %slice.23), channel_id=1, source_target_pairs={{0,1},{1,0},{2,3},{3,2},{4,5},{5,4},{6,7},{7,6},{8,9},{9,8},{10,11... | collective-permute-start | bytes 18440 | tf_op jit(solution)/shard_map/ppermute | solution.py:552
  39.7 0.8 %collective-permute-done.6.following = f32[12,128]{1,0:T(8,128)S(1)} collective-permute-done((f32[12,128]{1,0:T(8,128)S(1)}, f32[12,128]{1,0:T(8,128)S(1)}, u32[]{:S(2)}, u32[]{:S(2)}) %collective-permute-start.6) | collective-permute-done | bytes 6176 | tf_op jit(solution)/shard_map/ppermute | solution.py:552
  40.5 2.1 %collective-permute-start.7 = (f32[72,128]{1,0:T(8,128)S(1)}, f32[72,128]{1,0:T(8,128)S(1)}, u32[]{:S(2)}, u32[]{:S(2)}) collective-permute-start(f32[72,128]{1,0:T(8,128)S(1)} %gather.1.pack), channel_id=1, source_target_pairs={{0,128},{1,129},{2,130},{3,131},{4,132},{5,133},{6,134},{7,135},{8... | collective-permute-start | bytes 110600 | tf_op jit(solution)/shard_map/ppermute | solution.py:552
  42.6 3.7 %edge_second.1 = (f32[3,2,128,128]{3,2,1,0:T(8,128)S(1)}, f32[16,128]{1,0:T(8,128)S(1)}, f32[8,128]{1,0:T(8,128)S(1)}) custom-call(s32[1]{0:T(128)} %bitcast.dev, f32[243]{0:T(256)S(1)} %reshape.11.st, f32[3,2,128,128]{3,2,1,0:T(8,128)S(1)} %get-tuple-element.40.ui, f32[3,2,128,128]{3,2,1,0:T(8,128)S(1)} %get-tuple-element.42.ue, ...), custom_call_target="tpu_custom_call" | custom-call | flops 1000 | bytes 8000000 | tf_op jit(solution)/shard_map/edge_second/pallas_call | solution.py:633
  46.3 1.0 %collective-permute-done.7.cross = f32[72,128]{1,0:T(8,128)S(1)} collective-permute-done((f32[72,128]{1,0:T(8,128)S(1)}, f32[72,128]{1,0:T(8,128)S(1)}, u32[]{:S(2)}, u32[]{:S(2)}) %collective-permute-start.7) | collective-permute-done | bytes 36896 | tf_op jit(solution)/shard_map/ppermute | solution.py:552
  47.3 1.0 %join.1 = (f32[32,8,128]{2,1,0:T(8,128)S(1)}, f32[64,128]{1,0:T(8,128)S(1)}) custom-call(s32[32]{0:T(128)S(1)} %get-tuple-element.47.meta, f32[88,128]{1,0:T(8,128)S(1)} %get-tuple-element.58.coefs, f32[16,128]{1,0:T(8,128)S(1)} %collective-permute-done.3.mate_items, f32[420,128]{1,0:T(8,128)S(1)} %collective-permute-done.4.far, f32[72,128]{1,0:T(8,128)S(1)} %gather.1.pack, ...), custom_call_target="tpu_custom_call" | custom-call | flops 1000 | bytes 1000000 | tf_op jit(solution)/shard_map/join/pallas_call | solution.py:641
  48.3 11.9 %all_to_all.10.got = f32[32,8,128]{2,1,0:T(8,128)S(1)} all-to-all(f32[32,8,128]{2,1,0:T(8,128)S(1)} %get-tuple-element.67), channel_id=1, replica_groups={{0,1,2,3,4,5,6,7,8,9,10,11,12,13,14,15,16,17,18,19,20,21,22,23,24,25,26..., dimensions={0} | all-to-all | bytes 262144 | tf_op jit(solution)/shard_map/all_to_all | solution.py:556
  60.3 11.1 %all_to_all.11.got = f32[8,8,128]{2,1,0:T(8,128)S(1)} all-to-all(f32[8,8,128]{2,1,0:T(8,128)S(1)} %relay.1), channel_id=1, replica_groups={{0,32,64,96,128,160,192,224},{1,33,65,97,129,161,193,225},{2,34,66,98,1..., dimensions={0} | all-to-all | bytes 65536 | tf_op jit(solution)/shard_map/all_to_all | solution.py:556
  71.4 1.6 %final.1 = (f32[3,4,128,128]{3,2,1,0:T(8,128)}, f32[3,4,128,128]{3,2,1,0:T(8,128)}) custom-call(f32[8,128]{1,0:T(8,128)S(1)} %get-tuple-element.36.theta_v, f32[3,4,128,128]{3,2,1,0:T(8,128)S(1)} %get-tuple-element.35.field, f32[3,2,128,128]{3,2,1,0:T(8,128)S(1)} %get-tuple-element.40.ui, f32[3,2,128,128]{3,2,1,0:T(8,128)S(1)} %get-tuple-element.42.ue, ...), custom_call_target="tpu_custom_call" | custom-call | flops 1000 | bytes 1000000 | tf_op jit(solution)/shard_map/final/pallas_call | solution.py:654
  (27 shorter events, 0.5 us)
Async XLA Ops:
  0.6 1.1 %copy-start = (f32[3,4,128,128]{3,2,1,0:T(8,128)S(1)}, f32[3,4,128,128]{3,2,1,0:T(8,128)}, u32[]{:S(2)}) copy-start(f32[3,4,128,128]{3,2,1,0:T(8,128)} %rhs.1) | copy-start | bytes 2359300
  1.8 11.7 %copy-start.6 = (f32[27,3,3]{0,2,1:T(4,128)S(1)}, f32[27,3,3]{0,2,1:T(4,128)}, u32[]{:S(2)}) copy-start(f32[27,3,3]{0,2,1:T(4,128)} %param.9) | copy-start | bytes 2920
  1.8 12.0 %copy-start.1 = (bf16[4,3,128,128]{3,2,1,0:T(8,128)(2,1)S(1)}, bf16[4,3,128,128]{3,2,1,0:T(8,128)(2,1)}, u32[]{:S(2)}) copy-start(bf16[4,3,128,128]{3,2,1,0:T(8,128)(2,1)} %mortar.1) | copy-start | bytes 1179652
  1.8 12.0 %copy-start.2 = (f32[4,128,128]{2,1,0:T(8,128)S(1)}, f32[4,128,128]{2,1,0:T(8,128)}, u32[]{:S(2)}) copy-start(f32[4,128,128]{2,1,0:T(8,128)} %stiff.1) | copy-start | bytes 786436
  2.0 16.9 %collective-permute-start.1 = (f32[392,128]{1,0:T(8,128)S(1)}, f32[392,128]{1,0:T(8,128)S(1)}, u32[]{:S(2)}, u32[]{:S(2)}) collective-permute-start(f32[392,128]{1,0:T(8,128)S(1)} %get-tuple-element.38), channel_id=1, source_target_pairs={{0,255},{1,2},{2,1},{3,4},{4,3},{5,6},{6,5},{7,8},{8,7},{9,10},{10... | collective-permute-start | bytes 602120 | tf_op jit(solution)/shard_map/ppermute | solution.py:552
  4.7 14.2 %collective-permute-start = (f32[392,128]{1,0:T(8,128)S(1)}, f32[392,128]{1,0:T(8,128)S(1)}, u32[]{:S(2)}, u32[]{:S(2)}) collective-permute-start(f32[392,128]{1,0:T(8,128)S(1)} %get-tuple-element.37), channel_id=1, source_target_pairs={{0,1},{1,0},{2,3},{3,2},{4,5},{5,4},{6,7},{7,6},{8,9},{9,8},{10,11... | collective-permute-start | bytes 602120 | tf_op jit(solution)/shard_map/ppermute | solution.py:552
  13.6 0.7 copy-start.3
  13.6 0.7 copy-start.4
  13.8 0.7 copy-start.5
  18.9 6.5 %collective-permute-start.2 = (f32[12,128]{1,0:T(8,128)S(1)}, f32[12,128]{1,0:T(8,128)S(1)}, u32[]{:S(2)}, u32[]{:S(2)}) collective-permute-start(f32[12,128]{1,0:T(8,128)S(1)} %pad_maximum_fusion.1), channel_id=1, source_target_pairs={{0,128},{1,129},{2,130},{3,131},{4,132},{5,133},{6,134},{7,135},{8... | collective-permute-start | bytes 18440 | tf_op jit(solution)/shard_map/ppermute | solution.py:552
  26.4 2.1 %collective-permute-start.3 = (f32[16,128]{1,0:T(8,128)S(1)}, f32[16,128]{1,0:T(8,128)S(1)}, u32[]{:S(2)}, u32[]{:S(2)}) collective-permute-start(f32[16,128]{1,0:T(8,128)S(1)} %get-tuple-element.52.items), channel_id=1, source_target_pairs={{0,1},{1,0},{2,3},{3,2},{4,5},{5,4},{6,7},{7,6},{8,9},{9,8},{10,11... | collective-permute-start | bytes 24584 | tf_op jit(solution)/shard_map/ppermute | solution.py:552
  28.5 8.1 %collective-permute-start.4 = (f32[420,128]{1,0:T(8,128)S(1)}, f32[420,128]{1,0:T(8,128)S(1)}, u32[]{:S(2)}, u32[]{:S(2)}) collective-permute-start(f32[420,128]{1,0:T(8,128)S(1)} %pad_maximum_fusion), channel_id=1, source_target_pairs={{0,255},{1,2},{2,1},{3,4},{4,3},{5,6},{6,5},{7,8},{8,7},{9,10},{10... | collective-permute-start | bytes 645128 | tf_op jit(solution)/shard_map/ppermute | solution.py:552
  28.6 11.1 %collective-permute-start.5 = (f32[392,128]{1,0:T(8,128)S(1)}, f32[392,128]{1,0:T(8,128)S(1)}, u32[]{:S(2)}, u32[]{:S(2)}) collective-permute-start(f32[392,128]{1,0:T(8,128)S(1)} %get-tuple-element.55), channel_id=1, source_target_pairs={{0,1},{1,0},{2,3},{3,2},{4,5},{5,4},{6,7},{7,6},{8,9},{9,8},{10,11... | collective-permute-start | bytes 602120 | tf_op jit(solution)/shard_map/ppermute | solution.py:552
  36.6 3.9 %collective-permute-start.6 = (f32[12,128]{1,0:T(8,128)S(1)}, f32[12,128]{1,0:T(8,128)S(1)}, u32[]{:S(2)}, u32[]{:S(2)}) collective-permute-start(f32[12,128]{1,0:T(8,128)S(1)} %slice.23), channel_id=1, source_target_pairs={{0,1},{1,0},{2,3},{3,2},{4,5},{5,4},{6,7},{7,6},{8,9},{9,8},{10,11... | collective-permute-start | bytes 18440 | tf_op jit(solution)/shard_map/ppermute | solution.py:552
  40.5 6.8 %collective-permute-start.7 = (f32[72,128]{1,0:T(8,128)S(1)}, f32[72,128]{1,0:T(8,128)S(1)}, u32[]{:S(2)}, u32[]{:S(2)}) collective-permute-start(f32[72,128]{1,0:T(8,128)S(1)} %gather.1.pack), channel_id=1, source_target_pairs={{0,128},{1,129},{2,130},{3,131},{4,132},{5,133},{6,134},{7,135},{8... | collective-permute-start | bytes 110600 | tf_op jit(solution)/shard_map/ppermute | solution.py:552

commit v5 on v4

--- a/solution.py
+++ b/solution.py
@@ -74,9 +74,9 @@
     return jnp.where(flag, yes, no)
 
 
-def place_of(dev, at=0):
-    odd = dev[at] % 2 == 1
-    place = dev[at] % 128
+def place_of(dev):
+    odd = dev[0] % 2 == 1
+    place = dev[0] % 128
     return odd, place
 
 
@@ -183,21 +183,22 @@
 
 
 def inner_first_kernel(
-    dev, st, partner, active, field, dual, stiff, mortar,
-    ui, dots, theta, stiff_v, mortar_v, dual_v, meta, s, sems,
+    st, partner, active, field, dual, stiff, mortar,
+    ui, dots, theta, stiff_v, mortar_v, dual_v, masks, s, sems,
 ):
     stiff_copy = pltpu.make_async_copy(stiff, stiff_v, sems.at[0])
     mortar_copy = pltpu.make_async_copy(mortar, mortar_v, sems.at[1])
     stiff_copy.start()
     mortar_copy.start()
     dual_v[...] = dual[...]
+    masks[...] = jnp.zeros(masks.shape, F32)
     for t in range(PLANES):
         for slot in range(3):
-            meta[3 * t + slot] = partner[t, slot] % 4
-        meta[12 + t] = active[t]
-    meta[16] = dev[0]
-    for i in range(17, 32):
-        meta[i] = 0
+            for k in range(4):
+                at = 8 * (4 * slot + k) + t
+                chosen = jnp.where(partner[t, slot] % 4 == k, F32(1.0), F32(0.0))
+                masks[at : at + 1, :] = jnp.full((1, W), chosen, F32)
+        masks[96 + t : 97 + t, :] = jnp.full((1, W), F32(4.0) * active[t].astype(F32), F32)
     for c in range(3):
         for x in range(PLANES):
             s[1, c * 4 + x] = field[c, x]
@@ -266,12 +267,15 @@
     return jnp.concatenate([a, b, rest - b, jnp.zeros_like(a)], axis=0).astype(jnp.bfloat16)
 
 
-def contact(meta, slave, table, dual, mortar, back, picked):
+def contact(masks, slave, table, dual, mortar, back):
     parts = []
     for s in range(3):
-        for t in range(PLANES):
-            picked[8 * s + t : 8 * s + t + 1, :] = table[pl.ds(4 * s + meta[3 * t + s], 1), :]
-        parts.append(thirds(picked[8 * s : 8 * s + PLANES, :]))
+        chosen = None
+        for k in range(4):
+            j = 4 * s + k
+            term = masks[8 * j : 8 * j + PLANES, :] * table[j : j + 1, :]
+            chosen = term if chosen is None else chosen + term
+        parts.append(thirds(chosen))
     left = jnp.concatenate(parts, axis=1)
     blocks = [jnp.concatenate([mortar[t, s] for s in range(3)], axis=1) for t in range(PLANES)]
     pulled = []
@@ -281,23 +285,17 @@
         )
         pulled.append(got[t : t + 1] + (got[4 + t : 5 + t] + got[8 + t : 9 + t]))
     gap = dual * slave - jnp.concatenate(pulled, axis=0)
-    which = iota(0, (PLANES, W))
-    scale = jnp.zeros((PLANES, W), F32)
-    for t in range(PLANES):
-        scale = jnp.where(which == t, F32(4.0) * meta[12 + t].astype(F32), scale)
-    push = scale * gap
+    push = masks[96 : 96 + PLANES, :] * gap
     left = thirds(push)
     rows = []
     for t in range(PLANES):
         got = jnp.dot(left, blocks[t], preferred_element_type=F32)
         rows.append(got[t : t + 1] + (got[4 + t : 5 + t] + got[8 + t : 9 + t]))
     for s in range(3):
+        slot = jnp.concatenate([row[:, s * W : (s + 1) * W] for row in rows], axis=0)
         for k in range(4):
-            total = None
-            for t in range(PLANES):
-                term = jnp.where(meta[3 * t + s] == k, rows[t][:, s * W : (s + 1) * W], 0.0)
-                total = term if total is None else total + term
-            back[4 * s + k : 4 * s + k + 1, :] = -total
+            j = 4 * s + k
+            back[j : j + 1, :] = -jnp.sum(masks[8 * j : 8 * j + PLANES, :] * slot, axis=0, keepdims=True)
     return push * gap, dual * push
 
 
@@ -305,14 +303,14 @@
     return jnp.concatenate([rows, jnp.zeros((8 - PLANES, W), F32)], axis=0)
 
 
-def contact0_kernel(meta, faces, far, r_rows, dual, mortar, items, dots, table, picked):
-    odd, place = place_of(meta, 16)
+def contact0_kernel(dev, masks, faces, far, r_rows, dual, mortar, items, dots, table):
+    odd, place = place_of(dev)
     own, mate = faces[0:4, :], faces[4:8, :]
     other = pick(is_wrap(place), far[HALO : HALO + 4, :], faces[8:12, :])
     table[0:4, :] = pick(odd, mate, other)
     table[4:8, :] = own
     table[8:12, :] = pick(odd, other, mate)
-    energy, pushed = contact(meta, r_rows[4:8, :], table, dual[...], mortar, items, picked)
+    energy, pushed = contact(masks, r_rows[4:8, :], table, dual[...], mortar, items)
     items[12:16, :] = pushed
     dots[...] = pad8(energy)
 
@@ -334,16 +332,12 @@
     )
 
 
-def total_of(v):
-    return jnp.sum(jnp.sum(v, axis=0, keepdims=True), axis=1, keepdims=True)
-
-
 def join_kernel(
-    meta, coefs, mate_items, far, pack, cross, items, stiff_rows, u_rows, k_rows,
+    dev, masks, coefs, mate_items, far, pack, cross, items, stiff_rows, u_rows, k_rows,
     dual, mortar, dots_ui, dots_ue, dots_c, dots_ki, dots_ke,
-    send, rows, table, back, picked,
+    send, rows, table, back,
 ):
-    odd, place = place_of(meta, 16)
+    odd, place = place_of(dev)
     cut, swap_far = is_cut(place), is_wrap(place)
     even = jnp.logical_not(odd)
     swap_next = jnp.logical_or(place == 1, place == 126)
@@ -354,7 +348,7 @@
     table[4:8, :] = cross[0:4, :] + slave[1]
     table[8:12, :] = pick(odd, other, cross[4:8, :]) + slave[2]
 
-    energy, pushed = contact(meta, u_rows[4:8, :] + items[12:16, :], table, dual[...], mortar, back, picked)
+    energy, pushed = contact(masks, u_rows[4:8, :] + items[12:16, :], table, dual[...], mortar, back)
 
     low = jnp.logical_and(cut, even)
     high = jnp.logical_and(cut, odd)
@@ -416,16 +410,15 @@
         dots_ki[8:16, :] + dots_ke[8:16, :] + pad8(energy),
     )
     extra = (None, None, 2.0 * face + square, image)
-    wide8 = iota(1, (8, W))
-    row = jnp.zeros((8, W), F32)
-    for k, value in enumerate(values):
-        total = total_of(value)
-        if extra[k] is not None:
-            total = total + total_of(extra[k])
-        row = jnp.where(wide8 == k, total, row)
-    row = jnp.where(iota(0, (8, W)) == 0, row, 0.0)
-    send[...] = jnp.broadcast_to(row[None], (32, 8, W))
-    column = meta[16] % 32
+    dot_rows = []
+    for value, more in zip(values, extra):
+        row = jnp.sum(value, axis=0, keepdims=True)
+        if more is not None:
+            row = row + jnp.sum(more, axis=0, keepdims=True)
+        dot_rows.append(row)
+    block = jnp.concatenate(dot_rows + [jnp.zeros((4, W), F32)], axis=0)
+    send[...] = jnp.broadcast_to(block[None], (32, 8, W))
+    column = dev[0] % 32
     send[(column + 31) % 32, 4:8, :] = back[0:4, :]
     send[column, 4:8, :] = back[4:8, :]
     send[(column + 1) % 32, 4:8, :] = back[8:12, :]
@@ -457,7 +450,7 @@
     side = 4 * (1 - level // 4)
     crossing = pick(first, left, pick(last, right, 0.0))
     goal = side + (level + jnp.where(first, 1, jnp.where(last, 3, 0))) % 4
-    send[...] = jnp.broadcast_to(jnp.where(iota(0, (8, W)) == 0, dots, 0.0)[None], (8, 8, W))
+    send[...] = jnp.broadcast_to(jnp.where(iota(0, (8, W)) < 4, dots, 0.0)[None], (8, 8, W))
     send[level ^ 4, 4:8, :] = near
 
     @pl.when(jnp.logical_or(first, last))
@@ -468,11 +461,9 @@
 def final_kernel(theta_v, field, ui, ue, ki, ke, rows, got, inc, res, inc_s, res_s, work, sems):
     theta = theta_v[0:1, :]
     block = jnp.sum(got[...], axis=0)
-    row = block[0:1, :]
-    lane1 = iota(1, (1, W))
 
     def total(k):
-        value = jnp.sum(jnp.where(lane1 == k, row, 0.0), axis=1, keepdims=True)
+        value = jnp.sum(block[k : k + 1, :], axis=1, keepdims=True)
         return jnp.broadcast_to(value, (1, W))
 
     norm0, curve0, zz, zaz = total(0), total(1), total(2), total(3)
@@ -578,10 +569,10 @@
     )(dev, rhs)
     g_far = swap(a_far, FAR)
     g_mate = swap(a_mate, MATE)
-    ui, dots_ui, theta, stiff_v, mortar_v, dual_v, meta = call(
+    ui, dots_ui, theta, stiff_v, mortar_v, dual_v, masks = call(
         inner_first_kernel,
         "inner_first",
-        [smem()] * 4 + whole(2) + [anywhere()] * 2,
+        [smem()] * 3 + whole(2) + [anywhere()] * 2,
         (
             f32(*half),
             flat,
@@ -589,12 +580,11 @@
             f32(PLANES, W, W),
             jax.ShapeDtypeStruct(mortar.shape, mortar.dtype),
             f32(PLANES, W),
-            jax.ShapeDtypeStruct((32,), jnp.int32),
+            f32(104, W),
         ),
         [pltpu.VMEM((3, 12, W, W), F32), dma(2)],
         stage,
-        out_specs=(vmem(),) * 6 + (smem(),),
-    )(dev, st, partner, active, field, dual, stiff, mortar)
+    )(st, partner, active, field, dual, stiff, mortar)
     own_faces = jnp.concatenate([a_mate[HALO : HALO + 4], g_mate[HALO : HALO + 4], g_far[HALO : HALO + 4]])
     own_faces, ui = lax.optimization_barrier((own_faces, ui))
     faces = swap(own_faces, CROSS)
@@ -610,10 +600,10 @@
     items, dots_c = call(
         contact0_kernel,
         "contact0",
-        [smem()] + whole(5),
+        [smem()] + whole(6),
         (f32(16, W), f32(8, W)),
-        [pltpu.VMEM((16, W), F32), pltpu.VMEM((24, W), F32)],
-    )(meta, faces, g_far, r_rows, dual_v, mortar_v)
+        [pltpu.VMEM((16, W), F32)],
+    )(dev, masks, faces, g_far, r_rows, dual_v, mortar_v)
     u_rows = b_mate[HALO : HALO + 8]
     h_mate = swap(b_mate, MATE)
     mate_items = swap(items, MATE)
@@ -641,11 +631,11 @@
     send, rows = call(
         join_kernel,
         "join",
-        [smem()] + whole(16),
+        [smem()] + whole(17),
         (f32(32, 8, W), f32(64, W)),
-        [pltpu.VMEM((16, W), F32), pltpu.VMEM((16, W), F32), pltpu.VMEM((24, W), F32)],
+        [pltpu.VMEM((16, W), F32), pltpu.VMEM((16, W), F32)],
     )(
-        meta, coefs, mate_items, h_far, pack, cross, items, stiff_rows,
+        dev, masks, coefs, mate_items, h_far, pack, cross, items, stiff_rows,
         u_rows, k_rows, dual_v, mortar_v, dots_ui, dots_ue, dots_c, dots_ki, dots_ke,
     )
     got = exchange(send, PLANE_GROUPS)

time: 73.3 us -> 72.2 us (0.985)
  Pallas kernels: 19.5 us -> 17.8 us
    pallas_call x3, Pallas kernels: 6.4 us -> 4.77 us  [the longest x1 3.84 us: local(): call(inner_first_kernel, 'inner_first', [smem()] * 3 + whole(2) + [anywhe...]
where the time goes in v5:
time: 72.2 us; the launch traced here: 72 us
  starting transfers between devices  24.1 us (33%)
  blocking collectives  23.6 us (33%)
  Pallas kernels  17.8 us (25%)
  waiting for transfers between devices  3.54 us (5%)
  local copies, waits for them, and re-layouts  2.06 us (3%)
  between operations  0.78 us (1%)
    ppermute x8, starting transfers between devices, swap(): return lax.ppermute(x, 'slab', table)  24.1 us
    all_to_all x2, blocking collectives, exchange(): return lax.all_to_all(x, 'slab', 0, 0, tiled=True, axis_index_groups=groups)  23.6 us
    pallas_call x1, Pallas kernels, local(): call(inner_first_kernel, 'inner_first', [smem()] * 3 + whole(2) + [anywhe...  3.84 us
    pallas_call x1, Pallas kernels, local(): call(edge_first_kernel, 'edge_first', [smem(), smem()] + whole(5), (f32(*...  3.77 us
    pallas_call x1, Pallas kernels, local(): call(edge_second_kernel, 'edge_second', [smem(), smem()] + whole(6), (f32...  3.72 us
    pallas_call x1, Pallas kernels, local(): call(inner_second_kernel, 'inner_second', [smem()] + whole(3), (f32(*half...  3.71 us
    ppermute x8, waiting for transfers between devices, swap(): return lax.ppermute(x, 'slab', table)  3.54 us
    unnamed x15, local copies, waits for them, and re-layouts  1.89 us
  transfers between devices with their start and end apart: 8, of which 4 were waited for; matrix products, arithmetic and copies ran while one was open for 0% of the time, Pallas kernels for 21%

profile of v5, /device:TPU:1, one launch (start us, length us, event | category | flops | bytes accessed | tf_op | source)
XLA Modules:
  0.0 72.0 jit_solution(13112880128847260008)
XLA Ops:
  0.6 1.1 %copy-done = f32[3,4,128,128]{3,2,1,0:T(8,128)S(1)} copy-done((f32[3,4,128,128]{3,2,1,0:T(8,128)S(1)}, f32[3,4,128,128]{3,2,1,0:T(8,128)}, u32[]{:S(2)}) %copy-start) | copy-done | bytes 786456
  1.8 0.2 load.1
  2.0 2.7 %collective-permute-start.1 = (f32[392,128]{1,0:T(8,128)S(1)}, f32[392,128]{1,0:T(8,128)S(1)}, u32[]{:S(2)}, u32[]{:S(2)}) collective-permute-start(f32[392,128]{1,0:T(8,128)S(1)} %get-tuple-element.38), channel_id=1, source_target_pairs={{0,255},{1,2},{2,1},{3,4},{4,3},{5,6},{6,5},{7,8},{8,7},{9,10},{10... | collective-permute-start | bytes 602120 | tf_op jit(solution)/shard_map/ppermute | solution.py:543
  4.7 8.8 %collective-permute-start = (f32[392,128]{1,0:T(8,128)S(1)}, f32[392,128]{1,0:T(8,128)S(1)}, u32[]{:S(2)}, u32[]{:S(2)}) collective-permute-start(f32[392,128]{1,0:T(8,128)S(1)} %get-tuple-element.37), channel_id=1, source_target_pairs={{0,1},{1,0},{2,3},{3,2},{4,5},{5,4},{6,7},{7,6},{8,9},{9,8},{10,11... | collective-permute-start | bytes 602120 | tf_op jit(solution)/shard_map/ppermute | solution.py:543
  13.6 0.2 reshape.10.st
  13.8 0.5 copy-done.3
  14.4 3.8 %inner_first.1 = (f32[3,2,128,128]{3,2,1,0:T(8,128)S(1)}, f32[16,128]{1,0:T(8,128)S(1)}, f32[8,128]{1,0:T(8,128)S(1)}, f32[4,128,128]{2,1,0:T(8,128)S(1)}, bf16[...) custom-call(f32[243]{0:T(256)S(1)} %reshape.10.st, s32[4,3]{1,0:T(4,128)S(1)} %copy-done.3, ...), custom_call_target="tpu_custom_call" | custom-call | flops 1000 | bytes 8000000 | tf_op jit(solution)/shard_map/inner_first/pallas_call | solution.py:572
  18.4 1.2 %collective-permute-start.2 = (f32[12,128]{1,0:T(8,128)S(1)}, f32[12,128]{1,0:T(8,128)S(1)}, u32[]{:S(2)}, u32[]{:S(2)}) collective-permute-start(f32[12,128]{1,0:T(8,128)S(1)} %pad_maximum_fusion.1), channel_id=1, source_target_pairs={{0,128},{1,129},{2,130},{3,131},{4,132},{5,133},{6,134},{7,135},{8... | collective-permute-start | bytes 18440 | tf_op jit(solution)/shard_map/ppermute | solution.py:543
  19.6 3.8 %edge_first.1 = (f32[3,2,128,128]{3,2,1,0:T(8,128)S(1)}, f32[16,128]{1,0:T(8,128)S(1)}, f32[392,128]{1,0:T(8,128)S(1)}, f32[392,128]{1,0:T(8,128)S(1)}) custom-call(s32[1]{0:T(128)} %bitcast.dev, f32[243]{0:T(256)S(1)} %reshape.10.st, f32[3,4,128,128]{3,2,1,0:T(8,128)S(1)} %get-tuple-element.35.field, f32[392,128]{1,0:T(8,128)S(1)} %collective-permute-done.mate, ...), custom_call_target="tpu_custom_call" | custom-call | flops 1000 | bytes 8000000 | tf_op jit(solution)/shard_map/edge_first/pallas_call | solution.py:591
  23.4 1.5 %collective-permute-done.2.faces = f32[12,128]{1,0:T(8,128)S(1)} collective-permute-done((f32[12,128]{1,0:T(8,128)S(1)}, f32[12,128]{1,0:T(8,128)S(1)}, u32[]{:S(2)}, u32[]{:S(2)}) %collective-permute-start.2) | collective-permute-done | bytes 6176 | tf_op jit(solution)/shard_map/ppermute | solution.py:543
  24.9 0.5 contact0.1
  25.3 1.2 %collective-permute-start.3 = (f32[16,128]{1,0:T(8,128)S(1)}, f32[16,128]{1,0:T(8,128)S(1)}, u32[]{:S(2)}, u32[]{:S(2)}) collective-permute-start(f32[16,128]{1,0:T(8,128)S(1)} %get-tuple-element.52.items), channel_id=1, source_target_pairs={{0,1},{1,0},{2,3},{3,2},{4,5},{5,4},{6,7},{7,6},{8,9},{9,8},{10,11... | collective-permute-start | bytes 24584 | tf_op jit(solution)/shard_map/ppermute | solution.py:543
  26.6 0.8 %collective-permute-done.3.mate_items = f32[16,128]{1,0:T(8,128)S(1)} collective-permute-done((f32[16,128]{1,0:T(8,128)S(1)}, f32[16,128]{1,0:T(8,128)S(1)}, u32[]{:S(2)}, u32[]{:S(2)}) %collective-permute-start.3) | collective-permute-done | bytes 8224 | tf_op jit(solution)/shard_map/ppermute | solution.py:543
  27.5 4.9 %collective-permute-start.5 = (f32[392,128]{1,0:T(8,128)S(1)}, f32[392,128]{1,0:T(8,128)S(1)}, u32[]{:S(2)}, u32[]{:S(2)}) collective-permute-start(f32[392,128]{1,0:T(8,128)S(1)} %get-tuple-element.55), channel_id=1, source_target_pairs={{0,1},{1,0},{2,3},{3,2},{4,5},{5,4},{6,7},{7,6},{8,9},{9,8},{10,11... | collective-permute-start | bytes 602120 | tf_op jit(solution)/shard_map/ppermute | solution.py:543
  32.4 3.7 %inner_second.1 = (f32[3,2,128,128]{3,2,1,0:T(8,128)S(1)}, f32[16,128]{1,0:T(8,128)S(1)}, f32[8,128]{1,0:T(8,128)S(1)}, f32[88,128]{1,0:T(8,128)S(1)}) custom-call(f32[243]{0:T(256)S(1)} %reshape.10.st, f32[3,2,128,128]{3,2,1,0:T(8,128)S(1)} %get-tuple-element.40.ui, f32[3,2,128,128]{3,2,1,0:T(8,128)S(1)} %get-tuple-element.42.ue, ...), custom_call_target="tpu_custom_call" | custom-call | flops 1000 | bytes 8000000 | tf_op jit(solution)/shard_map/inner_second/pallas_call | solution.py:611
  36.1 2.5 %collective-permute-start.6 = (f32[12,128]{1,0:T(8,128)S(1)}, f32[12,128]{1,0:T(8,128)S(1)}, u32[]{:S(2)}, u32[]{:S(2)}) collective-permute-start(f32[12,128]{1,0:T(8,128)S(1)} %slice.23), channel_id=1, source_target_pairs={{0,1},{1,0},{2,3},{3,2},{4,5},{5,4},{6,7},{7,6},{8,9},{9,8},{10,11... | collective-permute-start | bytes 18440 | tf_op jit(solution)/shard_map/ppermute | solution.py:543
  38.6 0.8 %collective-permute-done.6.following = f32[12,128]{1,0:T(8,128)S(1)} collective-permute-done((f32[12,128]{1,0:T(8,128)S(1)}, f32[12,128]{1,0:T(8,128)S(1)}, u32[]{:S(2)}, u32[]{:S(2)}) %collective-permute-start.6) | collective-permute-done | bytes 6176 | tf_op jit(solution)/shard_map/ppermute | solution.py:543
  39.4 2.7 %collective-permute-start.7 = (f32[72,128]{1,0:T(8,128)S(1)}, f32[72,128]{1,0:T(8,128)S(1)}, u32[]{:S(2)}, u32[]{:S(2)}) collective-permute-start(f32[72,128]{1,0:T(8,128)S(1)} %gather.1.pack), channel_id=1, source_target_pairs={{0,128},{1,129},{2,130},{3,131},{4,132},{5,133},{6,134},{7,135},{8... | collective-permute-start | bytes 110600 | tf_op jit(solution)/shard_map/ppermute | solution.py:543
  42.1 3.7 %edge_second.1 = (f32[3,2,128,128]{3,2,1,0:T(8,128)S(1)}, f32[16,128]{1,0:T(8,128)S(1)}, f32[8,128]{1,0:T(8,128)S(1)}) custom-call(s32[1]{0:T(128)} %bitcast.dev, f32[243]{0:T(256)S(1)} %reshape.10.st, f32[3,2,128,128]{3,2,1,0:T(8,128)S(1)} %get-tuple-element.40.ui, f32[3,2,128,128]{3,2,1,0:T(8,128)S(1)} %get-tuple-element.42.ue, ...), custom_call_target="tpu_custom_call" | custom-call | flops 1000 | bytes 8000000 | tf_op jit(solution)/shard_map/edge_second/pallas_call | solution.py:623
  45.8 0.4 collective-permute-done.7.cross
  46.2 0.5 join.1
  46.7 11.9 %all_to_all.10.got = f32[32,8,128]{2,1,0:T(8,128)S(1)} all-to-all(f32[32,8,128]{2,1,0:T(8,128)S(1)} %get-tuple-element.67), channel_id=1, replica_groups={{0,1,2,3,4,5,6,7,8,9,10,11,12,13,14,15,16,17,18,19,20,21,22,23,24,25,26..., dimensions={0} | all-to-all | bytes 262144 | tf_op jit(solution)/shard_map/all_to_all | solution.py:547
  58.6 11.7 %all_to_all.11.got = f32[8,8,128]{2,1,0:T(8,128)S(1)} all-to-all(f32[8,8,128]{2,1,0:T(8,128)S(1)} %relay.1), channel_id=1, replica_groups={{0,32,64,96,128,160,192,224},{1,33,65,97,129,161,193,225},{2,34,66,98,1..., dimensions={0} | all-to-all | bytes 65536 | tf_op jit(solution)/shard_map/all_to_all | solution.py:547
  70.3 1.6 %final.1 = (f32[3,4,128,128]{3,2,1,0:T(8,128)}, f32[3,4,128,128]{3,2,1,0:T(8,128)}) custom-call(f32[8,128]{1,0:T(8,128)S(1)} %get-tuple-element.36.theta_v, f32[3,4,128,128]{3,2,1,0:T(8,128)S(1)} %get-tuple-element.35.field, f32[3,2,128,128]{3,2,1,0:T(8,128)S(1)} %get-tuple-element.40.ui, f32[3,2,128,128]{3,2,1,0:T(8,128)S(1)} %get-tuple-element.42.ue, ...), custom_call_target="tpu_custom_call" | custom-call | flops 1000 | bytes 1000000 | tf_op jit(solution)/shard_map/final/pallas_call | solution.py:644
  (27 shorter events, 0.5 us)
Async XLA Ops:
  0.6 1.1 %copy-start = (f32[3,4,128,128]{3,2,1,0:T(8,128)S(1)}, f32[3,4,128,128]{3,2,1,0:T(8,128)}, u32[]{:S(2)}) copy-start(f32[3,4,128,128]{3,2,1,0:T(8,128)} %rhs.1) | copy-start | bytes 2359300
  1.8 11.7 %copy-start.6 = (f32[27,3,3]{0,2,1:T(4,128)S(1)}, f32[27,3,3]{0,2,1:T(4,128)}, u32[]{:S(2)}) copy-start(f32[27,3,3]{0,2,1:T(4,128)} %param.9) | copy-start | bytes 2920
  1.8 12.0 %copy-start.1 = (bf16[4,3,128,128]{3,2,1,0:T(8,128)(2,1)S(1)}, bf16[4,3,128,128]{3,2,1,0:T(8,128)(2,1)}, u32[]{:S(2)}) copy-start(bf16[4,3,128,128]{3,2,1,0:T(8,128)(2,1)} %mortar.1) | copy-start | bytes 1179652
  1.8 12.0 %copy-start.2 = (f32[4,128,128]{2,1,0:T(8,128)S(1)}, f32[4,128,128]{2,1,0:T(8,128)}, u32[]{:S(2)}) copy-start(f32[4,128,128]{2,1,0:T(8,128)} %stiff.1) | copy-start | bytes 786436
  2.0 16.3 %collective-permute-start.1 = (f32[392,128]{1,0:T(8,128)S(1)}, f32[392,128]{1,0:T(8,128)S(1)}, u32[]{:S(2)}, u32[]{:S(2)}) collective-permute-start(f32[392,128]{1,0:T(8,128)S(1)} %get-tuple-element.38), channel_id=1, source_target_pairs={{0,255},{1,2},{2,1},{3,4},{4,3},{5,6},{6,5},{7,8},{8,7},{9,10},{10... | collective-permute-start | bytes 602120 | tf_op jit(solution)/shard_map/ppermute | solution.py:543
  4.7 13.6 %collective-permute-start = (f32[392,128]{1,0:T(8,128)S(1)}, f32[392,128]{1,0:T(8,128)S(1)}, u32[]{:S(2)}, u32[]{:S(2)}) collective-permute-start(f32[392,128]{1,0:T(8,128)S(1)} %get-tuple-element.37), channel_id=1, source_target_pairs={{0,1},{1,0},{2,3},{3,2},{4,5},{5,4},{6,7},{7,6},{8,9},{9,8},{10,11... | collective-permute-start | bytes 602120 | tf_op jit(solution)/shard_map/ppermute | solution.py:543
  13.6 0.7 copy-start.3
  13.6 0.7 copy-start.4
  13.8 0.7 copy-start.5
  18.4 6.5 %collective-permute-start.2 = (f32[12,128]{1,0:T(8,128)S(1)}, f32[12,128]{1,0:T(8,128)S(1)}, u32[]{:S(2)}, u32[]{:S(2)}) collective-permute-start(f32[12,128]{1,0:T(8,128)S(1)} %pad_maximum_fusion.1), channel_id=1, source_target_pairs={{0,128},{1,129},{2,130},{3,131},{4,132},{5,133},{6,134},{7,135},{8... | collective-permute-start | bytes 18440 | tf_op jit(solution)/shard_map/ppermute | solution.py:543
  25.3 2.1 %collective-permute-start.3 = (f32[16,128]{1,0:T(8,128)S(1)}, f32[16,128]{1,0:T(8,128)S(1)}, u32[]{:S(2)}, u32[]{:S(2)}) collective-permute-start(f32[16,128]{1,0:T(8,128)S(1)} %get-tuple-element.52.items), channel_id=1, source_target_pairs={{0,1},{1,0},{2,3},{3,2},{4,5},{5,4},{6,7},{7,6},{8,9},{9,8},{10,11... | collective-permute-start | bytes 24584 | tf_op jit(solution)/shard_map/ppermute | solution.py:543
  27.4 8.7 %collective-permute-start.4 = (f32[420,128]{1,0:T(8,128)S(1)}, f32[420,128]{1,0:T(8,128)S(1)}, u32[]{:S(2)}, u32[]{:S(2)}) collective-permute-start(f32[420,128]{1,0:T(8,128)S(1)} %pad_maximum_fusion), channel_id=1, source_target_pairs={{0,255},{1,2},{2,1},{3,4},{4,3},{5,6},{6,5},{7,8},{8,7},{9,10},{10... | collective-permute-start | bytes 645128 | tf_op jit(solution)/shard_map/ppermute | solution.py:543
  27.5 11.1 %collective-permute-start.5 = (f32[392,128]{1,0:T(8,128)S(1)}, f32[392,128]{1,0:T(8,128)S(1)}, u32[]{:S(2)}, u32[]{:S(2)}) collective-permute-start(f32[392,128]{1,0:T(8,128)S(1)} %get-tuple-element.55), channel_id=1, source_target_pairs={{0,1},{1,0},{2,3},{3,2},{4,5},{5,4},{6,7},{7,6},{8,9},{9,8},{10,11... | collective-permute-start | bytes 602120 | tf_op jit(solution)/shard_map/ppermute | solution.py:543
  36.1 3.3 %collective-permute-start.6 = (f32[12,128]{1,0:T(8,128)S(1)}, f32[12,128]{1,0:T(8,128)S(1)}, u32[]{:S(2)}, u32[]{:S(2)}) collective-permute-start(f32[12,128]{1,0:T(8,128)S(1)} %slice.23), channel_id=1, source_target_pairs={{0,1},{1,0},{2,3},{3,2},{4,5},{5,4},{6,7},{7,6},{8,9},{9,8},{10,11... | collective-permute-start | bytes 18440 | tf_op jit(solution)/shard_map/ppermute | solution.py:543
  39.4 6.8 %collective-permute-start.7 = (f32[72,128]{1,0:T(8,128)S(1)}, f32[72,128]{1,0:T(8,128)S(1)}, u32[]{:S(2)}, u32[]{:S(2)}) collective-permute-start(f32[72,128]{1,0:T(8,128)S(1)} %gather.1.pack), channel_id=1, source_target_pairs={{0,128},{1,129},{2,130},{3,131},{4,132},{5,133},{6,134},{7,135},{8... | collective-permute-start | bytes 110600 | tf_op jit(solution)/shard_map/ppermute | solution.py:543

commit v6 on v5

--- a/solution.py
+++ b/solution.py
@@ -183,11 +183,13 @@
 
 
 def inner_first_kernel(
-    st, partner, active, field, dual, stiff, mortar,
-    ui, dots, theta, stiff_v, mortar_v, dual_v, masks, s, sems,
+    st_from, partner, active, field, dual, stiff, mortar,
+    ui, dots, theta, stiff_v, mortar_v, dual_v, masks, s, sems, st,
 ):
     stiff_copy = pltpu.make_async_copy(stiff, stiff_v, sems.at[0])
     mortar_copy = pltpu.make_async_copy(mortar, mortar_v, sems.at[1])
+    st_copy = pltpu.make_async_copy(st_from, st, sems.at[2])
+    st_copy.start()
     stiff_copy.start()
     mortar_copy.start()
     dual_v[...] = dual[...]
@@ -203,6 +205,7 @@
         for x in range(PLANES):
             s[1, c * 4 + x] = field[c, x]
     fill_shifted(s, 4)
+    st_copy.wait()
     theta[...] = jnp.full((8, W), shift_of(st), F32)
     stiff_copy.wait()
     store_dots(dots, sweep(s, st, 4, inner, emitter(ui, stiff_v, inner, shift_of(st))))
@@ -228,9 +231,12 @@
     return 3 * x + 1
 
 
-def edge_first_kernel(dev, st, field, mate, far, stiff, ui, ue, dots, to_mate, to_far, s):
+def edge_first_kernel(dev, st_from, field, mate, far, stiff, ui, ue, dots, to_mate, to_far, s, st, sem):
     odd, _ = place_of(dev)
+    st_copy = pltpu.make_async_copy(st_from, st, sem)
+    st_copy.start()
     fill_halo(dev, s, mate, far, lambda c, i: field[c, 3 * i], lambda c, i: field[c, 1 + i])
+    st_copy.wait()
     store_dots(dots, sweep(s, st, 6, centre6, emitter(ue, stiff, outer, shift_of(st))))
     for c in range(3):
         low, high = ue[c, 0], ue[c, 1]
@@ -241,21 +247,27 @@
     to_far[HALO : HALO + 8, :] = rows
 
 
-def inner_second_kernel(st, ui, ue, stiff, ki, dots, stiff_rows, coefs, s):
+def inner_second_kernel(st_from, ui, ue, stiff, ki, dots, stiff_rows, coefs, s, st, sem):
+    st_copy = pltpu.make_async_copy(st_from, st, sem)
+    st_copy.start()
     for c in range(3):
         s[1, c * 4] = ue[c, 0]
         s[1, c * 4 + 1] = ui[c, 0]
         s[1, c * 4 + 2] = ui[c, 1]
         s[1, c * 4 + 3] = ue[c, 1]
     fill_shifted(s, 4)
+    st_copy.wait()
     store_dots(dots, sweep(s, st, 4, inner, emitter(ki, stiff, inner, None)))
     stiff_rows[...] = face_rows([stiff[t] for t in range(PLANES)])
     for i, (k, c) in enumerate(FACE_TERMS):
         coefs[i : i + 1, :] = jnp.full((1, W), coefficient(st, k, c, 2), F32)
 
 
-def edge_second_kernel(dev, st, ui, ue, mate, far, stiff, ki, ke, dots, rows, s):
+def edge_second_kernel(dev, st_from, ui, ue, mate, far, stiff, ki, ke, dots, rows, s, st, sem):
+    st_copy = pltpu.make_async_copy(st_from, st, sem)
+    st_copy.start()
     fill_halo(dev, s, mate, far, lambda c, i: ue[c, i], lambda c, i: ui[c, i])
+    st_copy.wait()
     store_dots(dots, sweep(s, st, 6, centre6, emitter(ke, stiff, outer, None)))
     rows[...] = face_rows([ke[2, 0], ki[2, 0], ki[2, 1], ke[2, 1]])
 
@@ -553,6 +565,7 @@
     shape = rhs.shape
     stage = 8000000
     flat = f32(16, W)
+    flat_st = pltpu.SMEM((243,), F32)
 
     def whole(n):
         return [vmem()] * n
@@ -572,7 +585,7 @@
     ui, dots_ui, theta, stiff_v, mortar_v, dual_v, masks = call(
         inner_first_kernel,
         "inner_first",
-        [smem()] * 3 + whole(2) + [anywhere()] * 2,
+        [anywhere()] + [smem()] * 2 + whole(2) + [anywhere()] * 2,
         (
             f32(*half),
             flat,
@@ -582,7 +595,7 @@
             f32(PLANES, W),
             f32(104, W),
         ),
-        [pltpu.VMEM((3, 12, W, W), F32), dma(2)],
+        [pltpu.VMEM((3, 12, W, W), F32), dma(3), flat_st],
         stage,
     )(st, partner, active, field, dual, stiff, mortar)
     own_faces = jnp.concatenate([a_mate[HALO : HALO + 4], g_mate[HALO : HALO + 4], g_far[HALO : HALO + 4]])
@@ -591,9 +604,9 @@
     ue, dots_ue, b_mate, b_far = call(
         edge_first_kernel,
         "edge_first",
-        [smem(), smem()] + whole(5),
+        [smem(), anywhere()] + whole(5),
         (f32(*half), flat, f32(HALO + 8, W), f32(HALO + 8, W)),
-        [pltpu.VMEM((3, 18, W, W), F32)],
+        [pltpu.VMEM((3, 18, W, W), F32), flat_st, dma()],
         stage,
     )(dev, st, field, g_mate, g_far, stiff_v, ui)
     faces, b_mate, b_far = lax.optimization_barrier((faces, b_mate, b_far))
@@ -611,9 +624,9 @@
     ki, dots_ki, stiff_rows, coefs = call(
         inner_second_kernel,
         "inner_second",
-        [smem()] + whole(3),
+        [anywhere()] + whole(3),
         (f32(*half), flat, f32(8, W), f32(88, W)),
-        [pltpu.VMEM((3, 12, W, W), F32)],
+        [pltpu.VMEM((3, 12, W, W), F32), flat_st, dma()],
         stage,
     )(st, ui, ue, stiff_v)
     h_far, ki = lax.optimization_barrier((h_far, ki))
@@ -623,9 +636,9 @@
     ke, dots_ke, k_rows = call(
         edge_second_kernel,
         "edge_second",
-        [smem(), smem()] + whole(6),
+        [smem(), anywhere()] + whole(6),
         (f32(*half), flat, f32(8, W)),
-        [pltpu.VMEM((3, 18, W, W), F32)],
+        [pltpu.VMEM((3, 18, W, W), F32), flat_st, dma()],
         stage,
     )(dev, st, ui, ue, h_mate, h_far, stiff_v, ki)
     send, rows = call(

time: 72.2 us -> 72 us (level)
  transfers between devices with their start and end apart: 8 -> 8, of which waited for: 4 -> 4; matrix products, arithmetic and copies ran while one was open for 0% -> 0% of each run, Pallas kernels for 21% -> 20%
where the time goes in v6:
time: 72 us; the launch traced here: 71.8 us
  starting transfers between devices  24.1 us (33%)
  blocking collectives  23.3 us (32%)
  Pallas kernels  17.4 us (24%)
  waiting for transfers between devices  4.13 us (6%)
  local copies, waits for them, and re-layouts  2.06 us (3%)
  between operations  0.81 us (1%)
    ppermute x8, starting transfers between devices, swap(): return lax.ppermute(x, 'slab', table)  24.1 us
    all_to_all x2, blocking collectives, exchange(): return lax.all_to_all(x, 'slab', 0, 0, tiled=True, axis_index_groups=groups)  23.3 us
    ppermute x8, waiting for transfers between devices, swap(): return lax.ppermute(x, 'slab', table)  4.13 us
    pallas_call x1, Pallas kernels, local(): call(inner_first_kernel, 'inner_first', [anywhere()] + [smem()] * 2 + who...  3.99 us
    pallas_call x1, Pallas kernels, local(): call(inner_second_kernel, 'inner_second', [anywhere()] + whole(3), (f32(*...  3.56 us
    pallas_call x1, Pallas kernels, local(): call(edge_first_kernel, 'edge_first', [smem(), anywhere()] + whole(5), (f...  3.54 us
    pallas_call x1, Pallas kernels, local(): call(edge_second_kernel, 'edge_second', [smem(), anywhere()] + whole(6),...  3.5 us
    unnamed x15, local copies, waits for them, and re-layouts  1.89 us
  transfers between devices with their start and end apart: 8, of which 4 were waited for; matrix products, arithmetic and copies ran while one was open for 0% of the time, Pallas kernels for 20%

profile of v6, /device:TPU:1, one launch (start us, length us, event | category | flops | bytes accessed | tf_op | source)
XLA Modules:
  0.0 71.8 jit_solution(14964154485454255668)
XLA Ops:
  0.6 1.1 %copy-done = f32[3,4,128,128]{3,2,1,0:T(8,128)S(1)} copy-done((f32[3,4,128,128]{3,2,1,0:T(8,128)S(1)}, f32[3,4,128,128]{3,2,1,0:T(8,128)}, u32[]{:S(2)}) %copy-start) | copy-done | bytes 786456
  1.8 0.2 load.1
  2.0 2.7 %collective-permute-start.1 = (f32[392,128]{1,0:T(8,128)S(1)}, f32[392,128]{1,0:T(8,128)S(1)}, u32[]{:S(2)}, u32[]{:S(2)}) collective-permute-start(f32[392,128]{1,0:T(8,128)S(1)} %get-tuple-element.38), channel_id=1, source_target_pairs={{0,255},{1,2},{2,1},{3,4},{4,3},{5,6},{6,5},{7,8},{8,7},{9,10},{10... | collective-permute-start | bytes 602120 | tf_op jit(solution)/shard_map/ppermute | solution.py:555
  4.7 8.8 %collective-permute-start = (f32[392,128]{1,0:T(8,128)S(1)}, f32[392,128]{1,0:T(8,128)S(1)}, u32[]{:S(2)}, u32[]{:S(2)}) collective-permute-start(f32[392,128]{1,0:T(8,128)S(1)} %get-tuple-element.37), channel_id=1, source_target_pairs={{0,1},{1,0},{2,3},{3,2},{4,5},{5,4},{6,7},{7,6},{8,9},{9,8},{10,11... | collective-permute-start | bytes 602120 | tf_op jit(solution)/shard_map/ppermute | solution.py:555
  13.6 0.2 reshape.10.st_from
  13.8 0.5 copy-done.3
  14.4 4.0 %inner_first.1 = (f32[3,2,128,128]{3,2,1,0:T(8,128)S(1)}, f32[16,128]{1,0:T(8,128)S(1)}, f32[8,128]{1,0:T(8,128)S(1)}, f32[4,128,128]{2,1,0:T(8,128)S(1)}, bf16[...) custom-call(f32[243]{0:T(256)S(1)} %reshape.10.st_from, s32[4,3]{1,0:T(4,128)S(1)} %copy-done.3, ...), custom_call_target="tpu_custom_call" | custom-call | flops 1000 | bytes 8000000 | tf_op jit(solution)/shard_map/inner_first/pallas_call | solution.py:585
  18.5 1.2 %collective-permute-start.2 = (f32[12,128]{1,0:T(8,128)S(1)}, f32[12,128]{1,0:T(8,128)S(1)}, u32[]{:S(2)}, u32[]{:S(2)}) collective-permute-start(f32[12,128]{1,0:T(8,128)S(1)} %pad_maximum_fusion.1), channel_id=1, source_target_pairs={{0,128},{1,129},{2,130},{3,131},{4,132},{5,133},{6,134},{7,135},{8... | collective-permute-start | bytes 18440 | tf_op jit(solution)/shard_map/ppermute | solution.py:555
  19.8 3.5 %edge_first.1 = (f32[3,2,128,128]{3,2,1,0:T(8,128)S(1)}, f32[16,128]{1,0:T(8,128)S(1)}, f32[392,128]{1,0:T(8,128)S(1)}, f32[392,128]{1,0:T(8,128)S(1)}) custom-call(s32[1]{0:T(128)} %bitcast.dev, f32[243]{0:T(256)S(1)} %reshape.10.st_from, f32[3,4,128,128]{3,2,1,0:T(8,128)S(1)} %get-tuple-element.35.field, f32[392,128]{1,0:T(8,128)S(1)} %collective-permute-done.mate, ...), custom_call_target="tpu_custom_call" | custom-call | flops 1000 | bytes 8000000 | tf_op jit(solution)/shard_map/edge_first/pallas_call | solution.py:604
  23.3 1.7 %collective-permute-done.2.faces = f32[12,128]{1,0:T(8,128)S(1)} collective-permute-done((f32[12,128]{1,0:T(8,128)S(1)}, f32[12,128]{1,0:T(8,128)S(1)}, u32[]{:S(2)}, u32[]{:S(2)}) %collective-permute-start.2) | collective-permute-done | bytes 6176 | tf_op jit(solution)/shard_map/ppermute | solution.py:555
  25.0 0.5 contact0.1
  25.5 1.2 %collective-permute-start.3 = (f32[16,128]{1,0:T(8,128)S(1)}, f32[16,128]{1,0:T(8,128)S(1)}, u32[]{:S(2)}, u32[]{:S(2)}) collective-permute-start(f32[16,128]{1,0:T(8,128)S(1)} %get-tuple-element.52.items), channel_id=1, source_target_pairs={{0,1},{1,0},{2,3},{3,2},{4,5},{5,4},{6,7},{7,6},{8,9},{9,8},{10,11... | collective-permute-start | bytes 24584 | tf_op jit(solution)/shard_map/ppermute | solution.py:555
  26.7 0.8 %collective-permute-done.3.mate_items = f32[16,128]{1,0:T(8,128)S(1)} collective-permute-done((f32[16,128]{1,0:T(8,128)S(1)}, f32[16,128]{1,0:T(8,128)S(1)}, u32[]{:S(2)}, u32[]{:S(2)}) %collective-permute-start.3) | collective-permute-done | bytes 8224 | tf_op jit(solution)/shard_map/ppermute | solution.py:555
  27.7 4.7 %collective-permute-start.5 = (f32[392,128]{1,0:T(8,128)S(1)}, f32[392,128]{1,0:T(8,128)S(1)}, u32[]{:S(2)}, u32[]{:S(2)}) collective-permute-start(f32[392,128]{1,0:T(8,128)S(1)} %get-tuple-element.55), channel_id=1, source_target_pairs={{0,1},{1,0},{2,3},{3,2},{4,5},{5,4},{6,7},{7,6},{8,9},{9,8},{10,11... | collective-permute-start | bytes 602120 | tf_op jit(solution)/shard_map/ppermute | solution.py:555
  32.4 3.6 %inner_second.1 = (f32[3,2,128,128]{3,2,1,0:T(8,128)S(1)}, f32[16,128]{1,0:T(8,128)S(1)}, f32[8,128]{1,0:T(8,128)S(1)}, f32[88,128]{1,0:T(8,128)S(1)}) custom-call(f32[243]{0:T(256)S(1)} %reshape.10.st_from, f32[3,2,128,128]{3,2,1,0:T(8,128)S(1)} %get-tuple-element.40.ui, f32[3,2,128,128]{3,2,1,0:T(8,128)S(1)} %get-tuple-element.42.ue, ...), custom_call_target="tpu_custom_call" | custom-call | flops 1000 | bytes 8000000 | tf_op jit(solution)/shard_map/inner_second/pallas_call | solution.py:624
  36.0 2.8 %collective-permute-start.6 = (f32[12,128]{1,0:T(8,128)S(1)}, f32[12,128]{1,0:T(8,128)S(1)}, u32[]{:S(2)}, u32[]{:S(2)}) collective-permute-start(f32[12,128]{1,0:T(8,128)S(1)} %slice.23), channel_id=1, source_target_pairs={{0,1},{1,0},{2,3},{3,2},{4,5},{5,4},{6,7},{7,6},{8,9},{9,8},{10,11... | collective-permute-start | bytes 18440 | tf_op jit(solution)/shard_map/ppermute | solution.py:555
  38.7 0.8 %collective-permute-done.6.following = f32[12,128]{1,0:T(8,128)S(1)} collective-permute-done((f32[12,128]{1,0:T(8,128)S(1)}, f32[12,128]{1,0:T(8,128)S(1)}, u32[]{:S(2)}, u32[]{:S(2)}) %collective-permute-start.6) | collective-permute-done | bytes 6176 | tf_op jit(solution)/shard_map/ppermute | solution.py:555
  39.6 2.5 %collective-permute-start.7 = (f32[72,128]{1,0:T(8,128)S(1)}, f32[72,128]{1,0:T(8,128)S(1)}, u32[]{:S(2)}, u32[]{:S(2)}) collective-permute-start(f32[72,128]{1,0:T(8,128)S(1)} %gather.1.pack), channel_id=1, source_target_pairs={{0,128},{1,129},{2,130},{3,131},{4,132},{5,133},{6,134},{7,135},{8... | collective-permute-start | bytes 110600 | tf_op jit(solution)/shard_map/ppermute | solution.py:555
  42.1 3.5 %edge_second.1 = (f32[3,2,128,128]{3,2,1,0:T(8,128)S(1)}, f32[16,128]{1,0:T(8,128)S(1)}, f32[8,128]{1,0:T(8,128)S(1)}) custom-call(s32[1]{0:T(128)} %bitcast.dev, f32[243]{0:T(256)S(1)} %reshape.10.st_from, f32[3,2,128,128]{3,2,1,0:T(8,128)S(1)} %get-tuple-element.40.ui, f32[3,2,128,128]{3,2,1,0:T(8,128)S(1)} %get-tuple-element.42.ue, ...), custom_call_target="tpu_custom_call" | custom-call | flops 1000 | bytes 8000000 | tf_op jit(solution)/shard_map/edge_second/pallas_call | solution.py:636
  45.6 0.8 %collective-permute-done.7.cross = f32[72,128]{1,0:T(8,128)S(1)} collective-permute-done((f32[72,128]{1,0:T(8,128)S(1)}, f32[72,128]{1,0:T(8,128)S(1)}, u32[]{:S(2)}, u32[]{:S(2)}) %collective-permute-start.7) | collective-permute-done | bytes 36896 | tf_op jit(solution)/shard_map/ppermute | solution.py:555
  46.4 0.5 join.1
  46.8 11.9 %all_to_all.10.got = f32[32,8,128]{2,1,0:T(8,128)S(1)} all-to-all(f32[32,8,128]{2,1,0:T(8,128)S(1)} %get-tuple-element.67), channel_id=1, replica_groups={{0,1,2,3,4,5,6,7,8,9,10,11,12,13,14,15,16,17,18,19,20,21,22,23,24,25,26..., dimensions={0} | all-to-all | bytes 262144 | tf_op jit(solution)/shard_map/all_to_all | solution.py:559
  58.8 11.4 %all_to_all.11.got = f32[8,8,128]{2,1,0:T(8,128)S(1)} all-to-all(f32[8,8,128]{2,1,0:T(8,128)S(1)} %relay.1), channel_id=1, replica_groups={{0,32,64,96,128,160,192,224},{1,33,65,97,129,161,193,225},{2,34,66,98,1..., dimensions={0} | all-to-all | bytes 65536 | tf_op jit(solution)/shard_map/all_to_all | solution.py:559
  70.1 1.6 %final.1 = (f32[3,4,128,128]{3,2,1,0:T(8,128)}, f32[3,4,128,128]{3,2,1,0:T(8,128)}) custom-call(f32[8,128]{1,0:T(8,128)S(1)} %get-tuple-element.36.theta_v, f32[3,4,128,128]{3,2,1,0:T(8,128)S(1)} %get-tuple-element.35.field, f32[3,2,128,128]{3,2,1,0:T(8,128)S(1)} %get-tuple-element.40.ui, f32[3,2,128,128]{3,2,1,0:T(8,128)S(1)} %get-tuple-element.42.ue, ...), custom_call_target="tpu_custom_call" | custom-call | flops 1000 | bytes 1000000 | tf_op jit(solution)/shard_map/final/pallas_call | solution.py:657
  (27 shorter events, 0.5 us)
Async XLA Ops:
  0.6 1.1 %copy-start = (f32[3,4,128,128]{3,2,1,0:T(8,128)S(1)}, f32[3,4,128,128]{3,2,1,0:T(8,128)}, u32[]{:S(2)}) copy-start(f32[3,4,128,128]{3,2,1,0:T(8,128)} %rhs.1) | copy-start | bytes 2359300
  1.8 11.7 %copy-start.6 = (f32[27,3,3]{0,2,1:T(4,128)S(1)}, f32[27,3,3]{0,2,1:T(4,128)}, u32[]{:S(2)}) copy-start(f32[27,3,3]{0,2,1:T(4,128)} %param.9) | copy-start | bytes 2920
  1.8 12.0 %copy-start.1 = (bf16[4,3,128,128]{3,2,1,0:T(8,128)(2,1)S(1)}, bf16[4,3,128,128]{3,2,1,0:T(8,128)(2,1)}, u32[]{:S(2)}) copy-start(bf16[4,3,128,128]{3,2,1,0:T(8,128)(2,1)} %mortar.1) | copy-start | bytes 1179652
  1.8 12.0 %copy-start.2 = (f32[4,128,128]{2,1,0:T(8,128)S(1)}, f32[4,128,128]{2,1,0:T(8,128)}, u32[]{:S(2)}) copy-start(f32[4,128,128]{2,1,0:T(8,128)} %stiff.1) | copy-start | bytes 786436
  2.0 16.5 %collective-permute-start.1 = (f32[392,128]{1,0:T(8,128)S(1)}, f32[392,128]{1,0:T(8,128)S(1)}, u32[]{:S(2)}, u32[]{:S(2)}) collective-permute-start(f32[392,128]{1,0:T(8,128)S(1)} %get-tuple-element.38), channel_id=1, source_target_pairs={{0,255},{1,2},{2,1},{3,4},{4,3},{5,6},{6,5},{7,8},{8,7},{9,10},{10... | collective-permute-start | bytes 602120 | tf_op jit(solution)/shard_map/ppermute | solution.py:555
  4.7 13.8 %collective-permute-start = (f32[392,128]{1,0:T(8,128)S(1)}, f32[392,128]{1,0:T(8,128)S(1)}, u32[]{:S(2)}, u32[]{:S(2)}) collective-permute-start(f32[392,128]{1,0:T(8,128)S(1)} %get-tuple-element.37), channel_id=1, source_target_pairs={{0,1},{1,0},{2,3},{3,2},{4,5},{5,4},{6,7},{7,6},{8,9},{9,8},{10,11... | collective-permute-start | bytes 602120 | tf_op jit(solution)/shard_map/ppermute | solution.py:555
  13.6 0.7 copy-start.3
  13.6 0.7 copy-start.4
  13.8 0.7 copy-start.5
  18.5 6.5 %collective-permute-start.2 = (f32[12,128]{1,0:T(8,128)S(1)}, f32[12,128]{1,0:T(8,128)S(1)}, u32[]{:S(2)}, u32[]{:S(2)}) collective-permute-start(f32[12,128]{1,0:T(8,128)S(1)} %pad_maximum_fusion.1), channel_id=1, source_target_pairs={{0,128},{1,129},{2,130},{3,131},{4,132},{5,133},{6,134},{7,135},{8... | collective-permute-start | bytes 18440 | tf_op jit(solution)/shard_map/ppermute | solution.py:555
  25.5 2.1 %collective-permute-start.3 = (f32[16,128]{1,0:T(8,128)S(1)}, f32[16,128]{1,0:T(8,128)S(1)}, u32[]{:S(2)}, u32[]{:S(2)}) collective-permute-start(f32[16,128]{1,0:T(8,128)S(1)} %get-tuple-element.52.items), channel_id=1, source_target_pairs={{0,1},{1,0},{2,3},{3,2},{4,5},{5,4},{6,7},{7,6},{8,9},{9,8},{10,11... | collective-permute-start | bytes 24584 | tf_op jit(solution)/shard_map/ppermute | solution.py:555
  27.6 8.4 %collective-permute-start.4 = (f32[420,128]{1,0:T(8,128)S(1)}, f32[420,128]{1,0:T(8,128)S(1)}, u32[]{:S(2)}, u32[]{:S(2)}) collective-permute-start(f32[420,128]{1,0:T(8,128)S(1)} %pad_maximum_fusion), channel_id=1, source_target_pairs={{0,255},{1,2},{2,1},{3,4},{4,3},{5,6},{6,5},{7,8},{8,7},{9,10},{10... | collective-permute-start | bytes 645128 | tf_op jit(solution)/shard_map/ppermute | solution.py:555
  27.7 11.1 %collective-permute-start.5 = (f32[392,128]{1,0:T(8,128)S(1)}, f32[392,128]{1,0:T(8,128)S(1)}, u32[]{:S(2)}, u32[]{:S(2)}) collective-permute-start(f32[392,128]{1,0:T(8,128)S(1)} %get-tuple-element.55), channel_id=1, source_target_pairs={{0,1},{1,0},{2,3},{3,2},{4,5},{5,4},{6,7},{7,6},{8,9},{9,8},{10,11... | collective-permute-start | bytes 602120 | tf_op jit(solution)/shard_map/ppermute | solution.py:555
  36.0 3.6 %collective-permute-start.6 = (f32[12,128]{1,0:T(8,128)S(1)}, f32[12,128]{1,0:T(8,128)S(1)}, u32[]{:S(2)}, u32[]{:S(2)}) collective-permute-start(f32[12,128]{1,0:T(8,128)S(1)} %slice.23), channel_id=1, source_target_pairs={{0,1},{1,0},{2,3},{3,2},{4,5},{5,4},{6,7},{7,6},{8,9},{9,8},{10,11... | collective-permute-start | bytes 18440 | tf_op jit(solution)/shard_map/ppermute | solution.py:555
  39.6 6.8 %collective-permute-start.7 = (f32[72,128]{1,0:T(8,128)S(1)}, f32[72,128]{1,0:T(8,128)S(1)}, u32[]{:S(2)}, u32[]{:S(2)}) collective-permute-start(f32[72,128]{1,0:T(8,128)S(1)} %gather.1.pack), channel_id=1, source_target_pairs={{0,128},{1,129},{2,130},{3,131},{4,132},{5,133},{6,134},{7,135},{8... | collective-permute-start | bytes 110600 | tf_op jit(solution)/shard_map/ppermute | solution.py:555
